TPU v7x, 32 devices: a whole 2x2x4 slice. The times are simulated.
32 devices in a mesh: dp: 8 (over y, x, core), mp: 4 (over z).
Axes of the slice: x: 2, y: 2, z: 4, core: 2. Of those that a mesh axis runs over, the one named last changes fastest.
Arguments:
- hidden_in: float32 [8192, 1280], P(('dp', 'mp')), may hold values from -6 to 6
- pre_gain: float32 [2, 1280], P(None, ('dp', 'mp')), may hold values from 0.1 to 1.9
- pre_bias: float32 [2, 1280], P(None, ('dp', 'mp')), may hold values from -3 to 3
- qkv_weight: bfloat16 [2, 3, 1280, 1280], P(None, None, 'dp', 'mp'), may hold values from -0.15625 to 0.15625
- qkv_bias: float32 [2, 3, 1280], P(None, None, ('dp', 'mp')), may hold values from -3 to 3
- proj_weight: bfloat16 [2, 1280, 1280], P(None, 'mp', 'dp'), may hold values from -0.625 to 0.625
- proj_bias: float32 [2, 1280], P(None, ('dp', 'mp')), may hold values from -2 to 2
- mid_gain: float32 [2, 1280], P(None, ('dp', 'mp')), may hold values from 0.1 to 1.9
- mid_bias: float32 [2, 1280], P(None, ('dp', 'mp')), may hold values from -3 to 3
- up_weight: bfloat16 [2, 1280, 5120], P(None, 'dp', 'mp'), may hold values from -0.15625 to 0.15625
- up_bias: float32 [2, 5120], P(None, ('dp', 'mp')), may hold values from -3 to 3
- down_weight: bfloat16 [2, 5120, 1280], P(None, 'mp', 'dp'), may hold values from -0.15625 to 0.15625
- down_bias: float32 [2, 1280], P(None, ('dp', 'mp')), may hold values from -2 to 2
- picture_ids: int32 [8192], P('dp'), may hold values from 0 to 5, as said below
- positions: int32 [2, 8192], P(None, 'dp'), may hold values from 0 to 31, as said below
- pad_mask: int32 [8192], P('dp'), may hold values from 0 to 1, as said below
- cotangent: float32 [8192, 1280], P(('dp', 'mp')), may hold values from -6 to 6
Outputs:
- out_hidden: float32 [8192, 1280], P(('dp', 'mp'))
- grad_hidden: float32 [8192, 1280], P(('dp', 'mp'))
- pre_gain_grad: float32 [2, 1280], P(None, ('dp', 'mp'))
- pre_bias_grad: float32 [2, 1280], P(None, ('dp', 'mp'))
- qkv_weight_grad: float32 [2, 3, 1280, 1280], P(None, None, 'dp', 'mp')
- qkv_bias_grad: float32 [2, 3, 1280], P(None, None, ('dp', 'mp'))
- proj_weight_grad: float32 [2, 1280, 1280], P(None, 'mp', 'dp')
- proj_bias_grad: float32 [2, 1280], P(None, ('dp', 'mp'))
- mid_gain_grad: float32 [2, 1280], P(None, ('dp', 'mp'))
- mid_bias_grad: float32 [2, 1280], P(None, ('dp', 'mp'))
- up_weight_grad: float32 [2, 1280, 5120], P(None, 'dp', 'mp')
- up_bias_grad: float32 [2, 5120], P(None, ('dp', 'mp'))
- down_weight_grad: float32 [2, 5120, 1280], P(None, 'mp', 'dp')
- down_bias_grad: float32 [2, 1280], P(None, ('dp', 'mp'))
Inputs may be any that keep to these rules, and one draw needn't show every extreme that they name: `picture_ids`: within each row of 1024 patches the ids never fall and each picture's patches stand together; the padding at a row's end carries one id beyond its pictures; each row begins with a picture 32 patches high and one 32 patches wide. `positions`: each picture is 10 to 32 patches high and wide, its patches in row-major order; padding has 0. `pad_mask`: 1 on a leading run of each row, 0 after it.
All inputs are finite; a program needn't handle non-finite values.
Results may differ from a plain program's by a relative error of at most 0.02.
Values may be sent and summed in bfloat16 or wider, within the bound.
A program may use at most 192 MiB of HBM per device.

v0:
```python
import jax
import jax.numpy as jnp
from jax import lax
from jax.sharding import PartitionSpec as P

D = 1280
HD = 80
FF = 5120
LAYERS = 2


EPSILON = 1e-06


def layer_norm(values, gain, shift):
    centre = values - jnp.mean(values, axis=-1, keepdims=True)
    spread = jnp.mean(centre * centre, axis=-1, keepdims=True)
    return centre * lax.rsqrt(spread + EPSILON) * gain + shift


def rotary_tables(coords):
    quarter = HD // 4
    powers = jnp.arange(quarter, dtype=jnp.float32) * (4.0 / HD)
    inverse = 10000.0 ** (-powers)
    height_angle = coords[0].astype(jnp.float32)[:, None] * inverse[None, :]
    width_angle = coords[1].astype(jnp.float32)[:, None] * inverse[None, :]
    angles = jnp.concatenate([height_angle, width_angle], axis=1)
    angles = jnp.concatenate([angles, angles], axis=1)
    return (jnp.cos(angles)[:, None, :], jnp.sin(angles)[:, None, :])


def rotate(values, cosine, sine):
    half_size = HD // 2
    turned = jnp.concatenate([-values[..., half_size:], values[..., :half_size]], axis=-1)
    return values * cosine + turned * sine


def quick_gelu(values):
    return values / (1.0 + jnp.exp(-1.702 * values))


def masked_scores(queries, key_rows, picture_ids, pad_mask, begin_row, block_rows):
    length = key_rows.shape[0]
    local_q = lax.dynamic_slice_in_dim(queries, begin_row, block_rows, 0)
    scores = jnp.einsum(
        "qhe,khe->hqk", local_q, key_rows, preferred_element_type=jnp.float32
    ) * HD ** (-0.5)
    own_ids = lax.dynamic_slice_in_dim(picture_ids, begin_row, block_rows, 0)
    rows_at = begin_row + jnp.arange(block_rows, dtype=jnp.int32)
    columns_at = jnp.arange(length, dtype=jnp.int32)
    allowed = (own_ids[:, None] == picture_ids[None, :]) & (pad_mask[None, :] == 1) | (
        rows_at[:, None] == columns_at[None, :]
    )
    return (local_q, jnp.where(allowed[None], scores, -1e30))


def attend_forward(queries, key_rows, value_rows, picture_ids, pad_mask):
    length = queries.shape[0]
    block_rows = min(512, length)
    block_count = length // block_rows

    def one_block(block_index):
        local_q, scores = masked_scores(
            queries, key_rows, picture_ids, pad_mask, block_index * block_rows, block_rows
        )
        row_max = jnp.max(scores, axis=-1, keepdims=True)
        exponent = jnp.exp(scores - row_max)
        totals = jnp.sum(exponent, axis=-1, keepdims=True)
        chances = (exponent / totals).astype(jnp.bfloat16)
        mixed = jnp.einsum("hqk,khe->qhe", chances, value_rows, preferred_element_type=jnp.float32)
        return (mixed.astype(jnp.bfloat16), (row_max + jnp.log(totals))[..., 0])

    mixed, log_totals = lax.map(one_block, jnp.arange(block_count, dtype=jnp.int32))
    return (mixed.reshape(length, -1), log_totals)


def attend_backward(queries, key_rows, value_rows, grad_mixed, log_totals, picture_ids, pad_mask):
    length = queries.shape[0]
    block_rows = min(512, length)
    block_count = length // block_rows
    scale = HD ** (-0.5)

    def one_block(carried, inputs):
        block_index, log_block = inputs
        begin_row = block_index * block_rows
        local_q, scores = masked_scores(
            queries, key_rows, picture_ids, pad_mask, begin_row, block_rows
        )
        chances = jnp.exp(scores - log_block[..., None])
        local_grad = lax.dynamic_slice_in_dim(grad_mixed, begin_row, block_rows, 0)
        grad_chance = jnp.einsum(
            "qhe,khe->hqk", local_grad, value_rows, preferred_element_type=jnp.float32
        )
        centre = jnp.sum(chances * grad_chance, axis=-1, keepdims=True)
        grad_scores = (chances * (grad_chance - centre)).astype(jnp.bfloat16)
        grad_query = (
            jnp.einsum("hqk,khe->qhe", grad_scores, key_rows, preferred_element_type=jnp.float32)
            * scale
        )
        grad_key = (
            carried[0]
            + jnp.einsum("hqk,qhe->khe", grad_scores, local_q, preferred_element_type=jnp.float32)
            * scale
        )
        grad_value = carried[1] + jnp.einsum(
            "hqk,qhe->khe",
            chances.astype(jnp.bfloat16),
            local_grad,
            preferred_element_type=jnp.float32,
        )
        return ((grad_key, grad_value), grad_query)

    zero_rows = jnp.zeros(key_rows.shape, jnp.float32)
    (grad_key, grad_value), grad_query = lax.scan(
        one_block, (zero_rows, zero_rows), (jnp.arange(block_count, dtype=jnp.int32), log_totals)
    )
    return (grad_query.reshape(key_rows.shape), grad_key, grad_value)


def body(
    hidden_in,
    pre_gain,
    pre_bias,
    qkv_weight,
    qkv_bias,
    proj_weight,
    proj_bias,
    mid_gain,
    mid_bias,
    up_weight,
    up_bias,
    down_weight,
    down_bias,
    picture_ids,
    positions,
    pad_mask,
    cotangent,
):
    gathered = (
        lax.all_gather(pre_gain, ("dp", "mp"), axis=1, tiled=True),
        lax.all_gather(pre_bias, ("dp", "mp"), axis=1, tiled=True),
        lax.all_gather(qkv_bias, ("dp", "mp"), axis=2, tiled=True),
        lax.all_gather(proj_bias, ("dp", "mp"), axis=1, tiled=True),
        lax.all_gather(mid_gain, ("dp", "mp"), axis=1, tiled=True),
        lax.all_gather(mid_bias, ("dp", "mp"), axis=1, tiled=True),
        lax.all_gather(up_bias, ("dp", "mp"), axis=1, tiled=True),
        lax.all_gather(down_bias, ("dp", "mp"), axis=1, tiled=True),
    )
    (
        pre_gain_all,
        pre_bias_all,
        qkv_bias_all,
        proj_bias_all,
        mid_gain_all,
        mid_bias_all,
        up_bias_all,
        down_bias_all,
    ) = gathered
    column_count = qkv_weight.shape[3]
    hidden_count = up_weight.shape[2]
    local_heads = column_count // HD
    tensor_rank = lax.axis_index("mp")
    qkv_bias_mine = lax.dynamic_slice_in_dim(
        qkv_bias_all, tensor_rank * column_count, column_count, 2
    )
    up_bias_mine = lax.dynamic_slice_in_dim(
        up_bias_all, tensor_rank * hidden_count, hidden_count, 1
    )
    cosine, sine = rotary_tables(positions)

    def gather_layer(layer_index):
        return (
            lax.all_gather(qkv_weight[layer_index], "dp", axis=1, tiled=True),
            lax.all_gather(proj_weight[layer_index], "dp", axis=1, tiled=True),
            lax.all_gather(up_weight[layer_index], "dp", axis=0, tiled=True),
            lax.all_gather(down_weight[layer_index], "dp", axis=1, tiled=True),
        )

    def attention_forward(hidden, layer_index, matrices):
        normed = layer_norm(hidden, pre_gain_all[layer_index], pre_bias_all[layer_index]).astype(
            jnp.bfloat16
        )
        all_rows = lax.all_gather(normed, "mp", axis=0, tiled=True)
        length = all_rows.shape[0]
        linear = (
            jnp.einsum("nd,jdc->jnc", all_rows, matrices[0], preferred_element_type=jnp.float32)
            + qkv_bias_mine[layer_index][:, None, :]
        )
        parts_qkv = linear.reshape(3, length, local_heads, HD)
        queries = rotate(parts_qkv[0], cosine, sine).astype(jnp.bfloat16)
        key_rows = rotate(parts_qkv[1], cosine, sine).astype(jnp.bfloat16)
        value_rows = parts_qkv[2].astype(jnp.bfloat16)
        mixed, log_totals = attend_forward(queries, key_rows, value_rows, picture_ids, pad_mask)
        partial_sum = jnp.dot(mixed, matrices[1], preferred_element_type=jnp.float32)
        attended = (
            lax.psum_scatter(
                partial_sum.astype(jnp.bfloat16), "mp", scatter_dimension=0, tiled=True
            ).astype(jnp.float32)
            + proj_bias_all[layer_index]
        )
        return (hidden + attended, (all_rows, queries, key_rows, value_rows, mixed, log_totals))

    def hidden_forward(middle, layer_index, matrices):
        normed = layer_norm(middle, mid_gain_all[layer_index], mid_bias_all[layer_index]).astype(
            jnp.bfloat16
        )
        all_rows = lax.all_gather(normed, "mp", axis=0, tiled=True)
        upward = (
            jnp.dot(all_rows, matrices[2], preferred_element_type=jnp.float32)
            + up_bias_mine[layer_index]
        )
        return (all_rows, upward, quick_gelu(upward).astype(jnp.bfloat16))

    inputs_kept = []
    weights_kept = []
    hidden = hidden_in
    for layer_index in range(LAYERS):
        matrices = gather_layer(layer_index)
        weights_kept.append(matrices)
        inputs_kept.append(hidden)
        middle = attention_forward(hidden, layer_index, matrices)[0]
        active = hidden_forward(middle, layer_index, matrices)[2]
        output_partial_sum = jnp.dot(active, matrices[3], preferred_element_type=jnp.float32)
        hidden = middle + (
            lax.psum_scatter(
                output_partial_sum.astype(jnp.bfloat16), "mp", scatter_dimension=0, tiled=True
            ).astype(jnp.float32)
            + down_bias_all[layer_index]
        )
    out_hidden = hidden
    gradient = cotangent
    layer_results = []
    vector_parts = []
    for layer_index in reversed(range(LAYERS)):
        matrices = gather_layer(layer_index)
        hidden = inputs_kept[layer_index]
        middle, saved = attention_forward(hidden, layer_index, matrices)
        attn_rows, queries, key_rows, value_rows, mixed, log_totals = saved
        mid_rows, upward, active = hidden_forward(middle, layer_index, matrices)
        grad_out = gradient.astype(jnp.bfloat16)
        down_bias_part = jnp.sum(grad_out.astype(jnp.float32), axis=0)
        grad_rows = lax.all_gather(grad_out, "mp", axis=0, tiled=True)
        down_grad = jnp.einsum("nf,nd->fd", active, grad_rows, preferred_element_type=jnp.float32)
        grad_active = jnp.einsum(
            "nd,fd->nf", grad_rows, matrices[3], preferred_element_type=jnp.float32
        )
        gelu_pull = jax.vjp(quick_gelu, upward)[1]
        grad_up = gelu_pull(grad_active)[0].astype(jnp.bfloat16)
        up_bias_part = jnp.sum(grad_up.astype(jnp.float32), axis=0)
        up_grad = jnp.einsum("nd,nf->df", mid_rows, grad_up, preferred_element_type=jnp.float32)
        grad_normed = lax.psum_scatter(
            jnp.einsum(
                "nf,df->nd", grad_up, matrices[2], preferred_element_type=jnp.float32
            ).astype(jnp.bfloat16),
            "mp",
            scatter_dimension=0,
            tiled=True,
        ).astype(jnp.float32)
        norm_pull = jax.vjp(
            layer_norm, middle, mid_gain_all[layer_index], mid_bias_all[layer_index]
        )[1]
        grad_middle, mid_gain_part, mid_bias_part = norm_pull(grad_normed)
        grad_middle = gradient + grad_middle
        grad_attn = grad_middle.astype(jnp.bfloat16)
        proj_bias_part = jnp.sum(grad_attn.astype(jnp.float32), axis=0)
        grad_rows = lax.all_gather(grad_attn, "mp", axis=0, tiled=True)
        length = grad_rows.shape[0]
        proj_grad = jnp.einsum("nc,nd->cd", mixed, grad_rows, preferred_element_type=jnp.float32)
        grad_mixed = jnp.einsum(
            "nd,cd->nc", grad_rows, matrices[1], preferred_element_type=jnp.float32
        ).astype(jnp.bfloat16)
        grad_query, grad_key, grad_value = attend_backward(
            queries,
            key_rows,
            value_rows,
            grad_mixed.reshape(length, local_heads, HD),
            log_totals,
            picture_ids,
            pad_mask,
        )
        turn_back = jax.vjp(lambda values: rotate(values, cosine, sine), grad_query)[1]
        grad_linear = (
            jnp.stack([turn_back(grad_query)[0], turn_back(grad_key)[0], grad_value])
            .reshape(3, length, column_count)
            .astype(jnp.bfloat16)
        )
        qkv_bias_part = jnp.sum(grad_linear.astype(jnp.float32), axis=1)
        qkv_grad = jnp.einsum(
            "nd,jnc->jdc", attn_rows, grad_linear, preferred_element_type=jnp.float32
        )
        grad_normed = lax.psum_scatter(
            jnp.einsum(
                "jnc,jdc->nd", grad_linear, matrices[0], preferred_element_type=jnp.float32
            ).astype(jnp.bfloat16),
            "mp",
            scatter_dimension=0,
            tiled=True,
        ).astype(jnp.float32)
        norm_pull = jax.vjp(
            layer_norm, hidden, pre_gain_all[layer_index], pre_bias_all[layer_index]
        )[1]
        grad_input, pre_gain_part, pre_bias_part = norm_pull(grad_normed)
        gradient = grad_middle + grad_input
        layer_results.append(
            (
                lax.psum_scatter(
                    qkv_grad.astype(jnp.bfloat16), "dp", scatter_dimension=1, tiled=True
                ).astype(jnp.float32),
                lax.psum_scatter(
                    proj_grad.astype(jnp.bfloat16), "dp", scatter_dimension=1, tiled=True
                ).astype(jnp.float32),
                lax.psum_scatter(
                    up_grad.astype(jnp.bfloat16), "dp", scatter_dimension=0, tiled=True
                ).astype(jnp.float32),
                lax.psum_scatter(
                    down_grad.astype(jnp.bfloat16), "dp", scatter_dimension=1, tiled=True
                ).astype(jnp.float32),
            )
        )
        qkv_padded = lax.dynamic_update_slice_in_dim(
            jnp.zeros((3, D), jnp.float32), qkv_bias_part, tensor_rank * column_count, 1
        )
        up_padded = lax.dynamic_update_slice_in_dim(
            jnp.zeros((FF,), jnp.float32), up_bias_part, tensor_rank * hidden_count, 0
        )
        vector_parts.append(
            (
                pre_gain_part,
                pre_bias_part,
                qkv_padded,
                proj_bias_part,
                mid_gain_part,
                mid_bias_part,
                up_padded,
                down_bias_part,
            )
        )
    ordered_vectors = vector_parts[::-1]
    stacked = [jnp.stack([entry[which] for entry in ordered_vectors]) for which in range(8)]
    vector_grads = (
        lax.psum_scatter(stacked[0], ("dp", "mp"), scatter_dimension=1, tiled=True),
        lax.psum_scatter(stacked[1], ("dp", "mp"), scatter_dimension=1, tiled=True),
        lax.psum_scatter(stacked[2], ("dp", "mp"), scatter_dimension=2, tiled=True),
        lax.psum_scatter(stacked[3], ("dp", "mp"), scatter_dimension=1, tiled=True),
        lax.psum_scatter(stacked[4], ("dp", "mp"), scatter_dimension=1, tiled=True),
        lax.psum_scatter(stacked[5], ("dp", "mp"), scatter_dimension=1, tiled=True),
        lax.psum_scatter(stacked[6], ("dp", "mp"), scatter_dimension=1, tiled=True),
        lax.psum_scatter(stacked[7], ("dp", "mp"), scatter_dimension=1, tiled=True),
    )
    ordered_layers = layer_results[::-1]
    qkv_weight_grad = jnp.stack([entry[0] for entry in ordered_layers])
    proj_weight_grad = jnp.stack([entry[1] for entry in ordered_layers])
    up_weight_grad = jnp.stack([entry[2] for entry in ordered_layers])
    down_weight_grad = jnp.stack([entry[3] for entry in ordered_layers])
    return (
        out_hidden,
        gradient,
        vector_grads[0],
        vector_grads[1],
        qkv_weight_grad,
        vector_grads[2],
        proj_weight_grad,
        vector_grads[3],
        vector_grads[4],
        vector_grads[5],
        up_weight_grad,
        vector_grads[6],
        down_weight_grad,
        vector_grads[7],
    )


def solution(mesh):
    return jax.shard_map(
        body,
        mesh=mesh,
        in_specs=(
            P(("dp", "mp"), None),
            P(None, ("dp", "mp")),
            P(None, ("dp", "mp")),
            P(None, None, "dp", "mp"),
            P(None, None, ("dp", "mp")),
            P(None, "mp", "dp"),
            P(None, ("dp", "mp")),
            P(None, ("dp", "mp")),
            P(None, ("dp", "mp")),
            P(None, "dp", "mp"),
            P(None, ("dp", "mp")),
            P(None, "mp", "dp"),
            P(None, ("dp", "mp")),
            P("dp"),
            P(None, "dp"),
            P("dp"),
            P(("dp", "mp"), None),
        ),
        out_specs=(
            P(("dp", "mp"), None),
            P(("dp", "mp"), None),
            P(None, ("dp", "mp")),
            P(None, ("dp", "mp")),
            P(None, None, "dp", "mp"),
            P(None, None, ("dp", "mp")),
            P(None, "mp", "dp"),
            P(None, ("dp", "mp")),
            P(None, ("dp", "mp")),
            P(None, ("dp", "mp")),
            P(None, "dp", "mp"),
            P(None, ("dp", "mp")),
            P(None, "mp", "dp"),
            P(None, ("dp", "mp")),
        ),
        check_vma=False,
    )
```

profile of v0, /device:TPU:0, one launch (start us, length us, event | category | flops | bytes accessed | tf_op | source)
XLA Modules:
  0.0 2345.4 jit_solution(13656360633133587744)
XLA Ops:
  9.7 69.8 %all-gather.8 = f32[32,40,2]{1,2,0:T(2,128)S(1)} all-gather(f32[1,40,2]{1,2,0:T(2,128)S(1)} %bitcast.458), channel_id=1, replica_groups=mesh['dp'=8,'mp'=4] {'dp','mp'}, dimensions={0}, use_global_device_ids=true | all-gather | bytes 10560 | tf_op jit(solution)/shard_map/all_gather | solution.py:140
  80.2 63.5 %all-gather.9 = f32[32,40,2]{1,2,0:T(2,128)S(1)} all-gather(f32[1,40,2]{1,2,0:T(2,128)S(1)} %bitcast.459), channel_id=1, replica_groups=mesh['dp'=8,'mp'=4] {'dp','mp'}, dimensions={0}, use_global_device_ids=true | all-gather | bytes 10560 | tf_op jit(solution)/shard_map/all_gather | solution.py:141
  146.8 92.1 %all_gather.92 = f32[2,3,1280]{1,0,2:T(2,128)S(1)} all-gather(f32[2,3,40]{1,0,2:T(2,128)S(1)} %copy.56), channel_id=1, replica_groups=mesh['dp'=8,'mp'=4] {'dp','mp'}, dimensions={2}, use_global_device_ids=true | all-gather | bytes 31680 | tf_op jit(solution)/shard_map/all_gather | solution.py:142
  242.1 11.8 all-gather.1
  261.8 25.1 %while.74 = (s32[]{:T(128)}, bf16[2,512,4,80]{1,3,2,0:T(8,128)(2,1)S(1)}, s32[2]{0:T(128)S(1)}, s32[1024]{0:T(1024)S(1)}, s32[1024]{0:T(1024)S(1)}, /*index=5*/b...) while((s32[]{:T(128)}, ...), condition=%wide.region_5.6_spmd, body=%wide.region_2.5_spmd.sunk | while | flops 685935104 | bytes 19828936 | solution.py:73
  291.7 20.1 while.77
  320.5 67.5 %all-gather.10 = f32[32,40,2]{1,2,0:T(2,128)S(1)} all-gather(f32[1,40,2]{1,2,0:T(2,128)S(1)} %bitcast.460), channel_id=1, replica_groups=mesh['dp'=8,'mp'=4] {'dp','mp'}, dimensions={0}, use_global_device_ids=true | all-gather | bytes 10560 | tf_op jit(solution)/shard_map/all_gather | solution.py:143
  388.1 64.1 %all-gather.11 = f32[32,40,2]{1,2,0:T(2,128)S(1)} all-gather(f32[1,40,2]{1,2,0:T(2,128)S(1)} %bitcast.461), channel_id=1, replica_groups=mesh['dp'=8,'mp'=4] {'dp','mp'}, dimensions={0}, use_global_device_ids=true | all-gather | bytes 10560 | tf_op jit(solution)/shard_map/all_gather | solution.py:144
  452.3 65.3 %all-gather.12 = f32[32,40,2]{1,2,0:T(2,128)S(1)} all-gather(f32[1,40,2]{1,2,0:T(2,128)S(1)} %bitcast.462), channel_id=1, replica_groups=mesh['dp'=8,'mp'=4] {'dp','mp'}, dimensions={0}, use_global_device_ids=true | all-gather | bytes 10560 | tf_op jit(solution)/shard_map/all_gather | solution.py:145
  523.2 65.4 %all-gather.13 = f32[32,160,2]{1,2,0:T(2,128)S(1)} all-gather(f32[1,160,2]{1,2,0:T(2,128)S(1)} %bitcast.457), channel_id=1, replica_groups=mesh['dp'=8,'mp'=4] {'dp','mp'}, dimensions={0}, use_global_device_ids=true | all-gather | bytes 42240 | tf_op jit(solution)/shard_map/all_gather | solution.py:146
  588.9 12.3 convolution_convert_fusion.10
  602.0 67.4 %all-gather.14 = f32[32,40,2]{1,2,0:T(2,128)S(1)} all-gather(f32[1,40,2]{1,2,0:T(2,128)S(1)} %bitcast.463), channel_id=1, replica_groups=mesh['dp'=8,'mp'=4] {'dp','mp'}, dimensions={0}, use_global_device_ids=true | all-gather | bytes 10560 | tf_op jit(solution)/shard_map/all_gather | solution.py:147
  673.3 16.2 all-gather.5
  689.9 55.5 %all-gather.36.cloned.1.call-done = bf16[1024,1280]{1,0:T(8,128)(2,1)} async-done(((bf16[256,1280]{1,0:T(8,128)(2,1)}), bf16[1024,1280]{1,0:T(8,128)(2,1)}) %all-gather.36.cloned.1.call-update) | async-done | bytes 2621456 | tf_op jit(solution)/shard_map/all_gather | solution.py:183
  754.1 20.1 while.76
  779.4 50.2 %reduce-scatter.41.cloned.1.call-done = bf16[256,1280]{1,0:T(8,128)(2,1)} async-done(((bf16[1024,1280]{1,0:T(8,128)(2,1)}), bf16[256,1280]{1,0:T(8,128)(2,1)}) %reduce-scatter.41.cloned.1.call-update) | async-done | bytes 655376 | tf_op jit(solution)/shard_map/reduce_scatter | solution.py:196
  835.4 28.5 %all-gather.60.cloned.1.call-done = bf16[1,1280,1280]{2,1,0:T(8,128)(2,1)} async-done(((bf16[1,160,1280]{2,1,0:T(8,128)(2,1)}), bf16[1,1280,1280]{2,1,0:T(8,128)(2,1)}) %all-gather.60.cloned.1.call-update) | async-done | bytes 3276816 | tf_op jit(solution)/shard_map/all_gather | solution.py:175
  863.9 57.0 %all-gather.42.cloned.1.call-done = bf16[1024,1280]{1,0:T(8,128)(2,1)} async-done(((bf16[256,1280]{1,0:T(8,128)(2,1)}), bf16[1024,1280]{1,0:T(8,128)(2,1)}) %all-gather.42.cloned.1.call-update) | async-done | bytes 2621456 | tf_op jit(solution)/shard_map/all_gather | solution.py:207
  929.6 46.9 %all-gather.40.cloned.1.call-done = bf16[1024,1280]{1,0:T(8,128)(2,1)} async-done(((bf16[256,1280]{1,0:T(8,128)(2,1)}), bf16[1024,1280]{1,0:T(8,128)(2,1)}) %all-gather.40.cloned.1.call-update) | async-done | bytes 2621456 | tf_op jit(solution)/shard_map/all_gather | solution.py:242
  976.5 33.4 %all-gather.62.cloned.1.call-done = bf16[1,1280,1280]{1,2,0:T(8,128)(2,1)} async-done(((bf16[1,1280,160]{1,2,0:T(8,128)(2,1)}), bf16[1,1280,1280]{1,2,0:T(8,128)(2,1)}) %all-gather.62.cloned.1.call-update) | async-done | bytes 3276816 | tf_op jit(solution)/shard_map/all_gather | solution.py:176
  1009.9 10.2 convert_reduce_fusion
  1026.5 52.2 %reduce-scatter.43.cloned.1.call-done = bf16[256,1280]{1,0:T(8,128)(2,1)} async-done(((bf16[1024,1280]{1,0:T(8,128)(2,1)}), bf16[256,1280]{1,0:T(8,128)(2,1)}) %reduce-scatter.43.cloned.1.call-update) | async-done | bytes 655376 | tf_op jit(solution)/shard_map/reduce_scatter | solution.py:251
  1086.1 26.4 %while.75 = (s32[]{:T(128)}, bf16[2,512,4,80]{1,3,2,0:T(8,128)(2,1)}, s32[2]{0:T(128)S(1)}, s32[1024]{0:T(1024)S(1)}, s32[1024]{0:T(1024)S(1)}, /*index=5*/bf16[...) while((s32[]{:T(128)}, ...), condition=%wide.region_15.16_spmd, body=%wide.region_12.15_spmd.sunk | while | flops 685935104 | bytes 19828936 | solution.py:73
  1117.6 21.8 all-gather.44.cloned.1.call-done
  1144.8 61.5 %while.78 = (s32[]{:T(128)}, f32[1024,4,80]{0,2,1:T(8,128)S(1)}, f32[1024,4,80]{0,2,1:T(8,128)}, f32[2,512,4,80]{1,0,3,2:T(2,128)}, s32[2]{0:T(128)S(1)}, /*inde...) while((s32[]{:T(128)}, f32[1024,4,80]{0,2,1:T(8,128)S(1)}, ...), condition=%wide.region_32.33_spmd.clone, body=%wide.region_30.32_spmd.clone.sunk | while | flops 1713077760 | bytes 76886264 | solution.py:114
  1162.7 12.7 dynamic_update_slice.71
  1193.6 12.7 dynamic_update_slice.71
  1219.1 50.9 %reduce-scatter.45.cloned.1.call-done = bf16[256,1280]{1,0:T(8,128)(2,1)} async-done(((bf16[1024,1280]{1,0:T(8,128)(2,1)}), bf16[256,1280]{1,0:T(8,128)(2,1)}) %reduce-scatter.45.cloned.1.call-update) | async-done | bytes 655376 | tf_op jit(solution)/shard_map/reduce_scatter | solution.py:291
  1275.3 54.6 %all-gather.38.cloned.1.call-done = bf16[1024,1280]{1,0:T(8,128)(2,1)} async-done(((bf16[256,1280]{1,0:T(8,128)(2,1)}), bf16[1024,1280]{1,0:T(8,128)(2,1)}) %all-gather.38.cloned.1.call-update) | async-done | bytes 2621456 | tf_op jit(solution)/shard_map/all_gather | solution.py:207
  1330.0 12.3 convolution_convert_fusion.8
  1343.1 50.2 %reduce-scatter.39.cloned.1.call-done = bf16[256,1280]{1,0:T(8,128)(2,1)} async-done(((bf16[1024,1280]{1,0:T(8,128)(2,1)}), bf16[256,1280]{1,0:T(8,128)(2,1)}) %reduce-scatter.39.cloned.1.call-update) | async-done | bytes 655376 | tf_op jit(solution)/shard_map/reduce_scatter | solution.py:225
  1398.7 50.8 %all-gather.48.cloned.1.call-done = bf16[1024,1280]{1,0:T(8,128)(2,1)} async-done(((bf16[256,1280]{1,0:T(8,128)(2,1)}), bf16[1024,1280]{1,0:T(8,128)(2,1)}) %all-gather.48.cloned.1.call-update) | async-done | bytes 2621456 | tf_op jit(solution)/shard_map/all_gather | solution.py:207
  1458.0 47.2 %all-gather.46.cloned.1.call-done = bf16[1024,1280]{1,0:T(8,128)(2,1)} async-done(((bf16[256,1280]{1,0:T(8,128)(2,1)}), bf16[1024,1280]{1,0:T(8,128)(2,1)}) %all-gather.46.cloned.1.call-update) | async-done | bytes 2621456 | tf_op jit(solution)/shard_map/all_gather | solution.py:242
  1505.2 9.6 convert_reduce_fusion.1
  1521.3 51.0 %reduce-scatter.49.cloned.1.call-done = bf16[256,1280]{1,0:T(8,128)(2,1)} async-done(((bf16[1024,1280]{1,0:T(8,128)(2,1)}), bf16[256,1280]{1,0:T(8,128)(2,1)}) %reduce-scatter.49.cloned.1.call-update) | async-done | bytes 655376 | tf_op jit(solution)/shard_map/reduce_scatter | solution.py:251
  1647.4 61.9 %while.79 = (s32[]{:T(128)}, f32[1024,4,80]{0,2,1:T(8,128)S(1)}, f32[1024,4,80]{0,2,1:T(8,128)}, f32[2,512,4,80]{1,0,3,2:T(2,128)}, s32[2]{0:T(128)S(1)}, /*inde...) while((s32[]{:T(128)}, f32[1024,4,80]{0,2,1:T(8,128)S(1)}, ...), condition=%wide.region_48.49_spmd.clone, body=%wide.region_46.48_spmd.clone.sunk | while | flops 1713077760 | bytes 76886264 | solution.py:114
  1665.7 12.7 dynamic_update_slice.72
  1696.7 12.7 dynamic_update_slice.72
  1751.0 69.2 %reduce-scatter.69.cloned.1.call-done = f32[160,2]{1,0:T(8,128)} async-done(((f32[5120,2]{1,0:T(8,128)}), f32[160,2]{1,0:T(8,128)}) %reduce-scatter.69.cloned.1.call-update) | async-done | bytes 1296
  1821.7 47.6 %reduce-scatter.59.cloned.1.call-done = bf16[160,1280]{1,0:T(8,128)(2,1)} async-done(((bf16[1280,1280]{1,0:T(8,128)(2,1)}), bf16[160,1280]{1,0:T(8,128)(2,1)}) %reduce-scatter.59.cloned.1.call-update) | async-done | bytes 409616 | tf_op jit(solution)/shard_map/reduce_scatter | solution.py:312
  1869.3 50.3 %reduce-scatter.57.cloned.1.call-done = bf16[160,1280]{1,0:T(8,128)(2,1)} async-done(((bf16[1280,1280]{1,0:T(8,128)(2,1)}), bf16[160,1280]{1,0:T(8,128)(2,1)}) %reduce-scatter.57.cloned.1.call-update) | async-done | bytes 409616 | tf_op jit(solution)/shard_map/reduce_scatter | solution.py:312
  1922.1 47.7 %reduce-scatter.63.cloned.1.call-done = bf16[1280,160]{0,1:T(8,128)(2,1)} async-done(((bf16[1280,1280]{0,1:T(8,128)(2,1)}), bf16[1280,160]{0,1:T(8,128)(2,1)}) %reduce-scatter.63.cloned.1.call-update) | async-done | bytes 409616 | tf_op jit(solution)/shard_map/reduce_scatter | solution.py:315
  1969.8 50.3 %reduce-scatter.61.cloned.1.call-done = bf16[1280,160]{0,1:T(8,128)(2,1)} async-done(((bf16[1280,1280]{0,1:T(8,128)(2,1)}), bf16[1280,160]{0,1:T(8,128)(2,1)}) %reduce-scatter.61.cloned.1.call-update) | async-done | bytes 409616 | tf_op jit(solution)/shard_map/reduce_scatter | solution.py:315
  2025.6 33.5 %reduce-scatter.55.cloned.1.call-done = bf16[320,160]{0,1:T(8,128)(2,1)} async-done(((bf16[320,1280]{0,1:T(8,128)(2,1)}), bf16[320,160]{0,1:T(8,128)(2,1)}) %reduce-scatter.55.cloned.1.call-update) | async-done | bytes 102416 | tf_op jit(solution)/shard_map/reduce_scatter | solution.py:309
  2059.1 39.2 %reduce-scatter.53.cloned.1.call-done = bf16[320,160]{0,1:T(8,128)(2,1)} async-done(((bf16[320,1280]{0,1:T(8,128)(2,1)}), bf16[320,160]{0,1:T(8,128)(2,1)}) %reduce-scatter.53.cloned.1.call-update) | async-done | bytes 102416 | tf_op jit(solution)/shard_map/reduce_scatter | solution.py:309
  2100.1 45.3 %reduce-scatter.65.cloned.1.call-done = bf16[160,960]{1,0:T(8,128)(2,1)} async-done(((bf16[1280,960]{1,0:T(8,128)(2,1)}), bf16[160,960]{1,0:T(8,128)(2,1)}) %reduce-scatter.65.cloned.1.call-update) | async-done | bytes 307216
  2149.2 50.5 %reduce-scatter.51.cloned.1.call-done = bf16[256,1280]{1,0:T(8,128)(2,1)} async-done(((bf16[1024,1280]{1,0:T(8,128)(2,1)}), bf16[256,1280]{1,0:T(8,128)(2,1)}) %reduce-scatter.51.cloned.1.call-update) | async-done | bytes 655376 | tf_op jit(solution)/shard_map/reduce_scatter | solution.py:291
  2206.2 123.3 %all-reduce.18.cloned.1.call-done = (f32[2,1280]{1,0:T(2,128)}, f32[2,1280]{1,0:T(2,128)}, f32[2,3,1280]{2,0,1:T(2,128)}, f32[2,1280]{1,0:T(2,128)}, f32[2,1280]...) async-done(((f32[2,1280]{1,0:T(2,128)}, f32[2,1280]{1,0:T(2,128)}, f32[2,3,1280]{2,0,1:T(2,128)}, f32[2,1280]{1,0:T(2,128)}, f32[2,1280]{1,0:T(2,128)}, ...) | async-done | bytes 92176
  (666 shorter events, 434.8 us)
Async XLA Ops:
  7.2 246.6 %all-gather.32.cloned.1.call-start = ((), (), s32[]{:S(2)}) async-start(), calls=%async_computation.19 | async-start | bytes 3276800 | tf_op jit(solution)/shard_map/all_gather | solution.py:183
  8.9 136.7 %copy-start.79 = (f32[256]{0:T(256)}, f32[256]{0:T(256)S(1)}, u32[]{:S(2)}) copy-start(f32[256]{0:T(256)S(1)} %broadcast_multiply_fusion.11) | copy-start | bytes 3076
  8.9 136.7 %copy-start.56 = (bf16[2,3,160,320]{3,2,1,0:T(8,128)(2,1)S(1)}, bf16[2,3,160,320]{3,2,1,0:T(8,128)(2,1)}, u32[]{:S(2)}) copy-start(bf16[2,3,160,320]{3,2,1,0:T(8,128)(2,1)} %param.32) | copy-start | bytes 1843204
  9.2 137.4 %copy-start.99 = (f32[256]{0:T(256)}, f32[256]{0:T(256)S(1)}, u32[]{:S(2)}) copy-start(f32[256]{0:T(256)S(1)} %fusion.208) | copy-start | bytes 3076
  145.6 108.3 %all-gather.52.cloned.1.call-start = ((), (), s32[]{:S(2)}) async-start(), calls=%async_computation.45 | async-start | bytes 3317760 | tf_op jit(solution)/shard_map/all_gather | solution.py:173
  146.6 371.3 %reduce-scatter.33.cloned.1.call-start = ((), (), s32[]{:S(2)}) async-start(), calls=%async_computation.20 | async-start | bytes 3276800 | tf_op jit(solution)/shard_map/reduce_scatter | solution.py:196
  291.2 228.2 %reduce-scatter.47.cloned.1.call-start = ((), (), s32[]{:S(2)}) async-start(), calls=%async_computation.34 | async-start | bytes 3276800 | tf_op jit(solution)/shard_map/reduce_scatter | solution.py:196
  317.3 135.0 %copy-start.123 = (f32[2,40]{1,0:T(2,128)S(1)}, f32[2,40]{1,0:T(2,128)}, u32[]{:S(2)}) copy-start(f32[2,40]{1,0:T(2,128)} %param.37) | copy-start | bytes 964
  317.3 200.6 %copy-start.3 = (f32[256,1280]{1,0:T(8,128)S(1)}, f32[256,1280]{1,0:T(8,128)}, u32[]{:S(2)}) copy-start(f32[256,1280]{1,0:T(8,128)} %param.29) | copy-start | bytes 3932164
  317.3 271.5 %all-gather.54.cloned.1.call-start = ((), (), s32[]{:S(2)}) async-start(), calls=%async_computation.46 | async-start | bytes 3686400 | tf_op jit(solution)/shard_map/all_gather | solution.py:175
  319.4 269.5 %all-gather.56.cloned.1.call-start = ((), (), s32[]{:S(2)}) async-start(), calls=%async_computation.47 | async-start | bytes 3686400 | tf_op jit(solution)/shard_map/all_gather | solution.py:176
  320.4 268.5 %all-gather.34.cloned.1.call-start = ((), (), s32[]{:S(2)}) async-start(), calls=%async_computation.21 | async-start | bytes 3276800 | tf_op jit(solution)/shard_map/all_gather | solution.py:207
  517.8 311.9 %copy-start.62 = (f32[1280]{0:T(1024)}, f32[1280]{0:T(1024)S(1)}, u32[]{:S(2)}) copy-start(f32[1280]{0:T(1024)S(1)} %get-tuple-element.478) | copy-start | bytes 15364
  517.8 563.7 %copy-start.67 = (f32[1280]{0:T(1024)}, f32[1280]{0:T(1024)S(1)}, u32[]{:S(2)}) copy-start(f32[1280]{0:T(1024)S(1)} %get-tuple-element.481) | copy-start | bytes 15364
  517.9 313.4 %copy-start.75 = (f32[1280]{0:T(1024)}, f32[1280]{0:T(1024)S(1)}, u32[]{:S(2)}) copy-start(f32[1280]{0:T(1024)S(1)} %get-tuple-element.483) | copy-start | bytes 15364
  523.1 147.0 %reduce-scatter.35.cloned.1.call-start = ((), (), s32[]{:S(2)}) async-start(), calls=%async_computation.22 | async-start | bytes 3276800 | tf_op jit(solution)/shard_map/reduce_scatter | solution.py:225
  588.8 421.1 %copy-start.115 = (f32[1280]{0:T(1024)}, f32[1280]{0:T(1024)S(1)}, u32[]{:S(2)}) copy-start(f32[1280]{0:T(1024)S(1)} %get-tuple-element.472) | copy-start | bytes 15364
  601.2 88.7 %all-gather.58.cloned.1.call-start = ((), (), s32[]{:S(2)}) async-start(), calls=%async_computation.48 | async-start | bytes 3317760 | tf_op jit(solution)/shard_map/all_gather | solution.py:173
  601.9 143.5 %all-gather.36.cloned.1.call-start = ((), (), s32[]{:S(2)}) async-start(), calls=%async_computation.23 | async-start | bytes 3276800 | tf_op jit(solution)/shard_map/all_gather | solution.py:183
  671.6 158.0 %copy-start.5 = (f32[256,1280]{1,0:T(8,128)}, f32[256,1280]{1,0:T(8,128)S(1)}, u32[]{:S(2)}) copy-start(f32[256,1280]{1,0:T(8,128)S(1)} %get-tuple-element.625) | copy-start | bytes 3932164
  673.1 156.5 %reduce-scatter.41.cloned.1.call-start = ((), (), s32[]{:S(2)}) async-start(), calls=%async_computation.28 | async-start | bytes 3276800 | tf_op jit(solution)/shard_map/reduce_scatter | solution.py:196
  778.6 85.4 %all-gather.60.cloned.1.call-start = ((), (), s32[]{:S(2)}) async-start(), calls=%async_computation.49 | async-start | bytes 3686400 | tf_op jit(solution)/shard_map/all_gather | solution.py:175
  779.1 141.8 %all-gather.42.cloned.1.call-start = ((), (), s32[]{:S(2)}) async-start(), calls=%async_computation.29 | async-start | bytes 3276800 | tf_op jit(solution)/shard_map/all_gather | solution.py:207
  833.2 143.3 %all-gather.40.cloned.1.call-start = ((), (), s32[]{:S(2)}) async-start(), calls=%async_computation.27 | async-start | bytes 3276800 | tf_op jit(solution)/shard_map/all_gather | solution.py:242
  834.8 175.2 %all-gather.62.cloned.1.call-start = ((), (), s32[]{:S(2)}) async-start(), calls=%async_computation.50 | async-start | bytes 3686400 | tf_op jit(solution)/shard_map/all_gather | solution.py:176
  835.4 243.4 %reduce-scatter.43.cloned.1.call-start = ((), (), s32[]{:S(2)}) async-start(), calls=%async_computation.30 | async-start | bytes 3276800 | tf_op jit(solution)/shard_map/reduce_scatter | solution.py:251
  1026.5 113.0 %all-gather.44.cloned.1.call-start = ((), (), s32[]{:S(2)}) async-start(), calls=%async_computation.31 | async-start | bytes 3276800 | tf_op jit(solution)/shard_map/all_gather | solution.py:266
  1084.8 134.3 %reduce-scatter.37.cloned.1.call-start = ((), (), s32[]{:S(2)}) async-start(), calls=%async_computation.24 | async-start | bytes 3276800 | tf_op jit(solution)/shard_map/reduce_scatter | solution.py:196
  1117.5 152.4 %reduce-scatter.45.cloned.1.call-start = ((), (), s32[]{:S(2)}) async-start(), calls=%async_computation.32 | async-start | bytes 3276800 | tf_op jit(solution)/shard_map/reduce_scatter | solution.py:291
  1219.0 111.0 %all-gather.38.cloned.1.call-start = ((), (), s32[]{:S(2)}) async-start(), calls=%async_computation.25 | async-start | bytes 3276800 | tf_op jit(solution)/shard_map/all_gather | solution.py:207
  1275.3 118.0 %reduce-scatter.39.cloned.1.call-start = ((), (), s32[]{:S(2)}) async-start(), calls=%async_computation.26 | async-start | bytes 3276800 | tf_op jit(solution)/shard_map/reduce_scatter | solution.py:225
  1342.3 107.1 %all-gather.48.cloned.1.call-start = ((), (), s32[]{:S(2)}) async-start(), calls=%async_computation.35 | async-start | bytes 3276800 | tf_op jit(solution)/shard_map/all_gather | solution.py:207
  1343.0 162.1 %all-gather.46.cloned.1.call-start = ((), (), s32[]{:S(2)}) async-start(), calls=%async_computation.33 | async-start | bytes 3276800 | tf_op jit(solution)/shard_map/all_gather | solution.py:242
  1398.2 107.0 %copy-start.114 = (f32[1280]{0:T(1024)S(1)}, f32[1280]{0:T(1024)}, u32[]{:S(2)}) copy-start(f32[1280]{0:T(1024)} %copy-done.113) | copy-start | bytes 15364
  1398.2 174.1 %reduce-scatter.49.cloned.1.call-start = ((), (), s32[]{:S(2)}) async-start(), calls=%async_computation.36 | async-start | bytes 3276800 | tf_op jit(solution)/shard_map/reduce_scatter | solution.py:251
  1521.2 120.6 %all-gather.50.cloned.1.call-start = ((), (), s32[]{:S(2)}) async-start(), calls=%async_computation.37 | async-start | bytes 3276800 | tf_op jit(solution)/shard_map/all_gather | solution.py:266
  1577.5 171.0 %reduce-scatter.67.cloned.1.call-start = ((), (), s32[]{:S(2)}) async-start(), calls=%async_computation.52 | async-start | bytes 2949120
  1599.3 220.9 %reduce-scatter.69.cloned.1.call-start = ((), (), s32[]{:S(2)}) async-start(), calls=%async_computation.53 | async-start | bytes 2703360
  1602.4 266.9 %reduce-scatter.59.cloned.1.call-start = ((), (), s32[]{:S(2)}) async-start(), calls=%async_computation.42 | async-start | bytes 3686400 | tf_op jit(solution)/shard_map/reduce_scatter | solution.py:312
  1610.4 309.2 %reduce-scatter.57.cloned.1.call-start = ((), (), s32[]{:S(2)}) async-start(), calls=%async_computation.41 | async-start | bytes 3686400 | tf_op jit(solution)/shard_map/reduce_scatter | solution.py:312
  1618.3 351.4 %reduce-scatter.63.cloned.1.call-start = ((), (), s32[]{:S(2)}) async-start(), calls=%async_computation.44 | async-start | bytes 3686400 | tf_op jit(solution)/shard_map/reduce_scatter | solution.py:315
  1627.2 392.9 %reduce-scatter.61.cloned.1.call-start = ((), (), s32[]{:S(2)}) async-start(), calls=%async_computation.43 | async-start | bytes 3686400 | tf_op jit(solution)/shard_map/reduce_scatter | solution.py:315
  1636.3 422.8 %reduce-scatter.55.cloned.1.call-start = ((), (), s32[]{:S(2)}) async-start(), calls=%async_computation.40 | async-start | bytes 1105920 | tf_op jit(solution)/shard_map/reduce_scatter | solution.py:309
  1641.7 456.5 %reduce-scatter.53.cloned.1.call-start = ((), (), s32[]{:S(2)}) async-start(), calls=%async_computation.39 | async-start | bytes 1105920 | tf_op jit(solution)/shard_map/reduce_scatter | solution.py:309
  1716.5 428.8 %reduce-scatter.65.cloned.1.call-start = ((), (), s32[]{:S(2)}) async-start(), calls=%async_computation.51 | async-start | bytes 2949120
  1738.0 461.7 %reduce-scatter.51.cloned.1.call-start = ((), (), s32[]{:S(2)}) async-start(), calls=%async_computation.38 | async-start | bytes 3276800 | tf_op jit(solution)/shard_map/reduce_scatter | solution.py:291
  1746.2 583.4 %all-reduce.18.cloned.1.call-start = ((), (), s32[]{:S(2)}) async-start(), calls=%async_computation.54 | async-start | bytes 184320
  1919.6 104.8 %copy-start.49 = (bf16[1024,4,80]{0,2,1:T(8,128)(2,1)S(1)}, bf16[1024,4,80]{0,2,1:T(8,128)(2,1)}, u32[]{:S(2)}) copy-start(bf16[1024,4,80]{0,2,1:T(8,128)(2,1)} %copy-done.47) | copy-start | bytes 1966084
  (119 other events, 2440.1 us)
Sparse Core Ops, SparseCore 0:
  145.7 68.6 all-gather.31
  216.9 31.2 all-gather.51
  291.3 49.5 reduce-scatter.32
  343.1 52.1 reduce-scatter.46
  397.5 32.3 all-gather.53
  432.3 32.9 all-gather.55
  523.2 52.3 all-gather.33
  601.3 50.9 reduce-scatter.34
  654.8 35.1 all-gather.57
  691.9 53.4 all-gather.35
  778.7 50.8 reduce-scatter.40
  831.4 32.5 all-gather.59
  866.1 54.8 all-gather.41
  922.9 53.5 all-gather.39
  978.3 31.6 all-gather.61
  1026.6 52.0 reduce-scatter.42
  1084.9 54.5 all-gather.43
  1141.6 50.8 reduce-scatter.36
  1219.1 50.8 reduce-scatter.44
  1275.4 54.4 all-gather.37
  1342.4 50.8 reduce-scatter.38
  1394.9 54.4 all-gather.47
  1451.6 53.5 all-gather.45
  1521.4 50.8 reduce-scatter.48
  1577.6 54.4 all-gather.49
  1635.3 42.4 reduce-scatter.66
  1679.9 140.1 reduce-scatter.68
  1823.6 45.6 reduce-scatter.58
  1872.7 46.8 reduce-scatter.56
  1922.9 46.8 reduce-scatter.62
  1973.2 46.8 reduce-scatter.60
  2023.3 35.7 reduce-scatter.54
  2062.5 35.7 reduce-scatter.52
  2101.6 43.6 reduce-scatter.64
  2147.6 52.0 reduce-scatter.50
  2206.0 123.5 all-reduce.17
where the time goes:
time: 2350 us
  waiting for transfers between devices  1210 us (51%)
  blocking collectives  583 us (25%)
  matrix products  284 us (12%)
  local copies, waits for them, and re-layouts  153 us (7%)
  other arithmetic  86.8 us (4%)
    unnamed x40, waiting for transfers between devices  241 us
    all_gather x4, waiting for transfers between devices, hidden_forward(): all_rows = lax.all_gather(normed, 'mp', axis=0, tiled=True)  162 us
    reduce_scatter x2, waiting for transfers between devices, body(): lax.psum_scatter(jnp.einsum('nf,df->nd', grad_up, matrices[2], preferred_...  103 us
    reduce_scatter x2, waiting for transfers between devices, body(): lax.psum_scatter(jnp.einsum('jnc,jdc->nd', grad_linear, matrices[0], pref...  101 us
    reduce_scatter x2, waiting for transfers between devices, body(): lax.psum_scatter(down_grad.astype(jnp.bfloat16), 'dp', scatter_dimension=...  98 us
    reduce_scatter x2, waiting for transfers between devices, body(): lax.psum_scatter(up_grad.astype(jnp.bfloat16), 'dp', scatter_dimension=0,...  97.9 us
    all_gather x2, waiting for transfers between devices, body(): grad_rows = lax.all_gather(grad_out, 'mp', axis=0, tiled=True)  94.1 us
    all_gather x1, blocking collectives, body(): lax.all_gather(qkv_bias, ('dp', 'mp'), axis=2, tiled=True)  92.1 us
  transfers between devices with their start and end apart: 36, of which 25 were waited for; matrix products, arithmetic and copies ran while one was open for 15% of the time, Pallas kernels for 0%

commit v1 on v0

v1 whole, which is shorter than its diff:
```python
import jax
import jax.numpy as jnp
from jax import lax
from jax.sharding import PartitionSpec as P

D = 1280
HD = 80
LAYERS = 2
EPSILON = 1e-06
F32 = jnp.float32
BF16 = jnp.bfloat16
HIGHEST = lax.Precision.HIGHEST


def normalise(values):
    centre = values - jnp.mean(values, axis=-1, keepdims=True)
    spread = jnp.mean(centre * centre, axis=-1, keepdims=True)
    scale = lax.rsqrt(spread + EPSILON)
    return centre * scale, scale


def norm_backward(values, gain, grad):
    normed, scale = normalise(values)
    inner = grad * gain
    mean_inner = jnp.mean(inner, axis=-1, keepdims=True)
    mean_cross = jnp.mean(inner * normed, axis=-1, keepdims=True)
    grad_values = scale * (inner - mean_inner - normed * mean_cross)
    return grad_values, jnp.sum(grad * normed, axis=0), jnp.sum(grad, axis=0)


def dot(left, right, left_dim, right_dim, kind=F32, precision=None):
    return lax.dot_general(
        left,
        right,
        (((left_dim,), (right_dim,)), ((), ())),
        preferred_element_type=F32,
        precision=precision,
    ).astype(kind)


def rotary_tables(coords):
    quarter = HD // 4
    powers = jnp.arange(quarter, dtype=F32) * (4.0 / HD)
    inverse = 10000.0 ** (-powers)
    height_angle = coords[0].astype(F32)[:, None] * inverse[None, :]
    width_angle = coords[1].astype(F32)[:, None] * inverse[None, :]
    angles = jnp.concatenate([height_angle, width_angle], axis=1)
    angles = jnp.concatenate([angles, angles], axis=1)
    return (jnp.cos(angles)[:, None, :], jnp.sin(angles)[:, None, :])


def rotate(values, cosine, sine):
    half_size = HD // 2
    turned = jnp.concatenate([-values[..., half_size:], values[..., :half_size]], axis=-1)
    return values * cosine + turned * sine


def rotate_back(values, cosine, sine):
    half_size = HD // 2
    turned = jnp.concatenate([-values[..., half_size:], values[..., :half_size]], axis=-1)
    return values * cosine - turned * sine


def masked_scores(queries, key_rows, codes):
    scores = jnp.einsum("qhe,khe->hqk", queries, key_rows, preferred_element_type=F32)
    scores = scores * HD ** (-0.5)
    return jnp.where((codes[:, None] == codes[None, :])[None], scores, -1e30)


def attend_forward(linear, cosine, sine, codes):
    length = linear.shape[0]
    parts = linear.reshape(length, 3, -1, HD)
    queries = rotate(parts[:, 0], cosine, sine).astype(BF16)
    key_rows = rotate(parts[:, 1], cosine, sine).astype(BF16)
    value_rows = parts[:, 2].astype(BF16)
    scores = masked_scores(queries, key_rows, codes)
    row_max = jnp.max(scores, axis=-1, keepdims=True)
    exponent = jnp.exp(scores - row_max)
    totals = jnp.sum(exponent, axis=-1, keepdims=True)
    chances = (exponent / totals).astype(BF16)
    mixed = jnp.einsum("hqk,khe->qhe", chances, value_rows, preferred_element_type=F32)
    return mixed.astype(BF16).reshape(length, -1), (
        queries,
        key_rows,
        value_rows,
        row_max + jnp.log(totals),
    )


def attend_backward(saved, mixed, grad_mixed, cosine, sine, codes):
    queries, key_rows, value_rows, log_totals = saved
    length = queries.shape[0]
    scale = HD ** (-0.5)
    grad_mixed = grad_mixed.reshape(value_rows.shape)
    scores = masked_scores(queries, key_rows, codes)
    chances = jnp.exp(scores - log_totals)
    grad_chance = jnp.einsum("qhe,khe->hqk", grad_mixed, value_rows, preferred_element_type=F32)
    centre = jnp.sum(chances * grad_chance, axis=-1, keepdims=True)
    grad_scores = (chances * (grad_chance - centre)).astype(BF16)
    grad_query = scale * jnp.einsum(
        "hqk,khe->qhe", grad_scores, key_rows, preferred_element_type=F32
    )
    grad_key = scale * jnp.einsum("hqk,qhe->khe", grad_scores, queries, preferred_element_type=F32)
    grad_value = jnp.einsum(
        "hqk,qhe->khe", chances.astype(BF16), grad_mixed, preferred_element_type=F32
    )
    return jnp.concatenate(
        [
            rotate_back(grad_query, cosine, sine).reshape(length, -1),
            rotate_back(grad_key, cosine, sine).reshape(length, -1),
            grad_value.reshape(length, -1),
        ],
        axis=1,
    ).astype(BF16)


def make_body(dp, mp):
    assert mp == 4 and dp >= 2 and dp & (dp - 1) == 0
    count = dp * mp
    high_bits = [1 << b for b in range(1, dp.bit_length() - 1)]

    def across(value, bit):
        return lax.ppermute(value, "dp", [(i, i ^ bit) for i in range(dp)])

    def core_side(value):
        return across(value, 1)

    def line_side(value):
        return lax.ppermute(value, "mp", [(i, i ^ 1) for i in range(mp)])

    def swapped(d, m):
        return (d & ~1 | m >> 1) * mp + ((d & 1) << 1 | m & 1)

    swap_pairs = [(d * mp + m, swapped(d, m)) for d in range(dp) for m in range(mp)]

    def swap(value):
        return lax.ppermute(value, ("dp", "mp"), swap_pairs)

    def gather_weight(mine):
        pair = swap(jnp.stack([mine, core_side(mine)]))
        if len(high_bits) == 2:
            low, high = high_bits
            by_low, by_high = across(pair, low), across(pair, high)
            pieces = [pair, by_low, by_high, across(by_low[:1], high), across(by_high[1:], low)]
        else:
            pieces = [pair]
            for bit in high_bits:
                pieces = pieces + [across(piece, bit) for piece in pieces]
        return jnp.concatenate(pieces, axis=0).reshape(D, mine.shape[-1])

    def scatter_weight(grad):
        blocks = grad.reshape(dp, D // dp, grad.shape[-1])

        def add(*terms):
            total = terms[0].astype(F32)
            for term in terms[1:]:
                total = total + term.astype(F32)
            return total.astype(BF16)

        if len(high_bits) == 2:
            low, high = high_bits
            first = across(blocks[6:7], high)
            second = across(blocks[7:8], low)
            by_low = jnp.concatenate([add(blocks[2:3], first), blocks[3:4]], axis=0)
            by_high = jnp.concatenate([blocks[4:5], add(blocks[5:6], second)], axis=0)
            blocks = add(blocks[:2], across(by_low, low), across(by_high, high))
        else:
            for bit in high_bits[::-1]:
                half = blocks.shape[0] // 2
                blocks = add(blocks[:half], across(blocks[half:], bit))
        blocks = swap(blocks)
        return blocks[0].astype(F32) + core_side(blocks[1]).astype(F32)

    def scatter_vectors(values):
        index = lax.axis_index("dp") * mp + lax.axis_index("mp")
        bit = count // 2
        while bit:
            half = values.shape[0] // 2
            top = (index & bit) != 0
            low, high = values[:half], values[half:]
            sent = jnp.where(top, low, high)
            if bit >= mp:
                got = across(sent, bit // mp)
            else:
                got = lax.ppermute(sent, "mp", [(i, i ^ bit) for i in range(mp)])
            values = jnp.where(top, high, low) + got
            bit //= 2
        return values[0]

    def gather_rows(mine):
        near = core_side(mine)
        far = line_side(mine)
        return [mine, near, far, core_side(far)]

    def scatter_rows(part):
        far = part(2) + core_side(part(3).astype(BF16)).astype(F32)
        far = line_side(far.astype(BF16))
        near = part(0) + core_side(part(1).astype(BF16)).astype(F32)
        return near + far.astype(F32)

    def body(
        hidden_in,
        pre_gain,
        pre_bias,
        qkv_weight,
        qkv_bias,
        proj_weight,
        proj_bias,
        mid_gain,
        mid_bias,
        up_weight,
        up_bias,
        down_weight,
        down_bias,
        picture_ids,
        positions,
        pad_mask,
        cotangent,
    ):
        dp_at, mp_at = lax.axis_index("dp"), lax.axis_index("mp")
        group_at = (dp_at & ~1) | (mp_at >> 1)
        quarter_at = ((dp_at & 1) << 1) | (mp_at & 1)
        depth = D // dp
        columns = qkv_weight.shape[3]
        units = up_weight.shape[2]
        heads = columns // HD

        place = jnp.arange(D, dtype=jnp.int32)
        moved = ((place // depth) ^ group_at) * depth + place % depth
        reorder = place[:, None] == moved[None, :]
        reorder_low = reorder.astype(BF16)
        reorder_full = reorder.astype(F32)

        def turn_low(values):
            return dot(values.astype(BF16), reorder_low, 1, 0)

        hidden = turn_low(swap(hidden_in.astype(BF16)))
        weights = []
        for layer in range(LAYERS):
            weights.append(
                (
                    gather_weight(qkv_weight[layer].transpose(1, 0, 2).reshape(depth, 3 * columns)),
                    gather_weight(proj_weight[layer].T),
                    gather_weight(up_weight[layer]),
                    gather_weight(down_weight[layer].T),
                )
            )

        wide = (pre_gain, pre_bias, proj_bias, mid_gain, mid_bias, down_bias)
        packed = jnp.concatenate(
            [item.reshape(-1) for item in wide] + [qkv_bias.reshape(-1), up_bias.reshape(-1)]
        )
        packed = lax.all_gather(packed, ("dp", "mp"), axis=0, tiled=False)
        each = D // count
        wide_count = len(wide) * LAYERS
        split = (wide_count + 3 * LAYERS) * each
        vectors = packed[:, :split].reshape(count, -1, each).transpose(1, 0, 2).reshape(-1, D)
        wide_all = dot(vectors[:wide_count], reorder_full, 1, 0, precision=HIGHEST)
        wide_all = wide_all.reshape(len(wide), LAYERS, D)
        pre_gain_all, pre_bias_all, proj_bias_all, mid_gain_all, mid_bias_all, down_bias_all = (
            wide_all[i] for i in range(len(wide))
        )
        qkv_bias_mine = lax.dynamic_slice_in_dim(
            vectors[wide_count:], quarter_at * columns, columns, 1
        ).reshape(LAYERS, 3 * columns)
        up_all = packed[:, split:].reshape(count, LAYERS, -1).transpose(1, 0, 2)
        up_bias_mine = lax.dynamic_slice_in_dim(
            up_all.reshape(LAYERS, -1), quarter_at * units, units, 1
        )

        length = picture_ids.shape[0]
        quarter = length // mp
        row_at = jnp.arange(length, dtype=jnp.int32)
        codes = jnp.where(pad_mask == 1, picture_ids, 1024 + row_at)
        row_facts = swap(jnp.concatenate([codes[None], positions], axis=0))
        row_facts = jnp.concatenate(
            [
                lax.dynamic_slice_in_dim(row_facts, (quarter_at ^ which) * quarter, quarter, 1)
                for which in (0, 2, 1, 3)
            ],
            axis=1,
        )
        codes = row_facts[0]
        cosine, sine = rotary_tables(row_facts[1:])

        kept = []
        for layer in range(LAYERS):
            w_qkv, w_proj, w_up, w_down = weights[layer]
            start = hidden
            normed = normalise(hidden)[0] * pre_gain_all[layer] + pre_bias_all[layer]
            rows = gather_rows(normed.astype(BF16))
            attn_rows = jnp.concatenate(rows, axis=0)
            linear = dot(attn_rows, w_qkv, 1, 0) + qkv_bias_mine[layer]
            mixed, saved = attend_forward(linear, cosine, sine, codes)
            attended = scatter_rows(
                lambda i, a=mixed, w=w_proj: dot(a[i * quarter : (i + 1) * quarter], w, 1, 1)
            )
            middle = hidden + (attended + proj_bias_all[layer])
            normed = normalise(middle)[0] * mid_gain_all[layer] + mid_bias_all[layer]
            rows = gather_rows(normed.astype(BF16))
            mid_rows = jnp.concatenate(rows, axis=0)
            upward = dot(mid_rows, w_up, 1, 0) + up_bias_mine[layer]
            sigmoid = 1.0 / (1.0 + jnp.exp(-1.702 * upward))
            active = (upward * sigmoid).astype(BF16)
            slope = (sigmoid + 1.702 * upward * sigmoid * (1.0 - sigmoid)).astype(BF16)
            output = scatter_rows(
                lambda i, a=active, w=w_down: dot(a[i * quarter : (i + 1) * quarter], w, 1, 1)
            )
            hidden = middle + (output + down_bias_all[layer])
            kept.append((start, attn_rows, mixed, saved, middle, mid_rows, active, slope))

        out_hidden = swap(turn_low(hidden).astype(BF16)).astype(F32)
        gradient = turn_low(swap(cotangent.astype(BF16)))
        grads = []
        parts = []
        for layer in reversed(range(LAYERS)):
            w_qkv, w_proj, w_up, w_down = weights[layer]
            start, attn_rows, mixed, saved, middle, mid_rows, active, slope = kept[layer]
            grad_out = gradient.astype(BF16)
            down_bias_part = jnp.sum(grad_out.astype(F32), axis=0)
            grad_rows = jnp.concatenate(gather_rows(grad_out), axis=0)
            grad_up = (dot(grad_rows, w_down, 1, 0) * slope.astype(F32)).astype(BF16)
            grad_normed = scatter_rows(
                lambda i, a=grad_up, w=w_up: dot(a[i * quarter : (i + 1) * quarter], w, 1, 1)
            )
            down_grad = scatter_weight(dot(grad_rows, active, 0, 0, BF16))
            up_bias_part = jnp.sum(grad_up.astype(F32), axis=0)
            up_grad = scatter_weight(dot(mid_rows, grad_up, 0, 0, BF16))
            grad_middle, mid_gain_part, mid_bias_part = norm_backward(
                middle, mid_gain_all[layer], grad_normed
            )
            gradient = gradient + grad_middle
            grad_out = gradient.astype(BF16)
            proj_bias_part = jnp.sum(grad_out.astype(F32), axis=0)
            grad_rows = jnp.concatenate(gather_rows(grad_out), axis=0)
            grad_mixed = dot(grad_rows, w_proj, 1, 0, BF16)
            proj_grad = scatter_weight(dot(grad_rows, mixed, 0, 0, BF16))
            grad_linear = attend_backward(saved, mixed, grad_mixed, cosine, sine, codes)
            grad_normed = scatter_rows(
                lambda i, a=grad_linear, w=w_qkv: dot(a[i * quarter : (i + 1) * quarter], w, 1, 1)
            )
            qkv_bias_part = jnp.sum(grad_linear.astype(F32), axis=0)
            qkv_grad = scatter_weight(dot(attn_rows, grad_linear, 0, 0, BF16))
            grad_start, pre_gain_part, pre_bias_part = norm_backward(
                start, pre_gain_all[layer], grad_normed
            )
            gradient = gradient + grad_start
            grads.append(
                (
                    qkv_grad.reshape(depth, 3, columns).transpose(1, 0, 2),
                    proj_grad.T,
                    up_grad,
                    down_grad.T,
                )
            )
            parts.append(
                (
                    (
                        pre_gain_part,
                        pre_bias_part,
                        proj_bias_part,
                        mid_gain_part,
                        mid_bias_part,
                        down_bias_part,
                    ),
                    qkv_bias_part.reshape(3, columns),
                    up_bias_part,
                )
            )
        grads, parts = grads[::-1], parts[::-1]
        grad_hidden = swap(turn_low(gradient).astype(BF16)).astype(F32)

        stacked = jnp.stack([part[0][i] for i in range(len(wide)) for part in parts])
        stacked = dot(stacked, reorder_full, 1, 0, precision=HIGHEST)
        qkv_padded = lax.dynamic_update_slice_in_dim(
            jnp.zeros((LAYERS * 3, D), F32),
            jnp.concatenate([part[1] for part in parts], axis=0),
            quarter_at * columns,
            1,
        )
        up_padded = lax.dynamic_update_slice_in_dim(
            jnp.zeros((LAYERS, units * mp), F32),
            jnp.stack([part[2] for part in parts]),
            quarter_at * units,
            1,
        )
        by_owner = jnp.concatenate([stacked, qkv_padded], axis=0).reshape(-1, count, each)
        by_owner = jnp.concatenate(
            [
                by_owner.transpose(1, 0, 2).reshape(count, -1),
                up_padded.reshape(LAYERS, count, -1).transpose(1, 0, 2).reshape(count, -1),
            ],
            axis=1,
        )
        mine = scatter_vectors(by_owner)
        wide_grads = mine[: wide_count * each].reshape(len(wide), LAYERS, each)
        qkv_bias_grad = mine[wide_count * each : split].reshape(LAYERS, 3, each)
        up_bias_grad = mine[split:].reshape(LAYERS, -1)
        matrices = [jnp.stack([entry[i] for entry in grads]) for i in range(4)]
        return (
            out_hidden,
            grad_hidden,
            wide_grads[0],
            wide_grads[1],
            matrices[0],
            qkv_bias_grad,
            matrices[1],
            wide_grads[2],
            wide_grads[3],
            wide_grads[4],
            matrices[2],
            up_bias_grad,
            matrices[3],
            wide_grads[5],
        )

    return body


def solution(mesh):
    rows = P(("dp", "mp"), None)
    vector = P(None, ("dp", "mp"))
    vectors = P(None, None, ("dp", "mp"))
    qkv = P(None, None, "dp", "mp")
    tall = P(None, "mp", "dp")
    broad = P(None, "dp", "mp")
    return jax.shard_map(
        make_body(mesh.shape["dp"], mesh.shape["mp"]),
        mesh=mesh,
        in_specs=(
            rows,
            vector,
            vector,
            qkv,
            vectors,
            tall,
            vector,
            vector,
            vector,
            broad,
            vector,
            tall,
            vector,
            P("dp"),
            P(None, "dp"),
            P("dp"),
            rows,
        ),
        out_specs=(
            rows,
            rows,
            vector,
            vector,
            qkv,
            vectors,
            tall,
            vector,
            vector,
            vector,
            broad,
            vector,
            tall,
            vector,
        ),
        check_vma=False,
    )
```

time: 2350 us -> 1050 us (0.45)
  waiting for transfers between devices: 1210 us -> 415 us
  blocking collectives: 583 us -> 0 us
  starting transfers between devices: 3.29 us -> 210 us
  local copies, waits for them, and re-layouts: 153 us -> 75.5 us
  matrix products: 284 us -> 220 us
    all_gather x10 -> x0, blocking collectives: 583 us -> none  [the longest x1 92.1 us: body(): lax.all_gather(qkv_bias, ('dp', 'mp'), axis=2, tiled=True)]
    reduce_scatter x16 -> x0, waiting for transfers between devices: 574 us -> none  [the longest x2 103 us: body(): lax.psum_scatter(jnp.einsum('nf,df->nd', grad_up, matrices[2], preferred_...]
    all_gather x16 -> x0, waiting for transfers between devices: 396 us -> none  [the longest x4 162 us: hidden_forward(): all_rows = lax.all_gather(normed, 'mp', axis=0, tiled=True)]
    ppermute x0 -> x154, waiting for transfers between devices: none -> 307 us  [the longest x115 210 us: across(): return lax.ppermute(value, 'dp', [(i, i ^ bit) for i in range(dp)])]
    ppermute x0 -> x154, starting transfers between devices: none -> 210 us  [the longest x115 120 us: across(): return lax.ppermute(value, 'dp', [(i, i ^ bit) for i in range(dp)])]
    unnamed x40 -> x2, waiting for transfers between devices: 241 us -> 108 us
    dynamic_update_slice x12 -> x1, local copies, waits for them, and re-layouts: 54.1 us -> 0.31 us  [body(): lax.dynamic_update_slice_in_dim(jnp.zeros((LAYERS * 3, D), F32), jnp.conc...]
    dot_general x58 -> x65, matrix products: 261 us -> 220 us  [the longest x53 144 us: dot(): lax.dot_general(left, right, (((left_dim,), (right_dim,)), ((), ())), pre...]
  transfers between devices with their start and end apart: 36 -> 155, of which waited for: 25 -> 49; matrix products, arithmetic and copies ran while one was open for 15% -> 29% of each run, Pallas kernels for 0% -> 0%
where the time goes in v1:
time: 1050 us; the launch traced here: 1030 us
  waiting for transfers between devices  415 us (40%)
  matrix products  220 us (21%)
  starting transfers between devices  210 us (20%)
  other arithmetic  90.7 us (9%)
  local copies, waits for them, and re-layouts  75.5 us (7%)
  between operations  18.2 us (2%)
    ppermute x115, waiting for transfers between devices, across(): return lax.ppermute(value, 'dp', [(i, i ^ bit) for i in range(dp)])  210 us
    dot_general x53, matrix products, dot(): lax.dot_general(left, right, (((left_dim,), (right_dim,)), ((), ())), pre...  144 us
    ppermute x115, starting transfers between devices, across(): return lax.ppermute(value, 'dp', [(i, i ^ bit) for i in range(dp)])  120 us
    unnamed x2, waiting for transfers between devices  108 us
    ppermute x16, waiting for transfers between devices, line_side(): return lax.ppermute(value, 'mp', [(i, i ^ 1) for i in range(mp)])  81.5 us
    ppermute x21, starting transfers between devices, swap(): return lax.ppermute(value, ('dp', 'mp'), swap_pairs)  75.6 us
    unnamed x406, local copies, waits for them, and re-layouts  29.3 us
  transfers between devices with their start and end apart: 155, of which 49 were waited for; matrix products, arithmetic and copies ran while one was open for 29% of the time, Pallas kernels for 0%

profile of v1, /device:TPU:0, one launch (start us, length us, event | category | flops | bytes accessed | tf_op | source)
XLA Modules:
  0.0 1028.9 jit_solution(5074835208850861943)
XLA Ops:
  25.9 6.6 collective-permute-start
  40.3 108.1 %all-reduce.3.cloned.1.call-done = f32[33280]{0:T(1024)} async-done(((f32[33280]{0:T(1024)}), f32[33280]{0:T(1024)}) %all-reduce.3.cloned.1.call-update) | async-done | bytes 133136
  173.7 5.9 collective-permute-done.15
  185.0 10.4 %collective-permute-start.1 = (bf16[256,1280]{1,0:T(8,128)(2,1)S(1)}, bf16[256,1280]{1,0:T(8,128)(2,1)S(1)}, u32[]{:S(2)}, u32[]{:S(2)}) collective-permute-start(bf16[256,1280]{1,0:T(8,128)(2,1)S(1)} %add_convert_fusion.6), channel_id=1, source_target_pairs={{0,4},{4,0},{8,12},{12,8},{16,20},{20,16},{24,28},{28,24},{1,5},{5... | collective-permute-start | bytes 1966088 | tf_op jit(solution)/shard_map/ppermute | solution.py:123
  198.2 7.5 collective-permute-done.8
  205.7 18.5 %collective-permute-start.30 = (bf16[2,160,1280]{2,1,0:T(8,128)(2,1)}, bf16[2,160,1280]{2,1,0:T(8,128)(2,1)}, u32[]{:S(2)}, u32[]{:S(2)}) collective-permute-start(bf16[2,160,1280]{2,1,0:T(8,128)(2,1)} %pad_maximum_fusion.14), channel_id=1, source_target_pairs={{0,0},{1,1},{2,4},{3,5},{4,2},{5,3},{6,6},{7,7},{8,8},{9,9},{10,12... | collective-permute-start | bytes 2457608 | tf_op jit(solution)/shard_map/ppermute | solution.py:137
  229.9 7.5 fusion.188
  237.4 8.0 fusion
  245.4 9.1 fusion.67
  265.5 11.8 %collective-permute-done.26 = bf16[2,160,1280]{2,1,0:T(8,128)(2,1)S(1)} collective-permute-done((bf16[2,160,1280]{2,1,0:T(8,128)(2,1)}, bf16[2,160,1280]{2,1,0:T(8,128)(2,1)S(1)}, u32[]{:S(2)}, u32[]{:S(2)}) %collective-permute-start.26) | collective-permute-done | bytes 819232 | tf_op jit(solution)/shard_map/ppermute | solution.py:123
  281.6 12.8 %collective-permute-done.32 = bf16[2,160,1280]{2,1,0:T(8,128)(2,1)S(1)} collective-permute-done((bf16[2,160,1280]{2,1,0:T(8,128)(2,1)}, bf16[2,160,1280]{2,1,0:T(8,128)(2,1)S(1)}, u32[]{:S(2)}, u32[]{:S(2)}) %collective-permute-start.32) | collective-permute-done | bytes 819232 | tf_op jit(solution)/shard_map/ppermute | solution.py:123
  303.4 10.8 %collective-permute-done.33 = bf16[1,160,1280]{2,1,0:T(8,128)(2,1)S(1)} collective-permute-done((bf16[1,160,1280]{2,1,0:T(8,128)(2,1)S(1)}, bf16[1,160,1280]{2,1,0:T(8,128)(2,1)S(1)}, u32[]{:S(2)}, u32[]{:S(2)}) %collective-permute-start.33) | collective-permute-done | bytes 409632 | tf_op jit(solution)/shard_map/ppermute | solution.py:123
  318.3 8.1 multiply_convert_fusion.5
  364.6 6.5 collective-permute-done.51
  377.1 8.7 collective-permute-start.38
  388.6 7.5 collective-permute-done.45
  396.1 6.5 collective-permute-start.75
  402.7 7.9 collective-permute-start.66
  417.0 7.8 fusion.191
  424.9 8.0 fusion.1
  432.9 9.1 fusion.66
  455.7 12.4 %collective-permute-done.61 = bf16[2,160,1280]{2,1,0:T(8,128)(2,1)S(1)} collective-permute-done((bf16[2,160,1280]{2,1,0:T(8,128)(2,1)}, bf16[2,160,1280]{2,1,0:T(8,128)(2,1)S(1)}, u32[]{:S(2)}, u32[]{:S(2)}) %collective-permute-start.61) | collective-permute-done | bytes 819232 | tf_op jit(solution)/shard_map/ppermute | solution.py:123
  469.8 15.9 %collective-permute-done.67 = bf16[2,160,1280]{2,1,0:T(8,128)(2,1)S(1)} collective-permute-done((bf16[2,160,1280]{2,1,0:T(8,128)(2,1)}, bf16[2,160,1280]{2,1,0:T(8,128)(2,1)S(1)}, u32[]{:S(2)}, u32[]{:S(2)}) %collective-permute-start.67) | collective-permute-done | bytes 819232 | tf_op jit(solution)/shard_map/ppermute | solution.py:123
  491.5 6.3 collective-permute-done.69
  507.6 7.9 multiply_convert_fusion.4
  515.5 10.0 convert_reduce_fusion
  545.6 8.8 collective-permute-done.136
  562.4 10.8 %collective-permute-done.151 = bf16[2,160,1280]{2,1,0:T(8,128)(2,1)S(1)} collective-permute-done((bf16[2,160,1280]{2,1,0:T(8,128)(2,1)S(1)}, bf16[2,160,1280]{2,1,0:T(8,128)(2,1)S(1)}, u32[]{:S(2)}, u32[]{:S(2)}) %collective-permute-start.151) | collective-permute-done | bytes 819232 | tf_op jit(solution)/shard_map/ppermute | solution.py:123
  577.4 7.9 collective-permute-start.152
  592.8 6.5 collective-permute-done.81
  613.5 22.4 %collective-permute-done.83 = bf16[256,1280]{1,0:T(8,128)(2,1)S(1)} collective-permute-done((bf16[256,1280]{1,0:T(8,128)(2,1)S(1)}, bf16[256,1280]{1,0:T(8,128)(2,1)S(1)}, u32[]{:S(2)}, u32[]{:S(2)}) %collective-permute-start.83) | collective-permute-done | bytes 655392 | tf_op jit(solution)/shard_map/ppermute | solution.py:129
  648.4 10.7 %multiply_reduce_fusion.1 = (f32[4,1024]{1,0:T(4,128)S(1)}, f32[4,1024,1024]{1,2,0:T(8,128)}) fusion(f32[4,1024,1024]{1,2,0:T(8,128)S(1)} %bitcast.467, f32[4,1024]{1,0:T(4,128)S(1)} %log_add_fusion.1, bf16[1024,4,80]{0,2,1:T(8,128)(2,1)} %bitcast.501, f32[1024,3,4,80]{0,3,2,1:T(8,128)} %bitcast.485), kind=kOutput, calls=%fused_computation.4 | convolution fusion | flops 683667456 | bytes 34897920 | tf_op jit(solution)/shard_map/qhe,khe->hqk/dot_general | solution.py:97
  659.1 8.1 multiply_convert_fusion.1
  699.4 8.9 collective-permute-done.127
  712.0 16.9 %collective-permute-done.87 = bf16[256,1280]{1,0:T(8,128)(2,1)S(1)} collective-permute-done((bf16[256,1280]{1,0:T(8,128)(2,1)S(1)}, bf16[256,1280]{1,0:T(8,128)(2,1)S(1)}, u32[]{:S(2)}, u32[]{:S(2)}) %collective-permute-start.87) | collective-permute-done | bytes 655392 | tf_op jit(solution)/shard_map/ppermute | solution.py:129
  734.6 9.9 collective-permute-done.113
  752.5 11.4 %collective-permute-start.117 = (bf16[160,960]{1,0:T(8,128)(2,1)S(1)}, bf16[160,960]{1,0:T(8,128)(2,1)S(1)}, u32[]{:S(2)}, u32[]{:S(2)}) collective-permute-start(bf16[160,960]{1,0:T(8,128)(2,1)S(1)} %slice_bitcast_fusion.42), channel_id=1, source_target_pairs={{0,4},{4,0},{8,12},{12,8},{16,20},{20,16},{24,28},{28,24},{1,5},{5... | collective-permute-start | bytes 921608 | tf_op jit(solution)/shard_map/ppermute | solution.py:123
  764.0 9.2 convert_reduce_fusion.1
  789.6 10.1 collective-permute-done.130
  801.3 9.0 collective-permute-done.142
  813.0 15.6 %collective-permute-done.133 = bf16[2,160,1280]{2,1,0:T(8,128)(2,1)S(1)} collective-permute-done((bf16[2,160,1280]{2,1,0:T(8,128)(2,1)S(1)}, bf16[2,160,1280]{2,1,0:T(8,128)(2,1)S(1)}, u32[]{:S(2)}, u32[]{:S(2)}) %collective-permute-start.133) | collective-permute-done | bytes 819232 | tf_op jit(solution)/shard_map/ppermute | solution.py:123
  831.1 7.9 collective-permute-start.134
  855.7 14.6 %collective-permute-done.95 = bf16[256,1280]{1,0:T(8,128)(2,1)} collective-permute-done((bf16[256,1280]{1,0:T(8,128)(2,1)S(1)}, bf16[256,1280]{1,0:T(8,128)(2,1)}, u32[]{:S(2)}, u32[]{:S(2)}) %collective-permute-start.95) | collective-permute-done | bytes 655392 | tf_op jit(solution)/shard_map/ppermute | solution.py:129
  880.9 9.7 fusion.63
  890.7 9.8 multiply_reduce_fusion
  900.4 7.9 multiply_convert_fusion
  961.4 11.4 %collective-permute-done.99 = bf16[256,1280]{1,0:T(8,128)(2,1)S(1)} collective-permute-done((bf16[256,1280]{1,0:T(8,128)(2,1)S(1)}, bf16[256,1280]{1,0:T(8,128)(2,1)S(1)}, u32[]{:S(2)}, u32[]{:S(2)}) %collective-permute-start.99) | collective-permute-done | bytes 655392 | tf_op jit(solution)/shard_map/ppermute | solution.py:129
  993.8 14.6 %collective-permute-done.104 = f32[2,1040]{1,0:T(2,128)S(1)} collective-permute-done((f32[2,1040]{1,0:T(2,128)S(1)}, f32[2,1040]{1,0:T(2,128)S(1)}, u32[]{:S(2)}, u32[]{:S(2)}) %collective-permute-start.104) | collective-permute-done | bytes 8352 | tf_op jit(solution)/shard_map/ppermute | solution.py:185
  (998 shorter events, 428.8 us)
Async XLA Ops:
  7.2 141.2 %all-reduce.3.cloned.1.call-start = ((), (), s32[]{:S(2)}) async-start(), calls=%async_computation | async-start | bytes 270336
  8.7 28.7 %collective-permute-start.10 = (s32[3,1024]{1,0:T(4,128)S(1)}, s32[3,1024]{1,0:T(4,128)S(1)}, u32[]{:S(2)}, u32[]{:S(2)}) collective-permute-start(s32[3,1024]{1,0:T(4,128)S(1)} %pad_add_fusion), channel_id=1, source_target_pairs={{0,0},{1,1},{2,4},{3,5},{4,2},{5,3},{6,6},{7,7},{8,8},{9,9},{10,12... | collective-permute-start | bytes 36872 | tf_op jit(solution)/shard_map/ppermute | solution.py:137
  18.3 135.3 %collective-permute-start.11 = (bf16[160,320]{1,0:T(8,128)(2,1)S(1)}, bf16[160,320]{1,0:T(8,128)(2,1)S(1)}, u32[]{:S(2)}, u32[]{:S(2)}) collective-permute-start(bf16[160,320]{1,0:T(8,128)(2,1)S(1)} %get-tuple-element.246), channel_id=1, source_target_pairs={{0,4},{4,0},{8,12},{12,8},{16,20},{20,16},{24,28},{28,24},{1,5},{5... | collective-permute-start | bytes 307208 | tf_op jit(solution)/shard_map/ppermute | solution.py:123
  25.9 131.5 %collective-permute-start = (bf16[256,1280]{1,0:T(8,128)(2,1)}, bf16[256,1280]{1,0:T(8,128)(2,1)}, u32[]{:S(2)}, u32[]{:S(2)}) collective-permute-start(bf16[256,1280]{1,0:T(8,128)(2,1)} %convert_element_type.728), channel_id=1, source_target_pairs={{0,0},{1,1},{2,4},{3,5},{4,2},{5,3},{6,6},{7,7},{8,8},{9,9},{10,12... | collective-permute-start | bytes 1966088 | tf_op jit(solution)/shard_map/ppermute | solution.py:137
  34.0 121.1 %collective-permute-start.4 = (bf16[160,960]{1,0:T(8,128)(2,1)S(1)}, bf16[160,960]{1,0:T(8,128)(2,1)S(1)}, u32[]{:S(2)}, u32[]{:S(2)}) collective-permute-start(bf16[160,960]{1,0:T(8,128)(2,1)S(1)} %reshape.624), channel_id=1, source_target_pairs={{0,4},{4,0},{8,12},{12,8},{16,20},{20,16},{24,28},{28,24},{1,5},{5... | collective-permute-start | bytes 921608 | tf_op jit(solution)/shard_map/ppermute | solution.py:123
  35.3 126.9 %collective-permute-start.23 = (bf16[160,1280]{1,0:T(8,128)(2,1)}, bf16[160,1280]{1,0:T(8,128)(2,1)}, u32[]{:S(2)}, u32[]{:S(2)}) collective-permute-start(bf16[160,1280]{1,0:T(8,128)(2,1)} %get-tuple-element.222), channel_id=1, source_target_pairs={{0,4},{4,0},{8,12},{12,8},{16,20},{20,16},{24,28},{28,24},{1,5},{5... | collective-permute-start | bytes 1228808 | tf_op jit(solution)/shard_map/ppermute | solution.py:123
  37.4 130.4 %collective-permute-start.29 = (bf16[160,1280]{1,0:T(8,128)(2,1)}, bf16[160,1280]{1,0:T(8,128)(2,1)}, u32[]{:S(2)}, u32[]{:S(2)}) collective-permute-start(bf16[160,1280]{1,0:T(8,128)(2,1)} %get-tuple-element.228), channel_id=1, source_target_pairs={{0,4},{4,0},{8,12},{12,8},{16,20},{20,16},{24,28},{28,24},{1,5},{5... | collective-permute-start | bytes 1228808 | tf_op jit(solution)/shard_map/ppermute | solution.py:123
  162.2 33.3 %collective-permute-start.2 = (bf16[256,1280]{1,0:T(8,128)(2,1)S(1)}, bf16[256,1280]{1,0:T(8,128)(2,1)S(1)}, u32[]{:S(2)}, u32[]{:S(2)}) collective-permute-start(bf16[256,1280]{1,0:T(8,128)(2,1)S(1)} %add_convert_fusion.6), channel_id=1, source_target_pairs={{0,1},{1,0},{2,3},{3,2},{4,5},{5,4},{6,7},{7,6},{8,9},{9,8},{10,11... | collective-permute-start | bytes 1966088 | tf_op jit(solution)/shard_map/ppermute | solution.py:129
  167.2 29.2 %collective-permute-start.7 = (bf16[2,160,960]{2,1,0:T(8,128)(2,1)S(1)}, bf16[2,160,960]{2,1,0:T(8,128)(2,1)S(1)}, u32[]{:S(2)}, u32[]{:S(2)}) collective-permute-start(bf16[2,160,960]{2,1,0:T(8,128)(2,1)S(1)} %collective-permute-done.5), channel_id=1, source_target_pairs={{0,16},{4,20},{8,24},{12,28},{16,0},{20,4},{24,8},{28,12},{1,17},{... | collective-permute-start | bytes 1843208 | tf_op jit(solution)/shard_map/ppermute | solution.py:123
  167.9 27.7 %collective-permute-start.6 = (bf16[2,160,960]{2,1,0:T(8,128)(2,1)S(1)}, bf16[2,160,960]{2,1,0:T(8,128)(2,1)S(1)}, u32[]{:S(2)}, u32[]{:S(2)}) collective-permute-start(bf16[2,160,960]{2,1,0:T(8,128)(2,1)S(1)} %collective-permute-done.5), channel_id=1, source_target_pairs={{0,8},{4,12},{8,0},{12,4},{16,24},{20,28},{24,16},{28,20},{1,9},{5... | collective-permute-start | bytes 1843208 | tf_op jit(solution)/shard_map/ppermute | solution.py:123
  170.4 85.5 %collective-permute-start.24 = (bf16[2,160,1280]{2,1,0:T(8,128)(2,1)S(1)}, bf16[2,160,1280]{2,1,0:T(8,128)(2,1)}, u32[]{:S(2)}, u32[]{:S(2)}) collective-permute-start(bf16[2,160,1280]{2,1,0:T(8,128)(2,1)S(1)} %pad_maximum_fusion.13), channel_id=1, source_target_pairs={{0,0},{1,1},{2,4},{3,5},{4,2},{5,3},{6,6},{7,7},{8,8},{9,9},{10,12... | collective-permute-start | bytes 2457608 | tf_op jit(solution)/shard_map/ppermute | solution.py:137
  185.0 39.2 %collective-permute-start.1 = (bf16[256,1280]{1,0:T(8,128)(2,1)S(1)}, bf16[256,1280]{1,0:T(8,128)(2,1)S(1)}, u32[]{:S(2)}, u32[]{:S(2)}) collective-permute-start(bf16[256,1280]{1,0:T(8,128)(2,1)S(1)} %add_convert_fusion.6), channel_id=1, source_target_pairs={{0,4},{4,0},{8,12},{12,8},{16,20},{20,16},{24,28},{28,24},{1,5},{5... | collective-permute-start | bytes 1966088 | tf_op jit(solution)/shard_map/ppermute | solution.py:123
  195.4 28.9 %collective-permute-start.3 = (bf16[256,1280]{1,0:T(8,128)(2,1)S(1)}, bf16[256,1280]{1,0:T(8,128)(2,1)S(1)}, u32[]{:S(2)}, u32[]{:S(2)}) collective-permute-start(bf16[256,1280]{1,0:T(8,128)(2,1)S(1)} %collective-permute-done.2), channel_id=1, source_target_pairs={{0,4},{4,0},{8,12},{12,8},{16,20},{20,16},{24,28},{28,24},{1,5},{5... | collective-permute-start | bytes 1966088 | tf_op jit(solution)/shard_map/ppermute | solution.py:123
  196.5 27.8 %collective-permute-start.9 = (bf16[1,160,960]{2,1,0:T(8,128)(2,1)S(1)}, bf16[1,160,960]{2,1,0:T(8,128)(2,1)S(1)}, u32[]{:S(2)}, u32[]{:S(2)}) collective-permute-start(bf16[1,160,960]{2,1,0:T(8,128)(2,1)S(1)} %slice.1018), channel_id=1, source_target_pairs={{0,8},{4,12},{8,0},{12,4},{16,24},{20,28},{24,16},{28,20},{1,9},{5... | collective-permute-start | bytes 921608 | tf_op jit(solution)/shard_map/ppermute | solution.py:123
  205.7 54.5 %collective-permute-start.30 = (bf16[2,160,1280]{2,1,0:T(8,128)(2,1)}, bf16[2,160,1280]{2,1,0:T(8,128)(2,1)}, u32[]{:S(2)}, u32[]{:S(2)}) collective-permute-start(bf16[2,160,1280]{2,1,0:T(8,128)(2,1)} %pad_maximum_fusion.14), channel_id=1, source_target_pairs={{0,0},{1,1},{2,4},{3,5},{4,2},{5,3},{6,6},{7,7},{8,8},{9,9},{10,12... | collective-permute-start | bytes 2457608 | tf_op jit(solution)/shard_map/ppermute | solution.py:137
  260.2 34.2 %collective-permute-start.32 = (bf16[2,160,1280]{2,1,0:T(8,128)(2,1)}, bf16[2,160,1280]{2,1,0:T(8,128)(2,1)S(1)}, u32[]{:S(2)}, u32[]{:S(2)}) collective-permute-start(bf16[2,160,1280]{2,1,0:T(8,128)(2,1)} %collective-permute-done.30), channel_id=1, source_target_pairs={{0,16},{4,20},{8,24},{12,28},{16,0},{20,4},{24,8},{28,12},{1,17},{... | collective-permute-start | bytes 2457608 | tf_op jit(solution)/shard_map/ppermute | solution.py:123
  260.6 36.8 %collective-permute-start.31 = (bf16[2,160,1280]{2,1,0:T(8,128)(2,1)}, bf16[2,160,1280]{2,1,0:T(8,128)(2,1)S(1)}, u32[]{:S(2)}, u32[]{:S(2)}) collective-permute-start(bf16[2,160,1280]{2,1,0:T(8,128)(2,1)} %collective-permute-done.30), channel_id=1, source_target_pairs={{0,8},{4,12},{8,0},{12,4},{16,24},{20,28},{24,16},{28,20},{1,9},{5... | collective-permute-start | bytes 2457608 | tf_op jit(solution)/shard_map/ppermute | solution.py:123
  263.8 35.5 %collective-permute-start.17 = (bf16[256,1280]{1,0:T(8,128)(2,1)S(1)}, bf16[256,1280]{1,0:T(8,128)(2,1)S(1)}, u32[]{:S(2)}, u32[]{:S(2)}) collective-permute-start(bf16[256,1280]{1,0:T(8,128)(2,1)S(1)} %convolution_convert_fusion.15), channel_id=1, source_target_pairs={{0,4},{4,0},{8,12},{12,8},{16,20},{20,16},{24,28},{28,24},{1,5},{5... | collective-permute-start | bytes 1966088 | tf_op jit(solution)/shard_map/ppermute | solution.py:123
  280.6 35.7 %collective-permute-start.28 = (bf16[1,160,1280]{2,1,0:T(8,128)(2,1)S(1)}, bf16[1,160,1280]{2,1,0:T(8,128)(2,1)S(1)}, u32[]{:S(2)}, u32[]{:S(2)}) collective-permute-start(bf16[1,160,1280]{2,1,0:T(8,128)(2,1)S(1)} %slice.1037), channel_id=1, source_target_pairs={{0,8},{4,12},{8,0},{12,4},{16,24},{20,28},{24,16},{28,20},{1,9},{5... | collective-permute-start | bytes 1228808 | tf_op jit(solution)/shard_map/ppermute | solution.py:123
  357.3 28.6 %collective-permute-start.39 = (bf16[256,1280]{1,0:T(8,128)(2,1)S(1)}, bf16[256,1280]{1,0:T(8,128)(2,1)S(1)}, u32[]{:S(2)}, u32[]{:S(2)}) collective-permute-start(bf16[256,1280]{1,0:T(8,128)(2,1)S(1)} %add_convert_fusion.4), channel_id=1, source_target_pairs={{0,1},{1,0},{2,3},{3,2},{4,5},{5,4},{6,7},{7,6},{8,9},{9,8},{10,11... | collective-permute-start | bytes 1966088 | tf_op jit(solution)/shard_map/ppermute | solution.py:129
  359.0 27.9 %collective-permute-start.44 = (bf16[2,160,960]{2,1,0:T(8,128)(2,1)S(1)}, bf16[2,160,960]{2,1,0:T(8,128)(2,1)S(1)}, u32[]{:S(2)}, u32[]{:S(2)}) collective-permute-start(bf16[2,160,960]{2,1,0:T(8,128)(2,1)S(1)} %collective-permute-done.42), channel_id=1, source_target_pairs={{0,16},{4,20},{8,24},{12,28},{16,0},{20,4},{24,8},{28,12},{1,17},{... | collective-permute-start | bytes 1843208 | tf_op jit(solution)/shard_map/ppermute | solution.py:123
  362.0 40.6 %collective-permute-start.60 = (bf16[2,160,1280]{2,1,0:T(8,128)(2,1)S(1)}, bf16[2,160,1280]{2,1,0:T(8,128)(2,1)}, u32[]{:S(2)}, u32[]{:S(2)}) collective-permute-start(bf16[2,160,1280]{2,1,0:T(8,128)(2,1)S(1)} %pad_maximum_fusion.15), channel_id=1, source_target_pairs={{0,0},{1,1},{2,4},{3,5},{4,2},{5,3},{6,6},{7,7},{8,8},{9,9},{10,12... | collective-permute-start | bytes 2457608 | tf_op jit(solution)/shard_map/ppermute | solution.py:137
  377.1 34.3 %collective-permute-start.38 = (bf16[256,1280]{1,0:T(8,128)(2,1)S(1)}, bf16[256,1280]{1,0:T(8,128)(2,1)S(1)}, u32[]{:S(2)}, u32[]{:S(2)}) collective-permute-start(bf16[256,1280]{1,0:T(8,128)(2,1)S(1)} %add_convert_fusion.4), channel_id=1, source_target_pairs={{0,4},{4,0},{8,12},{12,8},{16,20},{20,16},{24,28},{28,24},{1,5},{5... | collective-permute-start | bytes 1966088 | tf_op jit(solution)/shard_map/ppermute | solution.py:123
  396.1 46.6 %collective-permute-start.75 = (bf16[256,1280]{1,0:T(8,128)(2,1)}, bf16[256,1280]{1,0:T(8,128)(2,1)}, u32[]{:S(2)}, u32[]{:S(2)}) collective-permute-start(bf16[256,1280]{1,0:T(8,128)(2,1)} %convert_element_type.778), channel_id=1, source_target_pairs={{0,0},{1,1},{2,4},{3,5},{4,2},{5,3},{6,6},{7,7},{8,8},{9,9},{10,12... | collective-permute-start | bytes 1966088 | tf_op jit(solution)/shard_map/ppermute | solution.py:137
  402.7 45.8 %collective-permute-start.66 = (bf16[2,160,1280]{2,1,0:T(8,128)(2,1)}, bf16[2,160,1280]{2,1,0:T(8,128)(2,1)}, u32[]{:S(2)}, u32[]{:S(2)}) collective-permute-start(bf16[2,160,1280]{2,1,0:T(8,128)(2,1)} %pad_maximum_fusion.16), channel_id=1, source_target_pairs={{0,0},{1,1},{2,4},{3,5},{4,2},{5,3},{6,6},{7,7},{8,8},{9,9},{10,12... | collective-permute-start | bytes 2457608 | tf_op jit(solution)/shard_map/ppermute | solution.py:137
  410.6 42.0 %collective-permute-start.62 = (bf16[2,160,1280]{2,1,0:T(8,128)(2,1)}, bf16[2,160,1280]{2,1,0:T(8,128)(2,1)}, u32[]{:S(2)}, u32[]{:S(2)}) collective-permute-start(bf16[2,160,1280]{2,1,0:T(8,128)(2,1)} %collective-permute-done.60), channel_id=1, source_target_pairs={{0,16},{4,20},{8,24},{12,28},{16,0},{20,4},{24,8},{28,12},{1,17},{... | collective-permute-start | bytes 2457608 | tf_op jit(solution)/shard_map/ppermute | solution.py:123
  449.6 36.1 %collective-permute-start.67 = (bf16[2,160,1280]{2,1,0:T(8,128)(2,1)}, bf16[2,160,1280]{2,1,0:T(8,128)(2,1)S(1)}, u32[]{:S(2)}, u32[]{:S(2)}) collective-permute-start(bf16[2,160,1280]{2,1,0:T(8,128)(2,1)} %collective-permute-done.66), channel_id=1, source_target_pairs={{0,8},{4,12},{8,0},{12,4},{16,24},{20,28},{24,16},{28,20},{1,9},{5... | collective-permute-start | bytes 2457608 | tf_op jit(solution)/shard_map/ppermute | solution.py:123
  452.0 35.4 %collective-permute-start.53 = (bf16[256,1280]{1,0:T(8,128)(2,1)S(1)}, bf16[256,1280]{1,0:T(8,128)(2,1)S(1)}, u32[]{:S(2)}, u32[]{:S(2)}) collective-permute-start(bf16[256,1280]{1,0:T(8,128)(2,1)S(1)} %convolution_convert_fusion.13), channel_id=1, source_target_pairs={{0,4},{4,0},{8,12},{12,8},{16,20},{20,16},{24,28},{28,24},{1,5},{5... | collective-permute-start | bytes 1966088 | tf_op jit(solution)/shard_map/ppermute | solution.py:123
  452.6 36.1 %collective-permute-start.55 = (bf16[256,1280]{1,0:T(8,128)(2,1)S(1)}, bf16[256,1280]{1,0:T(8,128)(2,1)S(1)}, u32[]{:S(2)}, u32[]{:S(2)}) collective-permute-start(bf16[256,1280]{1,0:T(8,128)(2,1)S(1)} %fusion.42), channel_id=1, source_target_pairs={{0,1},{1,0},{2,3},{3,2},{4,5},{5,4},{6,7},{7,6},{8,9},{9,8},{10,11... | collective-permute-start | bytes 1966088 | tf_op jit(solution)/shard_map/ppermute | solution.py:129
  468.1 37.4 %collective-permute-start.77 = (bf16[256,1280]{1,0:T(8,128)(2,1)S(1)}, bf16[256,1280]{1,0:T(8,128)(2,1)S(1)}, u32[]{:S(2)}, u32[]{:S(2)}) collective-permute-start(bf16[256,1280]{1,0:T(8,128)(2,1)S(1)} %get-tuple-element.135), channel_id=1, source_target_pairs={{0,1},{1,0},{2,3},{3,2},{4,5},{5,4},{6,7},{7,6},{8,9},{9,8},{10,11... | collective-permute-start | bytes 1966088 | tf_op jit(solution)/shard_map/ppermute | solution.py:129
  469.2 38.1 %collective-permute-start.64 = (bf16[1,160,1280]{2,1,0:T(8,128)(2,1)S(1)}, bf16[1,160,1280]{2,1,0:T(8,128)(2,1)S(1)}, u32[]{:S(2)}, u32[]{:S(2)}) collective-permute-start(bf16[1,160,1280]{2,1,0:T(8,128)(2,1)S(1)} %slice.1067), channel_id=1, source_target_pairs={{0,8},{4,12},{8,0},{12,4},{16,24},{20,28},{24,16},{28,20},{1,9},{5... | collective-permute-start | bytes 1228808 | tf_op jit(solution)/shard_map/ppermute | solution.py:123
  538.9 37.2 %collective-permute-start.71 = (bf16[256,1280]{1,0:T(8,128)(2,1)S(1)}, bf16[256,1280]{1,0:T(8,128)(2,1)}, u32[]{:S(2)}, u32[]{:S(2)}) collective-permute-start(bf16[256,1280]{1,0:T(8,128)(2,1)S(1)} %convolution_convert_fusion.21), channel_id=1, source_target_pairs={{0,4},{4,0},{8,12},{12,8},{16,20},{20,16},{24,28},{28,24},{1,5},{5... | collective-permute-start | bytes 1966088 | tf_op jit(solution)/shard_map/ppermute | solution.py:123
  558.5 32.5 %collective-permute-start.79 = (bf16[256,1280]{1,0:T(8,128)(2,1)}, bf16[256,1280]{1,0:T(8,128)(2,1)}, u32[]{:S(2)}, u32[]{:S(2)}) collective-permute-start(bf16[256,1280]{1,0:T(8,128)(2,1)} %convolution_convert_fusion.19), channel_id=1, source_target_pairs={{0,4},{4,0},{8,12},{12,8},{16,20},{20,16},{24,28},{28,24},{1,5},{5... | collective-permute-start | bytes 1966088 | tf_op jit(solution)/shard_map/ppermute | solution.py:123
  573.2 31.9 %collective-permute-start.139 = (bf16[2,160,1280]{2,1,0:T(8,128)(2,1)}, bf16[2,160,1280]{2,1,0:T(8,128)(2,1)}, u32[]{:S(2)}, u32[]{:S(2)}) collective-permute-start(bf16[2,160,1280]{2,1,0:T(8,128)(2,1)} %pad_maximum_fusion.20), channel_id=1, source_target_pairs={{0,16},{4,20},{8,24},{12,28},{16,0},{20,4},{24,8},{28,12},{1,17},{... | collective-permute-start | bytes 2457608 | tf_op jit(solution)/shard_map/ppermute | solution.py:123
  576.1 28.9 %collective-permute-start.137 = (bf16[2,160,1280]{2,1,0:T(8,128)(2,1)}, bf16[2,160,1280]{2,1,0:T(8,128)(2,1)}, u32[]{:S(2)}, u32[]{:S(2)}) collective-permute-start(bf16[2,160,1280]{2,1,0:T(8,128)(2,1)} %pad_maximum_fusion.19), channel_id=1, source_target_pairs={{0,8},{4,12},{8,0},{12,4},{16,24},{20,28},{24,16},{28,20},{1,9},{5... | collective-permute-start | bytes 2457608 | tf_op jit(solution)/shard_map/ppermute | solution.py:123
  577.4 58.6 %collective-permute-start.152 = (bf16[2,160,1280]{2,1,0:T(8,128)(2,1)}, bf16[2,160,1280]{2,1,0:T(8,128)(2,1)}, u32[]{:S(2)}, u32[]{:S(2)}) collective-permute-start(bf16[2,160,1280]{2,1,0:T(8,128)(2,1)} %fusion.53), channel_id=1, source_target_pairs={{0,0},{1,1},{2,4},{3,5},{4,2},{5,3},{6,6},{7,7},{8,8},{9,9},{10,12... | collective-permute-start | bytes 2457608 | tf_op jit(solution)/shard_map/ppermute | solution.py:137
  605.0 30.9 %collective-permute-start.83 = (bf16[256,1280]{1,0:T(8,128)(2,1)S(1)}, bf16[256,1280]{1,0:T(8,128)(2,1)S(1)}, u32[]{:S(2)}, u32[]{:S(2)}) collective-permute-start(bf16[256,1280]{1,0:T(8,128)(2,1)S(1)} %get-tuple-element.140), channel_id=1, source_target_pairs={{0,1},{1,0},{2,3},{3,2},{4,5},{5,4},{6,7},{7,6},{8,9},{9,8},{10,11... | collective-permute-start | bytes 1966088 | tf_op jit(solution)/shard_map/ppermute | solution.py:129
  607.0 31.3 %collective-permute-start.140 = (bf16[2,160,1280]{2,1,0:T(8,128)(2,1)S(1)}, bf16[2,160,1280]{2,1,0:T(8,128)(2,1)S(1)}, u32[]{:S(2)}, u32[]{:S(2)}) collective-permute-start(bf16[2,160,1280]{2,1,0:T(8,128)(2,1)S(1)} %fusion.57), channel_id=1, source_target_pairs={{0,0},{1,1},{2,4},{3,5},{4,2},{5,3},{6,6},{7,7},{8,8},{9,9},{10,12... | collective-permute-start | bytes 2457608 | tf_op jit(solution)/shard_map/ppermute | solution.py:137
  607.9 32.0 %collective-permute-start.82 = (bf16[256,1280]{1,0:T(8,128)(2,1)S(1)}, bf16[256,1280]{1,0:T(8,128)(2,1)S(1)}, u32[]{:S(2)}, u32[]{:S(2)}) collective-permute-start(bf16[256,1280]{1,0:T(8,128)(2,1)S(1)} %get-tuple-element.140), channel_id=1, source_target_pairs={{0,4},{4,0},{8,12},{12,8},{16,20},{20,16},{24,28},{28,24},{1,5},{5... | collective-permute-start | bytes 1966088 | tf_op jit(solution)/shard_map/ppermute | solution.py:123
  638.0 94.2 %collective-permute-start.153 = (bf16[160,1280]{1,0:T(8,128)(2,1)}, bf16[160,1280]{1,0:T(8,128)(2,1)}, u32[]{:S(2)}, u32[]{:S(2)}) collective-permute-start(bf16[160,1280]{1,0:T(8,128)(2,1)} %slice_bitcast_fusion.4), channel_id=1, source_target_pairs={{0,4},{4,0},{8,12},{12,8},{16,20},{20,16},{24,28},{28,24},{1,5},{5... | collective-permute-start | bytes 1228808 | tf_op jit(solution)/shard_map/ppermute | solution.py:123
  709.2 38.8 %collective-permute-start.141 = (bf16[160,1280]{1,0:T(8,128)(2,1)S(1)}, bf16[160,1280]{1,0:T(8,128)(2,1)S(1)}, u32[]{:S(2)}, u32[]{:S(2)}) collective-permute-start(bf16[160,1280]{1,0:T(8,128)(2,1)S(1)} %copy-done.81), channel_id=1, source_target_pairs={{0,4},{4,0},{8,12},{12,8},{16,20},{20,16},{24,28},{28,24},{1,5},{5... | collective-permute-start | bytes 1228808 | tf_op jit(solution)/shard_map/ppermute | solution.py:123
  752.5 97.4 %collective-permute-start.117 = (bf16[160,960]{1,0:T(8,128)(2,1)S(1)}, bf16[160,960]{1,0:T(8,128)(2,1)S(1)}, u32[]{:S(2)}, u32[]{:S(2)}) collective-permute-start(bf16[160,960]{1,0:T(8,128)(2,1)S(1)} %slice_bitcast_fusion.42), channel_id=1, source_target_pairs={{0,4},{4,0},{8,12},{12,8},{16,20},{20,16},{24,28},{28,24},{1,5},{5... | collective-permute-start | bytes 921608 | tf_op jit(solution)/shard_map/ppermute | solution.py:123
  780.3 50.8 %collective-permute-start.91 = (bf16[256,1280]{1,0:T(8,128)(2,1)S(1)}, bf16[256,1280]{1,0:T(8,128)(2,1)S(1)}, u32[]{:S(2)}, u32[]{:S(2)}) collective-permute-start(bf16[256,1280]{1,0:T(8,128)(2,1)S(1)} %convolution_convert_fusion.17), channel_id=1, source_target_pairs={{0,4},{4,0},{8,12},{12,8},{16,20},{20,16},{24,28},{28,24},{1,5},{5... | collective-permute-start | bytes 1966088 | tf_op jit(solution)/shard_map/ppermute | solution.py:123
  780.4 31.4 %collective-permute-start.92 = (bf16[256,1280]{1,0:T(8,128)(2,1)S(1)}, bf16[256,1280]{1,0:T(8,128)(2,1)S(1)}, u32[]{:S(2)}, u32[]{:S(2)}) collective-permute-start(bf16[256,1280]{1,0:T(8,128)(2,1)S(1)} %convolution_convert_fusion.16), channel_id=1, source_target_pairs={{0,4},{4,0},{8,12},{12,8},{16,20},{20,16},{24,28},{28,24},{1,5},{5... | collective-permute-start | bytes 1966088 | tf_op jit(solution)/shard_map/ppermute | solution.py:123
  831.1 39.2 %collective-permute-start.134 = (bf16[2,160,1280]{2,1,0:T(8,128)(2,1)}, bf16[2,160,1280]{2,1,0:T(8,128)(2,1)}, u32[]{:S(2)}, u32[]{:S(2)}) collective-permute-start(bf16[2,160,1280]{2,1,0:T(8,128)(2,1)} %fusion.59), channel_id=1, source_target_pairs={{0,0},{1,1},{2,4},{3,5},{4,2},{5,3},{6,6},{7,7},{8,8},{9,9},{10,12... | collective-permute-start | bytes 2457608 | tf_op jit(solution)/shard_map/ppermute | solution.py:137
  842.7 27.6 %collective-permute-start.95 = (bf16[256,1280]{1,0:T(8,128)(2,1)S(1)}, bf16[256,1280]{1,0:T(8,128)(2,1)}, u32[]{:S(2)}, u32[]{:S(2)}) collective-permute-start(bf16[256,1280]{1,0:T(8,128)(2,1)S(1)} %get-tuple-element.143), channel_id=1, source_target_pairs={{0,1},{1,0},{2,3},{3,2},{4,5},{5,4},{6,7},{7,6},{8,9},{9,8},{10,11... | collective-permute-start | bytes 1966088 | tf_op jit(solution)/shard_map/ppermute | solution.py:129
  955.4 31.5 %collective-permute-start.109 = (bf16[2,160,960]{2,1,0:T(8,128)(2,1)}, bf16[2,160,960]{2,1,0:T(8,128)(2,1)}, u32[]{:S(2)}, u32[]{:S(2)}) collective-permute-start(bf16[2,160,960]{2,1,0:T(8,128)(2,1)} %pad_maximum_fusion.28), channel_id=1, source_target_pairs={{0,16},{4,20},{8,24},{12,28},{16,0},{20,4},{24,8},{28,12},{1,17},{... | collective-permute-start | bytes 1843208 | tf_op jit(solution)/shard_map/ppermute | solution.py:123
  959.7 27.1 %collective-permute-start.107 = (bf16[2,160,960]{2,1,0:T(8,128)(2,1)}, bf16[2,160,960]{2,1,0:T(8,128)(2,1)}, u32[]{:S(2)}, u32[]{:S(2)}) collective-permute-start(bf16[2,160,960]{2,1,0:T(8,128)(2,1)} %pad_maximum_fusion.27), channel_id=1, source_target_pairs={{0,8},{4,12},{8,0},{12,4},{16,24},{20,28},{24,16},{28,20},{1,9},{5... | collective-permute-start | bytes 1843208 | tf_op jit(solution)/shard_map/ppermute | solution.py:123
  (297 other events, 4346.0 us)
Sparse Core Ops, SparseCore 0:
  16.7 131.6 all-reduce.2

commit v2 on v1

--- a/solution.py
+++ b/solution.py
@@ -1,6 +1,8 @@
 import jax
 import jax.numpy as jnp
 from jax import lax
+from jax.experimental import pallas as pl
+from jax.experimental.pallas import tpu as pltpu
 from jax.sharding import PartitionSpec as P
 
 D = 1280
@@ -42,76 +44,199 @@
     quarter = HD // 4
     powers = jnp.arange(quarter, dtype=F32) * (4.0 / HD)
     inverse = 10000.0 ** (-powers)
-    height_angle = coords[0].astype(F32)[:, None] * inverse[None, :]
-    width_angle = coords[1].astype(F32)[:, None] * inverse[None, :]
-    angles = jnp.concatenate([height_angle, width_angle], axis=1)
-    angles = jnp.concatenate([angles, angles], axis=1)
-    return (jnp.cos(angles)[:, None, :], jnp.sin(angles)[:, None, :])
-
-
-def rotate(values, cosine, sine):
-    half_size = HD // 2
-    turned = jnp.concatenate([-values[..., half_size:], values[..., :half_size]], axis=-1)
-    return values * cosine + turned * sine
-
-
-def rotate_back(values, cosine, sine):
-    half_size = HD // 2
-    turned = jnp.concatenate([-values[..., half_size:], values[..., :half_size]], axis=-1)
-    return values * cosine - turned * sine
-
-
-def masked_scores(queries, key_rows, codes):
-    scores = jnp.einsum("qhe,khe->hqk", queries, key_rows, preferred_element_type=F32)
-    scores = scores * HD ** (-0.5)
-    return jnp.where((codes[:, None] == codes[None, :])[None], scores, -1e30)
-
-
-def attend_forward(linear, cosine, sine, codes):
-    length = linear.shape[0]
-    parts = linear.reshape(length, 3, -1, HD)
-    queries = rotate(parts[:, 0], cosine, sine).astype(BF16)
-    key_rows = rotate(parts[:, 1], cosine, sine).astype(BF16)
-    value_rows = parts[:, 2].astype(BF16)
-    scores = masked_scores(queries, key_rows, codes)
-    row_max = jnp.max(scores, axis=-1, keepdims=True)
-    exponent = jnp.exp(scores - row_max)
-    totals = jnp.sum(exponent, axis=-1, keepdims=True)
-    chances = (exponent / totals).astype(BF16)
-    mixed = jnp.einsum("hqk,khe->qhe", chances, value_rows, preferred_element_type=F32)
-    return mixed.astype(BF16).reshape(length, -1), (
-        queries,
-        key_rows,
-        value_rows,
-        row_max + jnp.log(totals),
-    )
-
-
-def attend_backward(saved, mixed, grad_mixed, cosine, sine, codes):
-    queries, key_rows, value_rows, log_totals = saved
-    length = queries.shape[0]
-    scale = HD ** (-0.5)
-    grad_mixed = grad_mixed.reshape(value_rows.shape)
-    scores = masked_scores(queries, key_rows, codes)
-    chances = jnp.exp(scores - log_totals)
-    grad_chance = jnp.einsum("qhe,khe->hqk", grad_mixed, value_rows, preferred_element_type=F32)
-    centre = jnp.sum(chances * grad_chance, axis=-1, keepdims=True)
-    grad_scores = (chances * (grad_chance - centre)).astype(BF16)
-    grad_query = scale * jnp.einsum(
-        "hqk,khe->qhe", grad_scores, key_rows, preferred_element_type=F32
-    )
-    grad_key = scale * jnp.einsum("hqk,qhe->khe", grad_scores, queries, preferred_element_type=F32)
-    grad_value = jnp.einsum(
-        "hqk,qhe->khe", chances.astype(BF16), grad_mixed, preferred_element_type=F32
-    )
-    return jnp.concatenate(
-        [
-            rotate_back(grad_query, cosine, sine).reshape(length, -1),
-            rotate_back(grad_key, cosine, sine).reshape(length, -1),
-            grad_value.reshape(length, -1),
+    height_angle = inverse[:, None] * coords[0].astype(F32)[None, :]
+    width_angle = inverse[:, None] * coords[1].astype(F32)[None, :]
+    angles = jnp.concatenate([height_angle, width_angle], axis=0)
+    return (jnp.cos(angles), jnp.sin(angles))
+
+
+TILE = 256
+MASKED = -1e30
+LOG2E = 1.4426950408889634
+SCORE_SCALE = HD**-0.5 * LOG2E
+
+
+def mat(left, right):
+    return lax.dot_general(left, right, (((1,), (0,)), ((), ())), preferred_element_type=F32)
+
+
+def mat_turned(left, right):
+    return lax.dot_general(left, right, (((1,), (1,)), ((), ())), preferred_element_type=F32)
+
+
+def tile_bias(code_col, code_row, keys, queries):
+    same = code_col[keys, :] == code_row[:, queries]
+    return jnp.where(same, 0.0, MASKED)
+
+
+def tiles(at):
+    return pl.ds(pl.multiple_of(at * TILE, TILE), TILE)
+
+
+def forward_kernel(active, lin, cosine, sine, code_row, code_col, qkv, mixed, log_sum, k_rows, top, total, acc):
+    heads, length = k_rows.shape[0], k_rows.shape[1]
+    blocks = length // TILE
+    cos, sin = cosine[...], sine[...]
+    half = HD // 2
+    for head in range(heads):
+        for which in range(2):
+            base = (which * heads + head) * HD
+            low, high = lin[base : base + half, :], lin[base + half : base + HD, :]
+            turned = jnp.concatenate([low * cos - high * sin, high * cos + low * sin], axis=0)
+            qkv[base : base + HD, :] = turned.astype(BF16)
+            if which == 1:
+                k_rows[head] = turned.T.astype(BF16)
+        base = (2 * heads + head) * HD
+        qkv[base : base + HD, :] = lin[base : base + HD, :].astype(BF16)
+
+    def query_block(q_at, carry):
+        queries = tiles(q_at)
+        top[...] = jnp.full(top.shape, MASKED, F32)
+        total[...] = jnp.zeros(total.shape, F32)
+        acc[...] = jnp.zeros(acc.shape, F32)
+
+        def key_block(k_at, carry):
+            @pl.when(active[q_at * blocks + k_at] != 0)
+            def _():
+                keys = tiles(k_at)
+                bias = tile_bias(code_col, code_row, keys, queries)
+                for head in range(heads):
+                    q_base, v_base = head * HD, (2 * heads + head) * HD
+                    scores = mat(k_rows[head, keys, :], qkv[q_base : q_base + HD, queries]) + bias
+                    old = top[head]
+                    new = jnp.maximum(old, jnp.max(scores, axis=0, keepdims=True))
+                    chance = jnp.exp2((scores - new) * SCORE_SCALE)
+                    fade = jnp.exp2((old - new) * SCORE_SCALE)
+                    top[head] = new
+                    total[head] = total[head] * fade + jnp.sum(chance, axis=0, keepdims=True)
+                    acc[head] = acc[head] * fade + mat(
+                        qkv[v_base : v_base + HD, keys], chance.astype(BF16)
+                    )
+
+            return carry
+
+        lax.fori_loop(0, blocks, key_block, 0)
+        for head in range(heads):
+            mixed[head * HD : (head + 1) * HD, queries] = (acc[head] / total[head]).astype(BF16)
+            log_sum[head, :, queries] = top[head] * SCORE_SCALE + jnp.log2(total[head])
+        return carry
+
+    lax.fori_loop(0, blocks, query_block, 0)
+
+
+def backward_kernel(active, qkv, mixed, grad_mixed, log_sum, cosine, sine, code_row, code_col, out, k_rows, v_rows, centre, grad_q, grad_k, grad_v):
+    heads, length = k_rows.shape[0], k_rows.shape[1]
+    blocks = length // TILE
+    for head in range(heads):
+        k_base, v_base = (heads + head) * HD, (2 * heads + head) * HD
+        k_rows[head] = qkv[k_base : k_base + HD, :].astype(F32).T.astype(BF16)
+        v_rows[head] = qkv[v_base : v_base + HD, :].astype(F32).T.astype(BF16)
+        rows = slice(head * HD, (head + 1) * HD)
+        centre[head] = jnp.sum(
+            grad_mixed[rows, :].astype(F32) * mixed[rows, :].astype(F32), axis=0, keepdims=True
+        )
+    grad_q[...] = jnp.zeros(grad_q.shape, F32)
+    grad_k[...] = jnp.zeros(grad_k.shape, F32)
+    grad_v[...] = jnp.zeros(grad_v.shape, F32)
+
+    def query_block(q_at, carry):
+        queries = tiles(q_at)
+
+        def key_block(k_at, carry):
+            @pl.when(active[q_at * blocks + k_at] != 0)
+            def _():
+                keys = tiles(k_at)
+                bias = tile_bias(code_col, code_row, keys, queries)
+                for head in range(heads):
+                    rows = slice(head * HD, (head + 1) * HD)
+                    k_base = (heads + head) * HD
+                    scores = mat(k_rows[head, keys, :], qkv[rows, queries]) + bias
+                    chance = jnp.exp2(scores * SCORE_SCALE - log_sum[head, :, queries])
+                    grad_chance = mat(v_rows[head, keys, :], grad_mixed[rows, queries])
+                    grad_score = (chance * (grad_chance - centre[head, :, queries])).astype(BF16)
+                    grad_v[head, :, keys] += mat_turned(grad_mixed[rows, queries], chance.astype(BF16))
+                    grad_k[head, :, keys] += mat_turned(qkv[rows, queries], grad_score)
+                    grad_q[head, :, queries] += mat(qkv[k_base : k_base + HD, keys], grad_score)
+
+            return carry
+
+        return lax.fori_loop(0, blocks, key_block, carry)
+
+    lax.fori_loop(0, blocks, query_block, 0)
+    half = HD // 2
+    scale = HD**-0.5
+    cos, sin = cosine[...] * scale, sine[...] * scale
+    for head in range(heads):
+        for which, grad in ((0, grad_q), (1, grad_k)):
+            base = (which * heads + head) * HD
+            low, high = grad[head, :half, :], grad[head, half:, :]
+            turned = jnp.concatenate([low * cos + high * sin, high * cos - low * sin], axis=0)
+            out[base : base + HD, :] = turned.astype(BF16)
+        base = (2 * heads + head) * HD
+        out[base : base + HD, :] = grad_v[head].astype(BF16)
+
+
+def whole(count):
+    return [pl.BlockSpec(memory_space=pltpu.VMEM)] * count
+
+
+def attend_forward(linear, facts):
+    active, cosine, sine, code_row, code_col = facts
+    width, length = linear.shape
+    heads = width // (3 * HD)
+    return pl.pallas_call(
+        forward_kernel,
+        name="attend_forward",
+        out_shape=(
+            jax.ShapeDtypeStruct((width, length), BF16),
+            jax.ShapeDtypeStruct((heads * HD, length), BF16),
+            jax.ShapeDtypeStruct((heads, 1, length), F32),
+        ),
+        in_specs=[pl.BlockSpec(memory_space=pltpu.SMEM)] + whole(5),
+        out_specs=tuple(whole(3)),
+        scratch_shapes=[
+            pltpu.VMEM((heads, length, HD), BF16),
+            pltpu.VMEM((heads, 1, TILE), F32),
+            pltpu.VMEM((heads, 1, TILE), F32),
+            pltpu.VMEM((heads, HD, TILE), F32),
         ],
-        axis=1,
-    ).astype(BF16)
+        compiler_params=pltpu.CompilerParams(vmem_limit_bytes=40 << 20),
+        cost_estimate=pl.CostEstimate(
+            flops=heads * length * length * HD * 4, bytes_accessed=10 << 20, transcendentals=heads * length * length
+        ),
+    )(active, linear, cosine, sine, code_row, code_col)
+
+
+def attend_backward(qkv, mixed, grad_mixed, log_sum, facts):
+    active, cosine, sine, code_row, code_col = facts
+    width, length = qkv.shape
+    heads = width // (3 * HD)
+    return pl.pallas_call(
+        backward_kernel,
+        name="attend_backward",
+        out_shape=jax.ShapeDtypeStruct((width, length), BF16),
+        in_specs=[pl.BlockSpec(memory_space=pltpu.SMEM)] + whole(8),
+        out_specs=pl.BlockSpec(memory_space=pltpu.VMEM),
+        scratch_shapes=[
+            pltpu.VMEM((heads, length, HD), BF16),
+            pltpu.VMEM((heads, length, HD), BF16),
+            pltpu.VMEM((heads, 1, length), F32),
+            pltpu.VMEM((heads, HD, length), F32),
+            pltpu.VMEM((heads, HD, length), F32),
+            pltpu.VMEM((heads, HD, length), F32),
+        ],
+        compiler_params=pltpu.CompilerParams(vmem_limit_bytes=40 << 20),
+        cost_estimate=pl.CostEstimate(
+            flops=heads * length * length * HD * 10, bytes_accessed=10 << 20, transcendentals=heads * length * length
+        ),
+    )(active, qkv, mixed, grad_mixed, log_sum, cosine, sine, code_row, code_col)
+
+
+def tile_overlap(codes):
+    blocks = codes.reshape(-1, TILE)
+    least, most = jnp.min(blocks, axis=1), jnp.max(blocks, axis=1)
+    meet = (least[:, None] <= most[None, :]) & (least[None, :] <= most[:, None])
+    return meet.astype(jnp.int32).reshape(-1)
 
 
 def make_body(dp, mp):
@@ -136,7 +261,7 @@
     def swap(value):
         return lax.ppermute(value, ("dp", "mp"), swap_pairs)
 
-    def gather_weight(mine):
+    def gather_blocks(mine):
         pair = swap(jnp.stack([mine, core_side(mine)]))
         if len(high_bits) == 2:
             low, high = high_bits
@@ -146,10 +271,16 @@
             pieces = [pair]
             for bit in high_bits:
                 pieces = pieces + [across(piece, bit) for piece in pieces]
-        return jnp.concatenate(pieces, axis=0).reshape(D, mine.shape[-1])
-
-    def scatter_weight(grad):
-        blocks = grad.reshape(dp, D // dp, grad.shape[-1])
+        return [
+            jnp.concatenate([piece[:, g] for piece in pieces], axis=0).reshape(D, mine.shape[-1])
+            for g in range(mine.shape[0])
+        ]
+
+    def scatter_blocks(grads):
+        blocks = [grad.reshape(dp, D // dp, grad.shape[-1]) for grad in grads]
+
+        def pick(begin, end):
+            return jnp.stack([block[begin:end] for block in blocks], axis=1)
 
         def add(*terms):
             total = terms[0].astype(F32)
@@ -159,17 +290,33 @@
 
         if len(high_bits) == 2:
             low, high = high_bits
-            first = across(blocks[6:7], high)
-            second = across(blocks[7:8], low)
-            by_low = jnp.concatenate([add(blocks[2:3], first), blocks[3:4]], axis=0)
-            by_high = jnp.concatenate([blocks[4:5], add(blocks[5:6], second)], axis=0)
-            blocks = add(blocks[:2], across(by_low, low), across(by_high, high))
+            first = across(pick(6, 7), high)
+            second = across(pick(7, 8), low)
+            by_low = jnp.concatenate([add(pick(2, 3), first), pick(3, 4)], axis=0)
+            by_high = jnp.concatenate([pick(4, 5), add(pick(5, 6), second)], axis=0)
+            total = add(pick(0, 2), across(by_low, low), across(by_high, high))
         else:
+            total = pick(0, dp)
             for bit in high_bits[::-1]:
-                half = blocks.shape[0] // 2
-                blocks = add(blocks[:half], across(blocks[half:], bit))
-        blocks = swap(blocks)
-        return blocks[0].astype(F32) + core_side(blocks[1]).astype(F32)
+                half = total.shape[0] // 2
+                total = add(total[:half], across(total[half:], bit))
+        total = swap(total)
+        return total[0].astype(F32) + core_side(total[1]).astype(F32)
+
+    def gather_vectors(mine):
+        index = lax.axis_index("dp") * mp + lax.axis_index("mp")
+        values = mine[None]
+        bit = 1
+        while bit < count:
+            if bit >= mp:
+                got = across(values, bit // mp)
+            else:
+                got = lax.ppermute(values, "mp", [(i, i ^ bit) for i in range(mp)])
+            values = jnp.concatenate([values, got], axis=0)
+            bit *= 2
+        at = jnp.arange(count, dtype=jnp.int32)
+        order = (at[:, None] ^ index) == at[None, :]
+        return dot(order.astype(F32), values, 1, 0, precision=HIGHEST)
 
     def scatter_vectors(values):
         index = lax.axis_index("dp") * mp + lax.axis_index("mp")
@@ -235,22 +382,36 @@
             return dot(values.astype(BF16), reorder_low, 1, 0)
 
         hidden = turn_low(swap(hidden_in.astype(BF16)))
+        qkv_width, proj_width = 3 * columns, columns
+        qkv_space, proj_space = -(-qkv_width // 128) * 128, -(-proj_width // 128) * 128
+
+        def pack_attention(for_qkv, for_proj):
+            return jnp.concatenate(
+                [
+                    jnp.pad(for_qkv, ((0, 0), (0, qkv_space - qkv_width))),
+                    jnp.pad(for_proj, ((0, 0), (0, proj_space - proj_width))),
+                ],
+                axis=1,
+            )
+
+        def unpack_attention(packed):
+            return packed[:, :qkv_width], packed[:, qkv_space : qkv_space + proj_width]
+
         weights = []
         for layer in range(LAYERS):
-            weights.append(
-                (
-                    gather_weight(qkv_weight[layer].transpose(1, 0, 2).reshape(depth, 3 * columns)),
-                    gather_weight(proj_weight[layer].T),
-                    gather_weight(up_weight[layer]),
-                    gather_weight(down_weight[layer].T),
-                )
-            )
+            mine = pack_attention(
+                qkv_weight[layer].transpose(1, 0, 2).reshape(depth, qkv_width),
+                proj_weight[layer].T,
+            )
+            w_qkv, w_proj = unpack_attention(gather_blocks(mine[None])[0])
+            w_up, w_down = gather_blocks(jnp.stack([up_weight[layer], down_weight[layer].T]))
+            weights.append((w_qkv, w_proj, w_up, w_down))
 
         wide = (pre_gain, pre_bias, proj_bias, mid_gain, mid_bias, down_bias)
         packed = jnp.concatenate(
             [item.reshape(-1) for item in wide] + [qkv_bias.reshape(-1), up_bias.reshape(-1)]
         )
-        packed = lax.all_gather(packed, ("dp", "mp"), axis=0, tiled=False)
+        packed = gather_vectors(packed)
         each = D // count
         wide_count = len(wide) * LAYERS
         split = (wide_count + 3 * LAYERS) * each
@@ -281,7 +442,7 @@
             axis=1,
         )
         codes = row_facts[0]
-        cosine, sine = rotary_tables(row_facts[1:])
+        facts = (tile_overlap(codes), *rotary_tables(row_facts[1:]), codes[None], codes[:, None])
 
         kept = []
         for layer in range(LAYERS):
@@ -290,10 +451,10 @@
             normed = normalise(hidden)[0] * pre_gain_all[layer] + pre_bias_all[layer]
             rows = gather_rows(normed.astype(BF16))
             attn_rows = jnp.concatenate(rows, axis=0)
-            linear = dot(attn_rows, w_qkv, 1, 0) + qkv_bias_mine[layer]
-            mixed, saved = attend_forward(linear, cosine, sine, codes)
+            linear = dot(w_qkv, attn_rows, 0, 1) + qkv_bias_mine[layer][:, None]
+            qkv, mixed, log_sum = attend_forward(linear, facts)
             attended = scatter_rows(
-                lambda i, a=mixed, w=w_proj: dot(a[i * quarter : (i + 1) * quarter], w, 1, 1)
+                lambda i, a=mixed, w=w_proj: dot(a[:, i * quarter : (i + 1) * quarter], w, 0, 1)
             )
             middle = hidden + (attended + proj_bias_all[layer])
             normed = normalise(middle)[0] * mid_gain_all[layer] + mid_bias_all[layer]
@@ -307,7 +468,7 @@
                 lambda i, a=active, w=w_down: dot(a[i * quarter : (i + 1) * quarter], w, 1, 1)
             )
             hidden = middle + (output + down_bias_all[layer])
-            kept.append((start, attn_rows, mixed, saved, middle, mid_rows, active, slope))
+            kept.append((start, attn_rows, qkv, mixed, log_sum, middle, mid_rows, active, slope))
 
         out_hidden = swap(turn_low(hidden).astype(BF16)).astype(F32)
         gradient = turn_low(swap(cotangent.astype(BF16)))
@@ -315,7 +476,7 @@
         parts = []
         for layer in reversed(range(LAYERS)):
             w_qkv, w_proj, w_up, w_down = weights[layer]
-            start, attn_rows, mixed, saved, middle, mid_rows, active, slope = kept[layer]
+            start, attn_rows, qkv, mixed, log_sum, middle, mid_rows, active, slope = kept[layer]
             grad_out = gradient.astype(BF16)
             down_bias_part = jnp.sum(grad_out.astype(F32), axis=0)
             grad_rows = jnp.concatenate(gather_rows(grad_out), axis=0)
@@ -323,9 +484,10 @@
             grad_normed = scatter_rows(
                 lambda i, a=grad_up, w=w_up: dot(a[i * quarter : (i + 1) * quarter], w, 1, 1)
             )
-            down_grad = scatter_weight(dot(grad_rows, active, 0, 0, BF16))
+            down_grad = dot(grad_rows, active, 0, 0, BF16)
             up_bias_part = jnp.sum(grad_up.astype(F32), axis=0)
-            up_grad = scatter_weight(dot(mid_rows, grad_up, 0, 0, BF16))
+            up_grad = dot(mid_rows, grad_up, 0, 0, BF16)
+            ffn_grads = scatter_blocks([up_grad, down_grad])
             grad_middle, mid_gain_part, mid_bias_part = norm_backward(
                 middle, mid_gain_all[layer], grad_normed
             )
@@ -333,14 +495,18 @@
             grad_out = gradient.astype(BF16)
             proj_bias_part = jnp.sum(grad_out.astype(F32), axis=0)
             grad_rows = jnp.concatenate(gather_rows(grad_out), axis=0)
-            grad_mixed = dot(grad_rows, w_proj, 1, 0, BF16)
-            proj_grad = scatter_weight(dot(grad_rows, mixed, 0, 0, BF16))
-            grad_linear = attend_backward(saved, mixed, grad_mixed, cosine, sine, codes)
+            grad_mixed = dot(w_proj, grad_rows, 0, 1, BF16)
+            proj_grad = dot(grad_rows, mixed, 0, 1, BF16)
+            grad_linear = attend_backward(qkv, mixed, grad_mixed, log_sum, facts)
             grad_normed = scatter_rows(
-                lambda i, a=grad_linear, w=w_qkv: dot(a[i * quarter : (i + 1) * quarter], w, 1, 1)
-            )
-            qkv_bias_part = jnp.sum(grad_linear.astype(F32), axis=0)
-            qkv_grad = scatter_weight(dot(attn_rows, grad_linear, 0, 0, BF16))
+                lambda i, a=grad_linear, w=w_qkv: dot(
+                    a[:, i * quarter : (i + 1) * quarter], w, 0, 1
+                )
+            )
+            qkv_bias_part = jnp.sum(grad_linear.astype(F32), axis=1)
+            qkv_grad = dot(attn_rows, grad_linear, 0, 1, BF16)
+            attn_grads = scatter_blocks([pack_attention(qkv_grad, proj_grad)])[0]
+            qkv_grad, proj_grad = unpack_attention(attn_grads)
             grad_start, pre_gain_part, pre_bias_part = norm_backward(
                 start, pre_gain_all[layer], grad_normed
             )
@@ -349,8 +515,8 @@
                 (
                     qkv_grad.reshape(depth, 3, columns).transpose(1, 0, 2),
                     proj_grad.T,
-                    up_grad,
-                    down_grad.T,
+                    ffn_grads[0],
+                    ffn_grads[1].T,
                 )
             )
             parts.append(

time: 1050 us -> 821 us (0.78)
  waiting for transfers between devices: 415 us -> 301 us
  matrix products: 220 us -> 148 us
  Pallas kernels: 0 us -> 53.9 us
  other arithmetic: 90.7 us -> 56.2 us
  starting transfers between devices: 210 us -> 183 us
  between operations: 18.2 us -> 3.77 us
  local copies, waits for them, and re-layouts: 75.5 us -> 62.9 us
    unnamed x2 -> x0, waiting for transfers between devices: 108 us -> none
    dot_general x12 -> x0, matrix products: 75.9 us -> none  [the longest x2 20.5 us: attend_backward(): jnp.einsum('qhe,khe->hqk', grad_mixed, value_rows, preferred_element_type...]
    ppermute x115 -> x78, waiting for transfers between devices: 210 us -> 143 us  [across(): return lax.ppermute(value, 'dp', [(i, i ^ bit) for i in range(dp)])]
    pallas_call x0 -> x4, Pallas kernels: none -> 53.9 us  [the longest x2 27 us: attend_backward(): pl.pallas_call(backward_kernel, name='attend_backward', out_shape=jax.Sha...]
    ppermute x16, waiting for transfers between devices: 81.5 us -> 131 us  [line_side(): return lax.ppermute(value, 'mp', [(i, i ^ 1) for i in range(mp)])]
    ppermute x115 -> x78, starting transfers between devices: 120 us -> 98.6 us  [across(): return lax.ppermute(value, 'dp', [(i, i ^ bit) for i in range(dp)])]
    convert_element_type x6 -> x1, other arithmetic: 17.5 us -> 0.07 us  [tile_overlap(): return meet.astype(jnp.int32).reshape(-1)]
    reduce_sum x4 -> x2, other arithmetic: 16.6 us -> 0.65 us  [body(): qkv_bias_part = jnp.sum(grad_linear.astype(F32), axis=1)]
  transfers between devices with their start and end apart: 155 -> 111, of which waited for: 49 -> 41; matrix products, arithmetic and copies ran while one was open for 29% -> 29% of each run, Pallas kernels for 0% -> 7%
where the time goes in v2:
time: 821 us; the launch traced here: 808 us
  waiting for transfers between devices  301 us (37%)
  starting transfers between devices  183 us (22%)
  matrix products  148 us (18%)
  local copies, waits for them, and re-layouts  62.9 us (8%)
  other arithmetic  56.2 us (7%)
  Pallas kernels  53.9 us (7%)
    dot_general x54, matrix products, dot(): lax.dot_general(left, right, (((left_dim,), (right_dim,)), ((), ())), pre...  148 us
    ppermute x78, waiting for transfers between devices, across(): return lax.ppermute(value, 'dp', [(i, i ^ bit) for i in range(dp)])  143 us
    ppermute x16, waiting for transfers between devices, line_side(): return lax.ppermute(value, 'mp', [(i, i ^ 1) for i in range(mp)])  131 us
    ppermute x78, starting transfers between devices, across(): return lax.ppermute(value, 'dp', [(i, i ^ bit) for i in range(dp)])  98.6 us
    ppermute x13, starting transfers between devices, swap(): return lax.ppermute(value, ('dp', 'mp'), swap_pairs)  71.4 us
    pallas_call x2, Pallas kernels, attend_backward(): pl.pallas_call(backward_kernel, name='attend_backward', out_shape=jax.Sha...  27 us
    pallas_call x2, Pallas kernels, attend_forward(): pl.pallas_call(forward_kernel, name='attend_forward', out_shape=(jax.Shap...  26.9 us
    ppermute x2, waiting for transfers between devices, scatter_vectors(): got = lax.ppermute(sent, 'mp', [(i, i ^ bit) for i in range(mp)])  23 us
  transfers between devices with their start and end apart: 111, of which 41 were waited for; matrix products, arithmetic and copies ran while one was open for 29% of the time, Pallas kernels for 7%

profile of v2, /device:TPU:0, one launch (start us, length us, event | category | flops | bytes accessed | tf_op | source)
XLA Modules:
  0.0 808.5 jit_solution(2126279716436047335)
XLA Ops:
  12.2 6.6 collective-permute-start
  60.9 15.8 %collective-permute-start.13 = (bf16[256,1280]{1,0:T(8,128)(2,1)}, bf16[256,1280]{1,0:T(8,128)(2,1)S(1)}, u32[]{:S(2)}, u32[]{:S(2)}) collective-permute-start(bf16[256,1280]{1,0:T(8,128)(2,1)} %add_convert_fusion.12), channel_id=1, source_target_pairs={{0,4},{4,0},{8,12},{12,8},{16,20},{20,16},{24,28},{28,24},{1,5},{5... | collective-permute-start | bytes 1966088 | tf_op jit(solution)/shard_map/ppermute | solution.py:248
  79.3 14.0 %collective-permute-start.23 = (bf16[2,2,160,1280]{3,2,1,0:T(8,128)(2,1)}, bf16[2,2,160,1280]{3,2,1,0:T(8,128)(2,1)}, u32[]{:S(2)}, u32[]{:S(2)}) collective-permute-start(bf16[2,2,160,1280]{3,2,1,0:T(8,128)(2,1)} %pad_maximum_fusion.9), channel_id=1, source_target_pairs={{0,0},{1,1},{2,4},{3,5},{4,2},{5,3},{6,6},{7,7},{8,8},{9,9},{10,12... | collective-permute-start | bytes 4915208 | tf_op jit(solution)/shard_map/ppermute | solution.py:262
  98.2 9.2 %collective-permute-done.6 = bf16[1,1,160,1408]{3,2,1,0:T(8,128)(2,1)S(1)} collective-permute-done((bf16[1,1,160,1408]{3,2,1,0:T(8,128)(2,1)S(1)}, bf16[1,1,160,1408]{3,2,1,0:T(8,128)(2,1)S(1)}, u32[]{:S(2)}, u32[]{:S(2)}) %collective-permute-start.6) | collective-permute-done | bytes 450592 | tf_op jit(solution)/shard_map/ppermute | solution.py:248
  108.9 5.3 broadcast_add_fusion.1.lin
  114.3 13.4 %attend_forward.2 = (bf16[960,1024]{1,0:T(8,128)(2,1)S(1)}, bf16[320,1024]{1,0:T(8,128)(2,1)S(1)}, f32[4,1,1024]{2,1,0:T(1,128)S(1)}) custom-call(s32[16]{0:T(128)S(1)} %reshape.619.active, f32[960,1024]{1,0:T(8,128)S(1)} %broadcast_add_fusion.1.lin, f32[40,1024]{1,0:T(8,128)S(1)} %get-tuple-element.224.cosine, f32[40,1024]{1,0:T(8,128)S(1)} %get-tuple-element.223.sine, ...), custom_call_target="tpu_custom_call" | custom-call | flops 1342177280 | bytes 10485760 | tf_op jit(solution)/shard_map/attend_forward/pallas_call | solution.py:187
  137.5 8.5 %collective-permute-start.32 = (bf16[2,1,160,1408]{3,2,1,0:T(8,128)(2,1)}, bf16[2,1,160,1408]{3,2,1,0:T(8,128)(2,1)}, u32[]{:S(2)}, u32[]{:S(2)}) collective-permute-start(bf16[2,1,160,1408]{3,2,1,0:T(8,128)(2,1)} %pad_maximum_fusion.16), channel_id=1, source_target_pairs={{0,0},{1,1},{2,4},{3,5},{4,2},{5,3},{6,6},{7,7},{8,8},{9,9},{10,12... | collective-permute-start | bytes 2703368 | tf_op jit(solution)/shard_map/ppermute | solution.py:262
  151.6 10.5 %collective-permute-done.18 = bf16[256,1280]{1,0:T(8,128)(2,1)S(1)} collective-permute-done((bf16[256,1280]{1,0:T(8,128)(2,1)S(1)}, bf16[256,1280]{1,0:T(8,128)(2,1)S(1)}, u32[]{:S(2)}, u32[]{:S(2)}) %collective-permute-start.18) | collective-permute-done | bytes 655392 | tf_op jit(solution)/shard_map/ppermute | solution.py:254
  164.9 17.5 %collective-permute-done.24 = bf16[2,2,160,1280]{3,2,1,0:T(8,128)(2,1)S(1)} collective-permute-done((bf16[2,2,160,1280]{3,2,1,0:T(8,128)(2,1)}, bf16[2,2,160,1280]{3,2,1,0:T(8,128)(2,1)S(1)}, u32[]{:S(2)}, u32[]{:S(2)}) %collective-permute-start.24) | collective-permute-done | bytes 1638432 | tf_op jit(solution)/shard_map/ppermute | solution.py:248
  186.5 14.9 %collective-permute-done.26 = bf16[1,2,160,1280]{3,2,1,0:T(8,128)(2,1)S(1)} collective-permute-done((bf16[1,2,160,1280]{3,2,1,0:T(8,128)(2,1)S(1)}, bf16[1,2,160,1280]{3,2,1,0:T(8,128)(2,1)S(1)}, u32[]{:S(2)}, u32[]{:S(2)}) %collective-permute-start.26) | collective-permute-done | bytes 819232 | tf_op jit(solution)/shard_map/ppermute | solution.py:248
  201.6 7.6 multiply_convert_fusion.3
  228.0 9.9 %collective-permute-done.33 = bf16[2,1,160,1408]{3,2,1,0:T(8,128)(2,1)S(1)} collective-permute-done((bf16[2,1,160,1408]{3,2,1,0:T(8,128)(2,1)}, bf16[2,1,160,1408]{3,2,1,0:T(8,128)(2,1)S(1)}, u32[]{:S(2)}, u32[]{:S(2)}) %collective-permute-start.33) | collective-permute-done | bytes 901152 | tf_op jit(solution)/shard_map/ppermute | solution.py:248
  241.4 5.6 collective-permute-done.30
  252.1 26.4 %collective-permute-start.37 = (bf16[256,1280]{1,0:T(8,128)(2,1)S(1)}, bf16[256,1280]{1,0:T(8,128)(2,1)S(1)}, u32[]{:S(2)}, u32[]{:S(2)}) collective-permute-start(bf16[256,1280]{1,0:T(8,128)(2,1)S(1)} %add_convert_fusion.10), channel_id=1, source_target_pairs={{0,4},{4,0},{8,12},{12,8},{16,20},{20,16},{24,28},{28,24},{1,5},{5... | collective-permute-start | bytes 1966088 | tf_op jit(solution)/shard_map/ppermute | solution.py:248
  278.5 5.7 collective-permute-done.38
  289.4 13.6 %attend_forward.3 = (bf16[960,1024]{1,0:T(8,128)(2,1)S(1)}, bf16[320,1024]{1,0:T(8,128)(2,1)S(1)}, f32[4,1,1024]{2,1,0:T(1,128)S(1)}) custom-call(s32[16]{0:T(128)S(1)} %reshape.619.active, f32[960,1024]{1,0:T(8,128)S(1)} %broadcast_add_fusion.lin, f32[40,1024]{1,0:T(8,128)S(1)} %get-tuple-element.224.cosine, f32[40,1024]{1,0:T(8,128)S(1)} %get-tuple-element.223.sine, ...), custom_call_target="tpu_custom_call" | custom-call | flops 1342177280 | bytes 10485760 | tf_op jit(solution)/shard_map/attend_forward/pallas_call | solution.py:187
  310.3 14.1 %collective-permute-done.58 = bf16[256,1280]{1,0:T(8,128)(2,1)S(1)} collective-permute-done((bf16[256,1280]{1,0:T(8,128)(2,1)S(1)}, bf16[256,1280]{1,0:T(8,128)(2,1)S(1)}, u32[]{:S(2)}, u32[]{:S(2)}) %collective-permute-start.58) | collective-permute-done | bytes 655392 | tf_op jit(solution)/shard_map/ppermute | solution.py:254
  328.7 9.2 %collective-permute-done.42 = bf16[256,1280]{1,0:T(8,128)(2,1)S(1)} collective-permute-done((bf16[256,1280]{1,0:T(8,128)(2,1)S(1)}, bf16[256,1280]{1,0:T(8,128)(2,1)S(1)}, u32[]{:S(2)}, u32[]{:S(2)}) %collective-permute-start.42) | collective-permute-done | bytes 655392 | tf_op jit(solution)/shard_map/ppermute | solution.py:254
  339.8 7.2 collective-permute-done.50
  347.0 8.5 %collective-permute-done.44 = bf16[256,1280]{1,0:T(8,128)(2,1)S(1)} collective-permute-done((bf16[256,1280]{1,0:T(8,128)(2,1)S(1)}, bf16[256,1280]{1,0:T(8,128)(2,1)S(1)}, u32[]{:S(2)}, u32[]{:S(2)}) %collective-permute-start.44) | collective-permute-done | bytes 655392 | tf_op jit(solution)/shard_map/ppermute | solution.py:254
  357.6 7.5 multiply_convert_fusion.2
  365.1 11.3 %convert_reduce_fusion = (f32[1280]{0:T(1024)}, bf16[1024,1280]{1,0:T(8,128)(2,1)S(1)}) fusion(f32[1024,1280]{1,0:T(8,128)} %get-tuple-element.246, f32[1280]{0:T(1024)S(1)} %copy-done.85, bf16[1280,1280]{1,0:T(8,128)(2,1)S(1)} %bitcast.421, bf16[256,1280]{1,0:T(8,128)(2,1)S(1)} %collective-permute-done.59, ...), kind=kOutput, calls=%fused_computation.17 | convolution fusion | flops 3385588480 | bytes 13772800 | tf_op jit(solution)/shard_map/dot_general | solution.py:34
  395.0 15.6 %collective-permute-done.105 = bf16[1,2,160,1280]{3,2,1,0:T(8,128)(2,1)S(1)} collective-permute-done((bf16[1,2,160,1280]{3,2,1,0:T(8,128)(2,1)S(1)}, bf16[1,2,160,1280]{3,2,1,0:T(8,128)(2,1)S(1)}, u32[]{:S(2)}, u32[]{:S(2)}) %collective-permute-start.105) | collective-permute-done | bytes 819232 | tf_op jit(solution)/shard_map/ppermute | solution.py:248
  415.9 10.9 %collective-permute-done.62 = bf16[256,1280]{1,0:T(8,128)(2,1)S(1)} collective-permute-done((bf16[256,1280]{1,0:T(8,128)(2,1)S(1)}, bf16[256,1280]{1,0:T(8,128)(2,1)S(1)}, u32[]{:S(2)}, u32[]{:S(2)}) %collective-permute-start.62) | collective-permute-done | bytes 655392 | tf_op jit(solution)/shard_map/ppermute | solution.py:254
  435.5 12.7 %collective-permute-done.64 = bf16[256,1280]{1,0:T(8,128)(2,1)} collective-permute-done((bf16[256,1280]{1,0:T(8,128)(2,1)S(1)}, bf16[256,1280]{1,0:T(8,128)(2,1)}, u32[]{:S(2)}, u32[]{:S(2)}) %collective-permute-start.64) | collective-permute-done | bytes 655392 | tf_op jit(solution)/shard_map/ppermute | solution.py:254
  448.2 11.8 %collective-permute-done.54 = bf16[256,1280]{1,0:T(8,128)(2,1)} collective-permute-done((bf16[256,1280]{1,0:T(8,128)(2,1)S(1)}, bf16[256,1280]{1,0:T(8,128)(2,1)}, u32[]{:S(2)}, u32[]{:S(2)}) %collective-permute-start.54) | collective-permute-done | bytes 655392 | tf_op jit(solution)/shard_map/ppermute | solution.py:254
  460.0 5.7 fusion.42
  465.7 6.5 collective-permute-start.55
  479.2 13.6 %attend_backward.2 = bf16[960,1024]{1,0:T(8,128)(2,1)S(1)} custom-call(s32[16]{0:T(128)S(1)} %reshape.619.active, bf16[960,1024]{1,0:T(8,128)(2,1)S(1)} %copy-done.5, bf16[320,1024]{1,0:T(8,128)(2,1)S(1)} %get-tuple-element.21.mixed, bf16[320,1024]{1,0:T(8,128)(2,1)S(1)} %convolution_convert_fusion.25.grad_mixed, ...), custom_call_target="tpu_custom_call" | custom-call | flops 3355443200 | bytes 10485760 | tf_op jit(solution)/shard_map/attend_backward/pallas_call | solution.py:214
  506.7 8.4 %collective-permute-done.93 = bf16[1,1,160,1408]{3,2,1,0:T(8,128)(2,1)S(1)} collective-permute-done((bf16[1,1,160,1408]{3,2,1,0:T(8,128)(2,1)S(1)}, bf16[1,1,160,1408]{3,2,1,0:T(8,128)(2,1)S(1)}, u32[]{:S(2)}, u32[]{:S(2)}) %collective-permute-start.93) | collective-permute-done | bytes 450592 | tf_op jit(solution)/shard_map/ppermute | solution.py:248
  518.3 14.5 %collective-permute-done.68 = bf16[256,1280]{1,0:T(8,128)(2,1)S(1)} collective-permute-done((bf16[256,1280]{1,0:T(8,128)(2,1)S(1)}, bf16[256,1280]{1,0:T(8,128)(2,1)S(1)}, u32[]{:S(2)}, u32[]{:S(2)}) %collective-permute-start.68) | collective-permute-done | bytes 655392 | tf_op jit(solution)/shard_map/ppermute | solution.py:254
  539.3 8.5 %collective-permute-start.97 = (bf16[2,1,160,1408]{3,2,1,0:T(8,128)(2,1)}, bf16[2,1,160,1408]{3,2,1,0:T(8,128)(2,1)}, u32[]{:S(2)}, u32[]{:S(2)}) collective-permute-start(bf16[2,1,160,1408]{3,2,1,0:T(8,128)(2,1)} %fusion.62), channel_id=1, source_target_pairs={{0,0},{1,1},{2,4},{3,5},{4,2},{5,3},{6,6},{7,7},{8,8},{9,9},{10,12... | collective-permute-start | bytes 2703368 | tf_op jit(solution)/shard_map/ppermute | solution.py:262
  561.2 8.5 %collective-permute-done.70 = bf16[256,1280]{1,0:T(8,128)(2,1)} collective-permute-done((bf16[256,1280]{1,0:T(8,128)(2,1)S(1)}, bf16[256,1280]{1,0:T(8,128)(2,1)}, u32[]{:S(2)}, u32[]{:S(2)}) %collective-permute-start.70) | collective-permute-done | bytes 655392 | tf_op jit(solution)/shard_map/ppermute | solution.py:254
  575.2 8.6 %convert_reduce_fusion.1 = (f32[1280]{0:T(1024)S(1)}, bf16[1024,1280]{1,0:T(8,128)(2,1)S(1)}) fusion(f32[1024,1280]{1,0:T(8,128)} %get-tuple-element.240, f32[1280]{0:T(1024)S(1)} %copy-done.83, bf16[1280,1280]{1,0:T(8,128)(2,1)S(1)} %bitcast.435, bf16[256,1280]{1,0:T(8,128)(2,1)S(1)} %collective-permute-done.71, ...), kind=kOutput, calls=%fused_computation.18 | convolution fusion | flops 3385588480 | bytes 13772800 | tf_op jit(solution)/shard_map/dot_general | solution.py:34
  585.5 4.4 convolution_convert_fusion.3
  593.0 4.8 convolution_convert_fusion.2
  603.0 16.2 %collective-permute-done.99 = bf16[1,2,160,1280]{3,2,1,0:T(8,128)(2,1)S(1)} collective-permute-done((bf16[1,2,160,1280]{3,2,1,0:T(8,128)(2,1)S(1)}, bf16[1,2,160,1280]{3,2,1,0:T(8,128)(2,1)S(1)}, u32[]{:S(2)}, u32[]{:S(2)}) %collective-permute-start.99) | collective-permute-done | bytes 819232 | tf_op jit(solution)/shard_map/ppermute | solution.py:248
  629.3 14.6 %collective-permute-done.76 = bf16[256,1280]{1,0:T(8,128)(2,1)} collective-permute-done((bf16[256,1280]{1,0:T(8,128)(2,1)}, bf16[256,1280]{1,0:T(8,128)(2,1)}, u32[]{:S(2)}, u32[]{:S(2)}) %collective-permute-start.76) | collective-permute-done | bytes 655392 | tf_op jit(solution)/shard_map/ppermute | solution.py:254
  647.8 10.9 %collective-permute-done.100 = bf16[2,2,160,1280]{3,2,1,0:T(8,128)(2,1)} collective-permute-done((bf16[2,2,160,1280]{3,2,1,0:T(8,128)(2,1)}, bf16[2,2,160,1280]{3,2,1,0:T(8,128)(2,1)}, u32[]{:S(2)}, u32[]{:S(2)}) %collective-permute-start.100) | collective-permute-done | bytes 1638432 | tf_op jit(solution)/shard_map/ppermute | solution.py:248
  664.1 14.2 %collective-permute-start.103 = (bf16[2,2,160,1280]{3,2,1,0:T(8,128)(2,1)}, bf16[2,2,160,1280]{3,2,1,0:T(8,128)(2,1)}, u32[]{:S(2)}, u32[]{:S(2)}) collective-permute-start(bf16[2,2,160,1280]{3,2,1,0:T(8,128)(2,1)} %add_convert_fusion.3), channel_id=1, source_target_pairs={{0,0},{1,1},{2,4},{3,5},{4,2},{5,3},{6,6},{7,7},{8,8},{9,9},{10,12... | collective-permute-start | bytes 4915208 | tf_op jit(solution)/shard_map/ppermute | solution.py:262
  681.4 13.4 %attend_backward.3 = bf16[960,1024]{1,0:T(8,128)(2,1)S(1)} custom-call(s32[16]{0:T(128)S(1)} %reshape.619.active, bf16[960,1024]{1,0:T(8,128)(2,1)S(1)} %copy-done.3, bf16[320,1024]{1,0:T(8,128)(2,1)S(1)} %copy-done.1, bf16[320,1024]{1,0:T(8,128)(2,1)S(1)} %convolution_convert_fusion.24.grad_mixed, f32[4,1,1024]{2,1,0:T(1,128)S(1)} %get-tuple-element.25.log_sum, ...), custom_call_target="tpu_custom_call" | custom-call | flops 3355443200 | bytes 10485760 | tf_op jit(solution)/shard_map/attend_backward/pallas_call | solution.py:214
  696.6 4.2 convolution_convert_fusion.5
  717.0 5.1 collective-permute-done.87
  729.3 4.5 collective-permute-done.80
  745.5 5.2 collective-permute-done.82
  755.0 4.0 fusion.43
  759.0 6.6 collective-permute-start.81
  768.2 20.3 %collective-permute-done.85 = f32[2,1040]{1,0:T(2,128)S(1)} collective-permute-done((f32[2,1040]{1,0:T(2,128)S(1)}, f32[2,1040]{1,0:T(2,128)S(1)}, u32[]{:S(2)}, u32[]{:S(2)}) %collective-permute-start.85) | collective-permute-done | bytes 8352 | tf_op jit(solution)/shard_map/ppermute | solution.py:332
  (711 shorter events, 308.7 us)
Async XLA Ops:
  6.9 24.0 %collective-permute-start.8 = (f32[1,1040]{1,0:T(1,128)S(1)}, f32[1,1040]{1,0:T(1,128)S(1)}, u32[]{:S(2)}, u32[]{:S(2)}) collective-permute-start(f32[1,1040]{1,0:T(1,128)S(1)} %broadcast_in_dim.14), channel_id=1, source_target_pairs={{0,1},{1,0},{2,3},{3,2},{4,5},{5,4},{6,7},{7,6},{8,9},{9,8},{10,11... | collective-permute-start | bytes 12488 | tf_op jit(solution)/shard_map/ppermute | solution.py:314
  12.2 39.5 %collective-permute-start = (bf16[256,1280]{1,0:T(8,128)(2,1)}, bf16[256,1280]{1,0:T(8,128)(2,1)}, u32[]{:S(2)}, u32[]{:S(2)}) collective-permute-start(bf16[256,1280]{1,0:T(8,128)(2,1)} %convert_element_type.538), channel_id=1, source_target_pairs={{0,0},{1,1},{2,4},{3,5},{4,2},{5,3},{6,6},{7,7},{8,8},{9,9},{10,12... | collective-permute-start | bytes 1966088 | tf_op jit(solution)/shard_map/ppermute | solution.py:262
  22.9 26.1 %collective-permute-start.2 = (bf16[1,160,1408]{2,1,0:T(8,128)(2,1)}, bf16[1,160,1408]{2,1,0:T(8,128)(2,1)}, u32[]{:S(2)}, u32[]{:S(2)}) collective-permute-start(bf16[1,160,1408]{2,1,0:T(8,128)(2,1)} %get-tuple-element.220), channel_id=1, source_target_pairs={{0,4},{4,0},{8,12},{12,8},{16,20},{20,16},{24,28},{28,24},{1,5},{5... | collective-permute-start | bytes 1351688 | tf_op jit(solution)/shard_map/ppermute | solution.py:248
  27.4 49.4 %collective-permute-start.22 = (bf16[2,160,1280]{2,1,0:T(8,128)(2,1)}, bf16[2,160,1280]{2,1,0:T(8,128)(2,1)}, u32[]{:S(2)}, u32[]{:S(2)}) collective-permute-start(bf16[2,160,1280]{2,1,0:T(8,128)(2,1)} %get-tuple-element.214), channel_id=1, source_target_pairs={{0,4},{4,0},{8,12},{12,8},{16,20},{20,16},{24,28},{28,24},{1,5},{5... | collective-permute-start | bytes 2457608 | tf_op jit(solution)/shard_map/ppermute | solution.py:248
  55.8 37.5 %collective-permute-start.14 = (bf16[256,1280]{1,0:T(8,128)(2,1)}, bf16[256,1280]{1,0:T(8,128)(2,1)}, u32[]{:S(2)}, u32[]{:S(2)}) collective-permute-start(bf16[256,1280]{1,0:T(8,128)(2,1)} %add_convert_fusion.12), channel_id=1, source_target_pairs={{0,1},{1,0},{2,3},{3,2},{4,5},{5,4},{6,7},{7,6},{8,9},{9,8},{10,11... | collective-permute-start | bytes 1966088 | tf_op jit(solution)/shard_map/ppermute | solution.py:254
  57.1 37.5 %collective-permute-start.4 = (bf16[2,1,160,1408]{3,2,1,0:T(8,128)(2,1)}, bf16[2,1,160,1408]{3,2,1,0:T(8,128)(2,1)S(1)}, u32[]{:S(2)}, u32[]{:S(2)}) collective-permute-start(bf16[2,1,160,1408]{3,2,1,0:T(8,128)(2,1)} %collective-permute-done.3), channel_id=1, source_target_pairs={{0,8},{4,12},{8,0},{12,4},{16,24},{20,28},{24,16},{28,20},{1,9},{5... | collective-permute-start | bytes 2703368 | tf_op jit(solution)/shard_map/ppermute | solution.py:248
  58.7 36.6 %collective-permute-start.5 = (bf16[2,1,160,1408]{3,2,1,0:T(8,128)(2,1)}, bf16[2,1,160,1408]{3,2,1,0:T(8,128)(2,1)}, u32[]{:S(2)}, u32[]{:S(2)}) collective-permute-start(bf16[2,1,160,1408]{3,2,1,0:T(8,128)(2,1)} %collective-permute-done.3), channel_id=1, source_target_pairs={{0,16},{4,20},{8,24},{12,28},{16,0},{20,4},{24,8},{28,12},{1,17},{... | collective-permute-start | bytes 2703368 | tf_op jit(solution)/shard_map/ppermute | solution.py:248
  60.9 47.9 %collective-permute-start.13 = (bf16[256,1280]{1,0:T(8,128)(2,1)}, bf16[256,1280]{1,0:T(8,128)(2,1)S(1)}, u32[]{:S(2)}, u32[]{:S(2)}) collective-permute-start(bf16[256,1280]{1,0:T(8,128)(2,1)} %add_convert_fusion.12), channel_id=1, source_target_pairs={{0,4},{4,0},{8,12},{12,8},{16,20},{20,16},{24,28},{28,24},{1,5},{5... | collective-permute-start | bytes 1966088 | tf_op jit(solution)/shard_map/ppermute | solution.py:248
  79.3 66.8 %collective-permute-start.23 = (bf16[2,2,160,1280]{3,2,1,0:T(8,128)(2,1)}, bf16[2,2,160,1280]{3,2,1,0:T(8,128)(2,1)}, u32[]{:S(2)}, u32[]{:S(2)}) collective-permute-start(bf16[2,2,160,1280]{3,2,1,0:T(8,128)(2,1)} %pad_maximum_fusion.9), channel_id=1, source_target_pairs={{0,0},{1,1},{2,4},{3,5},{4,2},{5,3},{6,6},{7,7},{8,8},{9,9},{10,12... | collective-permute-start | bytes 4915208 | tf_op jit(solution)/shard_map/ppermute | solution.py:262
  136.4 25.7 %collective-permute-start.18 = (bf16[256,1280]{1,0:T(8,128)(2,1)S(1)}, bf16[256,1280]{1,0:T(8,128)(2,1)S(1)}, u32[]{:S(2)}, u32[]{:S(2)}) collective-permute-start(bf16[256,1280]{1,0:T(8,128)(2,1)S(1)} %fusion.35), channel_id=1, source_target_pairs={{0,1},{1,0},{2,3},{3,2},{4,5},{5,4},{6,7},{7,6},{8,9},{9,8},{10,11... | collective-permute-start | bytes 1966088 | tf_op jit(solution)/shard_map/ppermute | solution.py:254
  137.5 77.3 %collective-permute-start.32 = (bf16[2,1,160,1408]{3,2,1,0:T(8,128)(2,1)}, bf16[2,1,160,1408]{3,2,1,0:T(8,128)(2,1)}, u32[]{:S(2)}, u32[]{:S(2)}) collective-permute-start(bf16[2,1,160,1408]{3,2,1,0:T(8,128)(2,1)} %pad_maximum_fusion.16), channel_id=1, source_target_pairs={{0,0},{1,1},{2,4},{3,5},{4,2},{5,3},{6,6},{7,7},{8,8},{9,9},{10,12... | collective-permute-start | bytes 2703368 | tf_op jit(solution)/shard_map/ppermute | solution.py:262
  146.0 36.3 %collective-permute-start.24 = (bf16[2,2,160,1280]{3,2,1,0:T(8,128)(2,1)}, bf16[2,2,160,1280]{3,2,1,0:T(8,128)(2,1)S(1)}, u32[]{:S(2)}, u32[]{:S(2)}) collective-permute-start(bf16[2,2,160,1280]{3,2,1,0:T(8,128)(2,1)} %collective-permute-done.23), channel_id=1, source_target_pairs={{0,8},{4,12},{8,0},{12,4},{16,24},{20,28},{24,16},{28,20},{1,9},{5... | collective-permute-start | bytes 4915208 | tf_op jit(solution)/shard_map/ppermute | solution.py:248
  148.9 37.0 %collective-permute-start.25 = (bf16[2,2,160,1280]{3,2,1,0:T(8,128)(2,1)}, bf16[2,2,160,1280]{3,2,1,0:T(8,128)(2,1)S(1)}, u32[]{:S(2)}, u32[]{:S(2)}) collective-permute-start(bf16[2,2,160,1280]{3,2,1,0:T(8,128)(2,1)} %collective-permute-done.23), channel_id=1, source_target_pairs={{0,16},{4,20},{8,24},{12,28},{16,0},{20,4},{24,8},{28,12},{1,17},{... | collective-permute-start | bytes 4915208 | tf_op jit(solution)/shard_map/ppermute | solution.py:248
  164.8 36.8 %collective-permute-start.19 = (bf16[256,1280]{1,0:T(8,128)(2,1)S(1)}, bf16[256,1280]{1,0:T(8,128)(2,1)S(1)}, u32[]{:S(2)}, u32[]{:S(2)}) collective-permute-start(bf16[256,1280]{1,0:T(8,128)(2,1)S(1)} %add_convert_fusion.11), channel_id=1, source_target_pairs={{0,4},{4,0},{8,12},{12,8},{16,20},{20,16},{24,28},{28,24},{1,5},{5... | collective-permute-start | bytes 1966088 | tf_op jit(solution)/shard_map/ppermute | solution.py:248
  213.2 90.5 %collective-permute-start.56 = (bf16[256,1280]{1,0:T(8,128)(2,1)S(1)}, bf16[256,1280]{1,0:T(8,128)(2,1)}, u32[]{:S(2)}, u32[]{:S(2)}) collective-permute-start(bf16[256,1280]{1,0:T(8,128)(2,1)S(1)} %convert_element_type.576), channel_id=1, source_target_pairs={{0,0},{1,1},{2,4},{3,5},{4,2},{5,3},{6,6},{7,7},{8,8},{9,9},{10,12... | collective-permute-start | bytes 1966088 | tf_op jit(solution)/shard_map/ppermute | solution.py:262
  214.8 23.0 %collective-permute-start.33 = (bf16[2,1,160,1408]{3,2,1,0:T(8,128)(2,1)}, bf16[2,1,160,1408]{3,2,1,0:T(8,128)(2,1)S(1)}, u32[]{:S(2)}, u32[]{:S(2)}) collective-permute-start(bf16[2,1,160,1408]{3,2,1,0:T(8,128)(2,1)} %collective-permute-done.32), channel_id=1, source_target_pairs={{0,8},{4,12},{8,0},{12,4},{16,24},{20,28},{24,16},{28,20},{1,9},{5... | collective-permute-start | bytes 2703368 | tf_op jit(solution)/shard_map/ppermute | solution.py:248
  223.4 23.7 %collective-permute-start.30 = (bf16[256,1280]{1,0:T(8,128)(2,1)S(1)}, bf16[256,1280]{1,0:T(8,128)(2,1)S(1)}, u32[]{:S(2)}, u32[]{:S(2)}) collective-permute-start(bf16[256,1280]{1,0:T(8,128)(2,1)S(1)} %fusion.38), channel_id=1, source_target_pairs={{0,1},{1,0},{2,3},{3,2},{4,5},{5,4},{6,7},{7,6},{8,9},{9,8},{10,11... | collective-permute-start | bytes 1966088 | tf_op jit(solution)/shard_map/ppermute | solution.py:254
  241.0 43.3 %collective-permute-start.36 = (bf16[1,1,160,1408]{3,2,1,0:T(8,128)(2,1)S(1)}, bf16[1,1,160,1408]{3,2,1,0:T(8,128)(2,1)S(1)}, u32[]{:S(2)}, u32[]{:S(2)}) collective-permute-start(bf16[1,1,160,1408]{3,2,1,0:T(8,128)(2,1)S(1)} %slice.820), channel_id=1, source_target_pairs={{0,8},{4,12},{8,0},{12,4},{16,24},{20,28},{24,16},{28,20},{1,9},{5... | collective-permute-start | bytes 1351688 | tf_op jit(solution)/shard_map/ppermute | solution.py:248
  250.0 34.1 %collective-permute-start.38 = (bf16[256,1280]{1,0:T(8,128)(2,1)S(1)}, bf16[256,1280]{1,0:T(8,128)(2,1)S(1)}, u32[]{:S(2)}, u32[]{:S(2)}) collective-permute-start(bf16[256,1280]{1,0:T(8,128)(2,1)S(1)} %add_convert_fusion.10), channel_id=1, source_target_pairs={{0,1},{1,0},{2,3},{3,2},{4,5},{5,4},{6,7},{7,6},{8,9},{9,8},{10,11... | collective-permute-start | bytes 1966088 | tf_op jit(solution)/shard_map/ppermute | solution.py:254
  250.4 74.0 %collective-permute-start.48 = (bf16[2,2,160,1280]{3,2,1,0:T(8,128)(2,1)S(1)}, bf16[2,2,160,1280]{3,2,1,0:T(8,128)(2,1)S(1)}, u32[]{:S(2)}, u32[]{:S(2)}) collective-permute-start(bf16[2,2,160,1280]{3,2,1,0:T(8,128)(2,1)S(1)} %collective-permute-done.47), channel_id=1, source_target_pairs={{0,8},{4,12},{8,0},{12,4},{16,24},{20,28},{24,16},{28,20},{1,9},{5... | collective-permute-start | bytes 4915208 | tf_op jit(solution)/shard_map/ppermute | solution.py:248
  252.1 33.4 %collective-permute-start.37 = (bf16[256,1280]{1,0:T(8,128)(2,1)S(1)}, bf16[256,1280]{1,0:T(8,128)(2,1)S(1)}, u32[]{:S(2)}, u32[]{:S(2)}) collective-permute-start(bf16[256,1280]{1,0:T(8,128)(2,1)S(1)} %add_convert_fusion.10), channel_id=1, source_target_pairs={{0,4},{4,0},{8,12},{12,8},{16,20},{20,16},{24,28},{28,24},{1,5},{5... | collective-permute-start | bytes 1966088 | tf_op jit(solution)/shard_map/ppermute | solution.py:248
  284.2 40.7 %collective-permute-start.49 = (bf16[2,2,160,1280]{3,2,1,0:T(8,128)(2,1)S(1)}, bf16[2,2,160,1280]{3,2,1,0:T(8,128)(2,1)S(1)}, u32[]{:S(2)}, u32[]{:S(2)}) collective-permute-start(bf16[2,2,160,1280]{3,2,1,0:T(8,128)(2,1)S(1)} %collective-permute-done.47), channel_id=1, source_target_pairs={{0,16},{4,20},{8,24},{12,28},{16,0},{20,4},{24,8},{28,12},{1,17},{... | collective-permute-start | bytes 4915208 | tf_op jit(solution)/shard_map/ppermute | solution.py:248
  308.4 29.5 %collective-permute-start.42 = (bf16[256,1280]{1,0:T(8,128)(2,1)S(1)}, bf16[256,1280]{1,0:T(8,128)(2,1)S(1)}, u32[]{:S(2)}, u32[]{:S(2)}) collective-permute-start(bf16[256,1280]{1,0:T(8,128)(2,1)S(1)} %fusion.36), channel_id=1, source_target_pairs={{0,1},{1,0},{2,3},{3,2},{4,5},{5,4},{6,7},{7,6},{8,9},{9,8},{10,11... | collective-permute-start | bytes 1966088 | tf_op jit(solution)/shard_map/ppermute | solution.py:254
  324.4 40.7 %collective-permute-start.57 = (bf16[256,1280]{1,0:T(8,128)(2,1)S(1)}, bf16[256,1280]{1,0:T(8,128)(2,1)S(1)}, u32[]{:S(2)}, u32[]{:S(2)}) collective-permute-start(bf16[256,1280]{1,0:T(8,128)(2,1)S(1)} %get-tuple-element.135), channel_id=1, source_target_pairs={{0,4},{4,0},{8,12},{12,8},{16,20},{20,16},{24,28},{28,24},{1,5},{5... | collective-permute-start | bytes 1966088 | tf_op jit(solution)/shard_map/ppermute | solution.py:248
  324.4 40.7 %collective-permute-start.59 = (bf16[256,1280]{1,0:T(8,128)(2,1)S(1)}, bf16[256,1280]{1,0:T(8,128)(2,1)S(1)}, u32[]{:S(2)}, u32[]{:S(2)}) collective-permute-start(bf16[256,1280]{1,0:T(8,128)(2,1)S(1)} %collective-permute-done.58), channel_id=1, source_target_pairs={{0,4},{4,0},{8,12},{12,8},{16,20},{20,16},{24,28},{28,24},{1,5},{5... | collective-permute-start | bytes 1966088 | tf_op jit(solution)/shard_map/ppermute | solution.py:248
  328.6 26.9 %collective-permute-start.51 = (bf16[1,2,160,1280]{3,2,1,0:T(8,128)(2,1)S(1)}, bf16[1,2,160,1280]{3,2,1,0:T(8,128)(2,1)S(1)}, u32[]{:S(2)}, u32[]{:S(2)}) collective-permute-start(bf16[1,2,160,1280]{3,2,1,0:T(8,128)(2,1)S(1)} %slice.833), channel_id=1, source_target_pairs={{0,8},{4,12},{8,0},{12,4},{16,24},{20,28},{24,16},{28,20},{1,9},{5... | collective-permute-start | bytes 2457608 | tf_op jit(solution)/shard_map/ppermute | solution.py:248
  378.5 36.7 %collective-permute-start.60 = (bf16[256,1280]{1,0:T(8,128)(2,1)S(1)}, bf16[256,1280]{1,0:T(8,128)(2,1)S(1)}, u32[]{:S(2)}, u32[]{:S(2)}) collective-permute-start(bf16[256,1280]{1,0:T(8,128)(2,1)S(1)} %convolution_convert_fusion.19), channel_id=1, source_target_pairs={{0,4},{4,0},{8,12},{12,8},{16,20},{20,16},{24,28},{28,24},{1,5},{5... | collective-permute-start | bytes 1966088 | tf_op jit(solution)/shard_map/ppermute | solution.py:248
  392.2 43.3 %collective-permute-start.52 = (bf16[256,1280]{1,0:T(8,128)(2,1)S(1)}, bf16[256,1280]{1,0:T(8,128)(2,1)S(1)}, u32[]{:S(2)}, u32[]{:S(2)}) collective-permute-start(bf16[256,1280]{1,0:T(8,128)(2,1)S(1)} %convolution_convert_fusion.21), channel_id=1, source_target_pairs={{0,4},{4,0},{8,12},{12,8},{16,20},{20,16},{24,28},{28,24},{1,5},{5... | collective-permute-start | bytes 1966088 | tf_op jit(solution)/shard_map/ppermute | solution.py:248
  393.3 37.6 %collective-permute-start.53 = (bf16[256,1280]{1,0:T(8,128)(2,1)S(1)}, bf16[256,1280]{1,0:T(8,128)(2,1)S(1)}, u32[]{:S(2)}, u32[]{:S(2)}) collective-permute-start(bf16[256,1280]{1,0:T(8,128)(2,1)S(1)} %convolution_convert_fusion.20), channel_id=1, source_target_pairs={{0,4},{4,0},{8,12},{12,8},{16,20},{20,16},{24,28},{28,24},{1,5},{5... | collective-permute-start | bytes 1966088 | tf_op jit(solution)/shard_map/ppermute | solution.py:248
  412.6 59.6 %collective-permute-start.106 = (bf16[2,2,160,1280]{3,2,1,0:T(8,128)(2,1)}, bf16[2,2,160,1280]{3,2,1,0:T(8,128)(2,1)}, u32[]{:S(2)}, u32[]{:S(2)}) collective-permute-start(bf16[2,2,160,1280]{3,2,1,0:T(8,128)(2,1)} %maximum_maximum_fusion.1), channel_id=1, source_target_pairs={{0,8},{4,12},{8,0},{12,4},{16,24},{20,28},{24,16},{28,20},{1,9},{5... | collective-permute-start | bytes 4915208 | tf_op jit(solution)/shard_map/ppermute | solution.py:248
  415.1 57.1 %collective-permute-start.108 = (bf16[2,2,160,1280]{3,2,1,0:T(8,128)(2,1)}, bf16[2,2,160,1280]{3,2,1,0:T(8,128)(2,1)}, u32[]{:S(2)}, u32[]{:S(2)}) collective-permute-start(bf16[2,2,160,1280]{3,2,1,0:T(8,128)(2,1)} %pad_maximum_fusion.12), channel_id=1, source_target_pairs={{0,16},{4,20},{8,24},{12,28},{16,0},{20,4},{24,8},{28,12},{1,17},{... | collective-permute-start | bytes 4915208 | tf_op jit(solution)/shard_map/ppermute | solution.py:248
  432.0 28.0 %collective-permute-start.54 = (bf16[256,1280]{1,0:T(8,128)(2,1)S(1)}, bf16[256,1280]{1,0:T(8,128)(2,1)}, u32[]{:S(2)}, u32[]{:S(2)}) collective-permute-start(bf16[256,1280]{1,0:T(8,128)(2,1)S(1)} %fusion.39), channel_id=1, source_target_pairs={{0,1},{1,0},{2,3},{3,2},{4,5},{5,4},{6,7},{7,6},{8,9},{9,8},{10,11... | collective-permute-start | bytes 1966088 | tf_op jit(solution)/shard_map/ppermute | solution.py:254
  435.5 40.8 %collective-permute-start.63 = (bf16[256,1280]{1,0:T(8,128)(2,1)S(1)}, bf16[256,1280]{1,0:T(8,128)(2,1)}, u32[]{:S(2)}, u32[]{:S(2)}) collective-permute-start(bf16[256,1280]{1,0:T(8,128)(2,1)S(1)} %get-tuple-element.140), channel_id=1, source_target_pairs={{0,4},{4,0},{8,12},{12,8},{16,20},{20,16},{24,28},{28,24},{1,5},{5... | collective-permute-start | bytes 1966088 | tf_op jit(solution)/shard_map/ppermute | solution.py:248
  448.2 28.1 %collective-permute-start.65 = (bf16[256,1280]{1,0:T(8,128)(2,1)}, bf16[256,1280]{1,0:T(8,128)(2,1)}, u32[]{:S(2)}, u32[]{:S(2)}) collective-permute-start(bf16[256,1280]{1,0:T(8,128)(2,1)} %collective-permute-done.64), channel_id=1, source_target_pairs={{0,4},{4,0},{8,12},{12,8},{16,20},{20,16},{24,28},{28,24},{1,5},{5... | collective-permute-start | bytes 1966088 | tf_op jit(solution)/shard_map/ppermute | solution.py:248
  465.7 90.5 %collective-permute-start.55 = (bf16[256,1280]{1,0:T(8,128)(2,1)}, bf16[256,1280]{1,0:T(8,128)(2,1)}, u32[]{:S(2)}, u32[]{:S(2)}) collective-permute-start(bf16[256,1280]{1,0:T(8,128)(2,1)} %fusion.42), channel_id=1, source_target_pairs={{0,0},{1,1},{2,4},{3,5},{4,2},{5,3},{6,6},{7,7},{8,8},{9,9},{10,12... | collective-permute-start | bytes 1966088 | tf_op jit(solution)/shard_map/ppermute | solution.py:262
  475.4 74.9 %collective-permute-start.109 = (bf16[2,2,160,1280]{3,2,1,0:T(8,128)(2,1)S(1)}, bf16[2,2,160,1280]{3,2,1,0:T(8,128)(2,1)S(1)}, u32[]{:S(2)}, u32[]{:S(2)}) collective-permute-start(bf16[2,2,160,1280]{3,2,1,0:T(8,128)(2,1)S(1)} %add_convert_fusion.2), channel_id=1, source_target_pairs={{0,0},{1,1},{2,4},{3,5},{4,2},{5,3},{6,6},{7,7},{8,8},{9,9},{10,12... | collective-permute-start | bytes 4915208 | tf_op jit(solution)/shard_map/ppermute | solution.py:262
  539.3 30.4 %collective-permute-start.97 = (bf16[2,1,160,1408]{3,2,1,0:T(8,128)(2,1)}, bf16[2,1,160,1408]{3,2,1,0:T(8,128)(2,1)}, u32[]{:S(2)}, u32[]{:S(2)}) collective-permute-start(bf16[2,1,160,1408]{3,2,1,0:T(8,128)(2,1)} %fusion.62), channel_id=1, source_target_pairs={{0,0},{1,1},{2,4},{3,5},{4,2},{5,3},{6,6},{7,7},{8,8},{9,9},{10,12... | collective-permute-start | bytes 2703368 | tf_op jit(solution)/shard_map/ppermute | solution.py:262
  571.5 56.3 %collective-permute-start.98 = (bf16[1,160,1408]{2,1,0:T(8,128)(2,1)}, bf16[1,160,1408]{2,1,0:T(8,128)(2,1)}, u32[]{:S(2)}, u32[]{:S(2)}) collective-permute-start(bf16[1,160,1408]{2,1,0:T(8,128)(2,1)} %slice_bitcast_fusion.18), channel_id=1, source_target_pairs={{0,4},{4,0},{8,12},{12,8},{16,20},{20,16},{24,28},{28,24},{1,5},{5... | collective-permute-start | bytes 1351688 | tf_op jit(solution)/shard_map/ppermute | solution.py:248
  620.8 37.9 %collective-permute-start.100 = (bf16[2,2,160,1280]{3,2,1,0:T(8,128)(2,1)}, bf16[2,2,160,1280]{3,2,1,0:T(8,128)(2,1)}, u32[]{:S(2)}, u32[]{:S(2)}) collective-permute-start(bf16[2,2,160,1280]{3,2,1,0:T(8,128)(2,1)} %maximum_maximum_fusion), channel_id=1, source_target_pairs={{0,8},{4,12},{8,0},{12,4},{16,24},{20,28},{24,16},{28,20},{1,9},{5... | collective-permute-start | bytes 4915208 | tf_op jit(solution)/shard_map/ppermute | solution.py:248
  622.4 37.9 %collective-permute-start.102 = (bf16[2,2,160,1280]{3,2,1,0:T(8,128)(2,1)}, bf16[2,2,160,1280]{3,2,1,0:T(8,128)(2,1)}, u32[]{:S(2)}, u32[]{:S(2)}) collective-permute-start(bf16[2,2,160,1280]{3,2,1,0:T(8,128)(2,1)} %pad_maximum_fusion.11), channel_id=1, source_target_pairs={{0,16},{4,20},{8,24},{12,28},{16,0},{20,4},{24,8},{28,12},{1,17},{... | collective-permute-start | bytes 4915208 | tf_op jit(solution)/shard_map/ppermute | solution.py:248
  629.2 49.1 %collective-permute-start.75 = (bf16[256,1280]{1,0:T(8,128)(2,1)}, bf16[256,1280]{1,0:T(8,128)(2,1)}, u32[]{:S(2)}, u32[]{:S(2)}) collective-permute-start(bf16[256,1280]{1,0:T(8,128)(2,1)} %get-tuple-element.143), channel_id=1, source_target_pairs={{0,4},{4,0},{8,12},{12,8},{16,20},{20,16},{24,28},{28,24},{1,5},{5... | collective-permute-start | bytes 1966088 | tf_op jit(solution)/shard_map/ppermute | solution.py:248
  643.9 34.4 %collective-permute-start.77 = (bf16[256,1280]{1,0:T(8,128)(2,1)}, bf16[256,1280]{1,0:T(8,128)(2,1)}, u32[]{:S(2)}, u32[]{:S(2)}) collective-permute-start(bf16[256,1280]{1,0:T(8,128)(2,1)} %collective-permute-done.76), channel_id=1, source_target_pairs={{0,4},{4,0},{8,12},{12,8},{16,20},{20,16},{24,28},{28,24},{1,5},{5... | collective-permute-start | bytes 1966088 | tf_op jit(solution)/shard_map/ppermute | solution.py:248
  664.1 124.5 %collective-permute-start.103 = (bf16[2,2,160,1280]{3,2,1,0:T(8,128)(2,1)}, bf16[2,2,160,1280]{3,2,1,0:T(8,128)(2,1)}, u32[]{:S(2)}, u32[]{:S(2)}) collective-permute-start(bf16[2,2,160,1280]{3,2,1,0:T(8,128)(2,1)} %add_convert_fusion.3), channel_id=1, source_target_pairs={{0,0},{1,1},{2,4},{3,5},{4,2},{5,3},{6,6},{7,7},{8,8},{9,9},{10,12... | collective-permute-start | bytes 4915208 | tf_op jit(solution)/shard_map/ppermute | solution.py:262
  725.9 39.7 %collective-permute-start.88 = (bf16[2,1,160,1408]{3,2,1,0:T(8,128)(2,1)}, bf16[2,1,160,1408]{3,2,1,0:T(8,128)(2,1)}, u32[]{:S(2)}, u32[]{:S(2)}) collective-permute-start(bf16[2,1,160,1408]{3,2,1,0:T(8,128)(2,1)} %pad_maximum_fusion.17), channel_id=1, source_target_pairs={{0,8},{4,12},{8,0},{12,4},{16,24},{20,28},{24,16},{28,20},{1,9},{5... | collective-permute-start | bytes 2703368 | tf_op jit(solution)/shard_map/ppermute | solution.py:248
  727.5 38.1 %collective-permute-start.90 = (bf16[2,1,160,1408]{3,2,1,0:T(8,128)(2,1)}, bf16[2,1,160,1408]{3,2,1,0:T(8,128)(2,1)}, u32[]{:S(2)}, u32[]{:S(2)}) collective-permute-start(bf16[2,1,160,1408]{3,2,1,0:T(8,128)(2,1)} %pad_maximum_fusion.18), channel_id=1, source_target_pairs={{0,16},{4,20},{8,24},{12,28},{16,0},{20,4},{24,8},{28,12},{1,17},{... | collective-permute-start | bytes 2703368 | tf_op jit(solution)/shard_map/ppermute | solution.py:248
  759.0 39.1 %collective-permute-start.81 = (bf16[256,1280]{1,0:T(8,128)(2,1)}, bf16[256,1280]{1,0:T(8,128)(2,1)}, u32[]{:S(2)}, u32[]{:S(2)}) collective-permute-start(bf16[256,1280]{1,0:T(8,128)(2,1)} %fusion.43), channel_id=1, source_target_pairs={{0,0},{1,1},{2,4},{3,5},{4,2},{5,3},{6,6},{7,7},{8,8},{9,9},{10,12... | collective-permute-start | bytes 1966088 | tf_op jit(solution)/shard_map/ppermute | solution.py:262
  765.6 22.9 %collective-permute-start.85 = (f32[2,1040]{1,0:T(2,128)S(1)}, f32[2,1040]{1,0:T(2,128)S(1)}, u32[]{:S(2)}, u32[]{:S(2)}) collective-permute-start(f32[2,1040]{1,0:T(2,128)S(1)} %broadcast_select_fusion.1), channel_id=1, source_target_pairs={{0,2},{1,3},{2,0},{3,1},{4,6},{5,7},{6,4},{7,5},{8,10},{9,11},{10,... | collective-permute-start | bytes 24968 | tf_op jit(solution)/shard_map/ppermute | solution.py:332
  767.4 32.9 %collective-permute-start.91 = (bf16[2,1,160,1408]{3,2,1,0:T(8,128)(2,1)S(1)}, bf16[2,1,160,1408]{3,2,1,0:T(8,128)(2,1)S(1)}, u32[]{:S(2)}, u32[]{:S(2)}) collective-permute-start(bf16[2,1,160,1408]{3,2,1,0:T(8,128)(2,1)S(1)} %fusion.61), channel_id=1, source_target_pairs={{0,0},{1,1},{2,4},{3,5},{4,2},{5,3},{6,6},{7,7},{8,8},{9,9},{10,12... | collective-permute-start | bytes 2703368 | tf_op jit(solution)/shard_map/ppermute | solution.py:262
  (189 other events, 2641.8 us)

commit v3 on v2

--- a/solution.py
+++ b/solution.py
@@ -1,3 +1,5 @@
+import functools
+
 import jax
 import jax.numpy as jnp
 from jax import lax
@@ -73,21 +75,12 @@
     return pl.ds(pl.multiple_of(at * TILE, TILE), TILE)
 
 
-def forward_kernel(active, lin, cosine, sine, code_row, code_col, qkv, mixed, log_sum, k_rows, top, total, acc):
+def forward_kernel(active, qkv, code_row, code_col, mixed, log_sum, k_rows, top, total, acc):
     heads, length = k_rows.shape[0], k_rows.shape[1]
     blocks = length // TILE
-    cos, sin = cosine[...], sine[...]
-    half = HD // 2
     for head in range(heads):
-        for which in range(2):
-            base = (which * heads + head) * HD
-            low, high = lin[base : base + half, :], lin[base + half : base + HD, :]
-            turned = jnp.concatenate([low * cos - high * sin, high * cos + low * sin], axis=0)
-            qkv[base : base + HD, :] = turned.astype(BF16)
-            if which == 1:
-                k_rows[head] = turned.T.astype(BF16)
-        base = (2 * heads + head) * HD
-        qkv[base : base + HD, :] = lin[base : base + HD, :].astype(BF16)
+        base = (heads + head) * HD
+        k_rows[head] = turned(qkv[base : base + HD, :]).astype(BF16)
 
     def query_block(q_at, carry):
         queries = tiles(q_at)
@@ -180,20 +173,19 @@
     return [pl.BlockSpec(memory_space=pltpu.VMEM)] * count
 
 
-def attend_forward(linear, facts):
-    active, cosine, sine, code_row, code_col = facts
-    width, length = linear.shape
+def attend_forward(qkv, facts):
+    active, _, _, code_row, code_col = facts
+    width, length = qkv.shape
     heads = width // (3 * HD)
     return pl.pallas_call(
         forward_kernel,
         name="attend_forward",
         out_shape=(
-            jax.ShapeDtypeStruct((width, length), BF16),
             jax.ShapeDtypeStruct((heads * HD, length), BF16),
             jax.ShapeDtypeStruct((heads, 1, length), F32),
         ),
-        in_specs=[pl.BlockSpec(memory_space=pltpu.SMEM)] + whole(5),
-        out_specs=tuple(whole(3)),
+        in_specs=[pl.BlockSpec(memory_space=pltpu.SMEM)] + whole(3),
+        out_specs=tuple(whole(2)),
         scratch_shapes=[
             pltpu.VMEM((heads, length, HD), BF16),
             pltpu.VMEM((heads, 1, TILE), F32),
@@ -202,9 +194,11 @@
         ],
         compiler_params=pltpu.CompilerParams(vmem_limit_bytes=40 << 20),
         cost_estimate=pl.CostEstimate(
-            flops=heads * length * length * HD * 4, bytes_accessed=10 << 20, transcendentals=heads * length * length
+            flops=heads * length * length * HD * 4,
+            bytes_accessed=4 << 20,
+            transcendentals=heads * length * length,
         ),
-    )(active, linear, cosine, sine, code_row, code_col)
+    )(active, qkv, code_row, code_col)
 
 
 def attend_backward(qkv, mixed, grad_mixed, log_sum, facts):
@@ -239,6 +233,783 @@
     return meet.astype(jnp.int32).reshape(-1)
 
 
+(
+    ACT, ALL, ATTN, BACKWARD, CORE, CORNER, CORNERS, CROSS, DIAGONAL, DOWN, ENDS, ENTER, ENTERED,
+    ENTER_AT, ENTER_BIAS, ENTER_GAIN, ENTER_W, FAR_IN, FAR_OUT, FAR_OWN, FINAL, FIRST,
+    FIRST_BIAS, FORWARD, FROM_HIGH, FROM_LOW, GRAD, HELD, HERE, HIGH, LEAVE, LEAVE_BIAS,
+    LEAVE_GAIN, LEAVE_SHIFT, LEAVE_W, LINE, LINE_IN, LINE_OUT, LOW, MINE, MIX, MIXED, MIX_AT,
+    MIX_GAIN, MIX_SHIFT, NEAR_IN, NEAR_OUT, OWN, OWNED, PAIR, PROJ, QKV, REMOTE, REORDER, RESULT,
+    ROWS, ROWS2, ROWS_OUT, SECOND, SECOND_BIAS, SLOPE, SOURCE, STATE, SUMS, TARGET, UNIT_SUMS,
+    UP, VALUE, WIDE_SUMS,
+) = range(69)
+COTANGENT, COSINE, SINE = 100, 101, 102
+FIRST_HBM = 200
+COTANGENT_HBM = FIRST_HBM + 50
+(
+    ACT_HBM, FACTS_HBM, HIDDEN_HBM, MOVED_HBM, ROWS2_HBM, ROWS_HBM, ROW_FACTS_HBM, SLOPE_HBM,
+    VECTORS_HBM, VECTOR_HBM,
+) = range(FIRST_HBM, FIRST_HBM + 10)
+
+
+STRIP = 256
+PARTS = 2
+MESH_ID = pl.DeviceIdType.MESH
+
+
+def strips(at):
+    return pl.ds(pl.multiple_of(at * STRIP, STRIP), STRIP)
+
+
+def partners():
+    dp_at, mp_at = lax.axis_index("dp"), lax.axis_index("mp")
+    core = dp_at + 1 - 2 * lax.rem(dp_at, 2)
+    cross = mp_at + 2 - 4 * (mp_at // 2)
+    return {
+        CORE: {"dp": core},
+        LINE: {"mp": mp_at + 1 - 2 * lax.rem(mp_at, 2)},
+        CROSS: {"mp": cross},
+        DIAGONAL: {"dp": core, "mp": cross},
+        LOW: {"dp": dp_at + 2 - 4 * lax.rem(dp_at // 2, 2)},
+        HIGH: {"dp": dp_at + 4 - 8 * lax.rem(dp_at // 4, 2)},
+    }
+
+
+def greet(names):
+    barrier, devices = pltpu.get_barrier_semaphore(), partners()
+    for name in names:
+        pl.semaphore_signal(barrier, inc=1, device_id=devices[name], device_id_type=MESH_ID)
+    return lambda: pl.semaphore_wait(barrier, len(names))
+
+
+class Courier:
+    def __init__(self, ref):
+        self.ref, self.devices = ref, partners()
+        self.remotes, self.locals = 0, 0
+        self.open = {}
+        self.aligned = lax.rem(lax.axis_index("dp"), 2) == lax.axis_index("mp") // 2
+
+    def slot(self):
+        self.remotes += 1
+        return self.remotes - 1
+
+    def remote(self, source, target, partner, at, received=None):
+        sems = self.ref[REMOTE]
+        received = at if received is None else received
+        return pltpu.make_async_remote_copy(
+            src_ref=source,
+            dst_ref=target,
+            send_sem=sems.at[0, at],
+            recv_sem=sems.at[1, received],
+            device_id=self.devices[partner],
+            device_id_type=MESH_ID,
+        )
+
+    def send(self, source, target, partner):
+        copy = self.remote(source, target, partner, self.slot())
+        copy.start()
+        return copy
+
+    def near(self, source, target):
+        return pltpu.make_async_copy(source, target, self.ref[HERE].at[self.locals])
+
+    def local(self, source, target):
+        copy = self.near(source, target)
+        self.locals += 1
+        copy.start()
+        return copy
+
+    def swap(self, source, target):
+        at, copy = self.slot(), self.near(source, target)
+        self.locals += 1
+        away = lambda: self.remote(source, target, DIAGONAL, at)
+        pl.when(self.aligned)(copy.start)
+        pl.when(jnp.logical_not(self.aligned))(lambda: away().start())
+
+        def finish():
+            pl.when(self.aligned)(copy.wait)
+            pl.when(jnp.logical_not(self.aligned))(lambda: away().wait())
+
+        return finish
+
+    def begin(self, pack, step):
+        ref = self.ref
+        buffer = lambda part: ref[(pack, part)]
+        if step == 1:
+            mine, pair = buffer(MINE), buffer(PAIR)
+            first, second, copy = self.slot(), self.slot(), self.near(mine, pair.at[0])
+            self.locals += 1
+            across = lambda: self.remote(mine, pair.at[1], CROSS, first)
+            beside = lambda: self.remote(mine, pair.at[1], CORE, first)
+            over = lambda: self.remote(mine, pair.at[0], DIAGONAL, second)
+
+            def start_aligned():
+                copy.start()
+                across().start()
+
+            def start_other():
+                beside().start()
+                over().start()
+
+            def wait_aligned():
+                copy.wait()
+                across().wait()
+
+            def wait_other():
+                beside().wait()
+                over().wait()
+
+            pl.when(self.aligned)(start_aligned)
+            pl.when(jnp.logical_not(self.aligned))(start_other)
+
+            def finish():
+                pl.when(self.aligned)(wait_aligned)
+                pl.when(jnp.logical_not(self.aligned))(wait_other)
+
+        elif step > 4:
+            self.finish(pack, step - 1)
+            finish = self.reduce(pack, step)
+        else:
+            self.finish(pack, step - 1)
+            if step == 4:
+                depth = buffer(CORNERS).shape[1]
+                block = lambda at: buffer(GRAD).at[at * depth : (at + 1) * depth]
+                copies = [
+                    self.send(block(6), buffer(CORNERS).at[0], HIGH),
+                    self.send(block(7), buffer(CORNERS).at[1], LOW),
+                ]
+            elif step == 2:
+                pair = buffer(PAIR)
+                copies = [self.send(pair, buffer(side), side) for side in (LOW, HIGH)]
+            else:
+                copies = [
+                    self.send(buffer(LOW).at[0], buffer(CORNER).at[0], HIGH),
+                    self.send(buffer(HIGH).at[1], buffer(CORNER).at[1], LOW),
+                ]
+
+            def finish():
+                for copy in copies:
+                    copy.wait()
+
+        self.open[pack, step] = finish
+
+    def fetch(self, columns, terms):
+        held = self.ref[HELD, columns]
+        loads = [self.local(term, held.at[at]) for at, term in enumerate(terms)]
+        for load in loads:
+            load.wait()
+        return lambda at: held[at].astype(F32)
+
+    def reduce(self, pack, step):
+        ref = self.ref
+        buffer = lambda part: ref[pack, part]
+        if step == 7:
+            ends = buffer(ENDS)
+            columns = ends.shape[2]
+            term = self.fetch(columns, [ends.at[0], ends.at[1]])
+            result = ref[RESULT, columns, pack]
+            result[...] = term(0) + term(1)
+            return self.local(result, buffer(RESULT)).wait
+        depth, columns = buffer(GRAD).shape[0] // 8, buffer(GRAD).shape[1]
+        block = lambda at: buffer(GRAD).at[at * depth : (at + 1) * depth]
+        sums = ref[SUMS, pack]
+        if step == 5:
+            corners, from_low, from_high = buffer(CORNERS), buffer(FROM_LOW), buffer(FROM_HIGH)
+            copies = [
+                self.send(block(3), from_low.at[1], LOW),
+                self.send(block(4), from_high.at[0], HIGH),
+            ]
+            term = self.fetch(columns, [block(2), block(5), corners.at[0], corners.at[1]])
+            for at in range(2):
+                sums[at] = (term(at) + term(2 + at)).astype(BF16)
+            copies.append(self.send(sums.at[0], from_low.at[0], LOW))
+            copies.append(self.send(sums.at[1], from_high.at[1], HIGH))
+
+            def finish():
+                for copy in copies:
+                    copy.wait()
+
+            return finish
+        ends, sides = buffer(ENDS), (buffer(FROM_LOW), buffer(FROM_HIGH))
+        term = self.fetch(
+            columns, [block(0), block(1)] + [side.at[at] for side in sides for at in range(2)]
+        )
+        for at in range(2):
+            sums[at] = (term(at) + term(2 + at) + term(4 + at)).astype(BF16)
+        first, second = self.slot(), self.slot()
+        copy = self.near(sums.at[0], ends.at[0])
+        self.locals += 1
+        beside = lambda: self.remote(sums.at[1], ends.at[0], CORE, first)
+        over = lambda: self.remote(sums.at[0], ends.at[1], DIAGONAL, second)
+        across = lambda: self.remote(sums.at[1], ends.at[1], CROSS, first, second)
+
+        def start_aligned():
+            copy.start()
+            beside().start()
+
+        def start_other():
+            over().start()
+            across().start()
+
+        def wait_aligned():
+            copy.wait()
+            beside().wait_send()
+            over().wait_recv()
+
+        def wait_other():
+            over().wait()
+            across().wait_send()
+            beside().wait_recv()
+
+        pl.when(self.aligned)(start_aligned)
+        pl.when(jnp.logical_not(self.aligned))(start_other)
+
+        def finish():
+            pl.when(self.aligned)(wait_aligned)
+            pl.when(jnp.logical_not(self.aligned))(wait_other)
+
+        return finish
+
+    def finish(self, pack, step):
+        finish = self.open.pop((pack, step), None)
+        if finish is not None:
+            finish()
+
+    def finish_all(self):
+        for finish in self.open.values():
+            finish()
+        self.open = {}
+
+
+PACK_PARTS = {
+    1: (PAIR,),
+    2: (LOW, HIGH),
+    3: (CORNER,),
+    4: (CORNERS,),
+    5: (FROM_LOW, FROM_HIGH),
+    6: (ENDS,),
+    7: (RESULT,),
+}
+PACK_NEEDS = {
+    1: (MINE,),
+    2: (PAIR,),
+    3: (LOW, HIGH),
+    4: (GRAD,),
+    5: (GRAD, CORNERS),
+    6: (GRAD, FROM_LOW, FROM_HIGH),
+    7: (ENDS,),
+}
+
+
+def pack_buffers(jobs, packs):
+    needs, makes, scratch = {}, {}, {}
+    for pack, step in jobs:
+        for part in PACK_NEEDS[step]:
+            name = (pack, part)
+            if name not in makes:
+                needs[name] = packs[name]
+        if step < 4:
+            depth, columns = packs[(pack, MINE)].shape
+        else:
+            depth, columns = packs[(pack, GRAD)].shape
+            depth //= 8
+            scratch[HELD, columns] = pltpu.VMEM((6, depth, columns), BF16)
+            if step in (5, 6):
+                scratch[SUMS, pack] = pltpu.VMEM((2, depth, columns), BF16)
+        for part in PACK_PARTS[step]:
+            made = jax.ShapeDtypeStruct((2, depth, columns), BF16)
+            if part == RESULT:
+                made = jax.ShapeDtypeStruct((depth, columns), F32)
+                scratch[RESULT, columns, pack] = pltpu.VMEM((depth, columns), F32)
+            makes[(pack, part)] = made
+    return needs, makes, scratch, 4 * len(jobs), 9 * len(jobs)
+
+
+def start_kernel(jobs, names, *refs):
+    ref = dict(zip(names, refs))
+    greeted = greet((CORE, LINE, CROSS, DIAGONAL, LOW, HIGH))
+    courier = Courier(ref)
+    greeted()
+    facts = courier.swap(ref[FACTS_HBM], ref[ROW_FACTS_HBM])
+    vector, vectors = ref[VECTOR_HBM], ref[VECTORS_HBM]
+    courier.local(vector, vectors.at[0]).wait()
+    rows = None
+    size = 1
+    for partner in (LINE, CROSS, CORE, LOW, HIGH):
+        courier.send(vectors.at[0:size], vectors.at[size : 2 * size], partner).wait()
+        size *= 2
+        if partner == CROSS:
+            courier.begin(*jobs[0])
+            rows = courier.swap(ref[HIDDEN_HBM], ref[MOVED_HBM])
+    for job in jobs[1:]:
+        courier.begin(*job)
+    rows()
+    facts()
+    courier.finish_all()
+
+
+def start_call(collective, hidden, facts, vector, jobs, packs):
+    anywhere = pl.BlockSpec(memory_space=pl.ANY)
+    needs, makes, _, remote, here = pack_buffers(jobs, packs)
+    shape = jax.ShapeDtypeStruct
+    inputs = {HIDDEN_HBM: hidden, FACTS_HBM: facts, VECTOR_HBM: vector, **needs}
+    outputs = {
+        MOVED_HBM: shape(hidden.shape, hidden.dtype),
+        ROW_FACTS_HBM: shape(facts.shape, facts.dtype),
+        VECTORS_HBM: shape((32, *vector.shape), vector.dtype),
+        **makes,
+    }
+    names = (*inputs, *outputs, REMOTE, HERE)
+    results = pl.pallas_call(
+        functools.partial(start_kernel, jobs, names),
+        name="start_exchange",
+        out_shape=tuple(outputs.values()),
+        in_specs=[anywhere] * len(inputs),
+        out_specs=(anywhere,) * len(outputs),
+        scratch_shapes=[
+            pltpu.SemaphoreType.DMA((2, remote + 7)),
+            pltpu.SemaphoreType.DMA((here + 3,)),
+        ],
+        compiler_params=pltpu.CompilerParams(collective_id=collective, has_side_effects=True),
+        cost_estimate=pl.CostEstimate(flops=0, bytes_accessed=64 << 20, transcendentals=0),
+    )(*inputs.values())
+    results = dict(zip(outputs, results))
+    packs.update({name: results[name] for name in makes})
+    return results
+
+
+def turned(values):
+    return values.astype(F32).T
+
+
+def joined(pieces, axis=0):
+    return pieces[0] if len(pieces) == 1 else jnp.concatenate(pieces, axis=axis)
+
+
+def chain_kernel(stages, backward, names, plan, jobs, *refs):
+    ref = dict(zip(names, refs))
+    enter, mix, leave = stages
+    value, state, own, far_own = ref[VALUE], ref[STATE], ref[OWN], ref[FAR_OWN]
+    count, width = value.shape
+    step = count // PARTS
+    greeted = greet(tuple(partners()) if jobs or MOVED_HBM in ref else (CORE, LINE))
+    courier = Courier(ref)
+    send, local = courier.send, courier.local
+    core, line = CORE, LINE
+    waiting = list(jobs)
+
+    def point(at):
+        while waiting and waiting[0][0] <= at:
+            courier.begin(*waiting.pop(0)[1:])
+
+    def chunk(slot, part):
+        return slice(slot * count + part * step, slot * count + (part + 1) * step)
+
+    def place(part):
+        return slice(part * step, (part + 1) * step)
+
+    made = {(pack, part): (pack, at) for _, pack, at in jobs for part in PACK_PARTS[at]}
+    loads = {}
+
+    def load(name, blocks):
+        return [
+            local(ref[piece].at[index, :, begin:end], ref[name].at[row : row + depth, :])
+            for piece, index, row, depth, begin, end in blocks
+        ]
+
+    for name, blocks in plan:
+        loads[name] = load(name, [block for block in blocks if block[0] not in made])
+
+    def loaded(name):
+        late = [block for weight, blocks in plan if weight == name for block in blocks]
+        late = [block for block in late if block[0] in made]
+        for block in late:
+            courier.finish(*made[block[0]])
+        for copy in loads[name] + load(name, late):
+            copy.wait()
+
+    if mix and backward:
+        loads[SLOPE] = [local(ref[SLOPE_HBM], ref[SLOPE])]
+    saves = []
+    if backward:
+        ref[WIDE_SUMS][...] = jnp.zeros(ref[WIDE_SUMS].shape, F32)
+
+    def add_wide(row, sums):
+        if sums.ndim == 1:
+            sums = sums[None]
+        ref[WIDE_SUMS][row : row + 1, :] += sums
+
+    def product(pieces, weight, stores, transposed_source=False):
+        def strip(at, carry):
+            columns = strips(at)
+            result = mat_turned(pieces, weight[columns, : pieces.shape[1]])
+            begin = 0
+            for size, store in stores:
+                store(columns, result[begin : begin + size])
+                begin += size
+            return carry
+
+        lax.fori_loop(0, width // STRIP, strip, 0)
+
+    def put(target, index):
+        def store(columns, result):
+            target[index, :, columns] = result.astype(target.dtype)
+
+        return store
+
+    def scatter(prefix, source, weight):
+        far_out, far_in = ref[prefix, FAR_OUT], ref[prefix, FAR_IN]
+        line_out, line_in = ref[prefix, LINE_OUT], ref[prefix, LINE_IN]
+        near_out, near_in = ref[prefix, NEAR_OUT], ref[prefix, NEAR_IN]
+
+        def far(part):
+            product(
+                source([(2, part), (3, part)]),
+                weight,
+                [(step, put(far_own, part)), (step, put(far_out, part))],
+            )
+            return send(far_out.at[part], far_in.at[part], core)
+
+        def pass_on(part, passing):
+            passing.wait()
+            line_out[part] = (far_own[part] + far_in[part].astype(F32)).astype(BF16)
+            return send(line_out.at[part], line_in.at[part], line)
+
+        def near():
+            product(
+                source([(1, part) for part in range(PARTS)]),
+                weight,
+                [(step, put(near_out, part)) for part in range(PARTS)],
+            )
+            return send(near_out, near_in, core)
+
+        def mine():
+            product(
+                source([(0, part) for part in range(PARTS)]),
+                weight,
+                [(step, put(own, part)) for part in range(PARTS)],
+            )
+
+        def total(part):
+            return own[part] + near_in[part].astype(F32) + line_in[part].astype(F32)
+
+        return far, pass_on, near, mine, total
+
+    def lower(values, gain, shift):
+        if backward:
+            return values.astype(BF16)
+        return (normalise(values)[0] * gain[...] + shift[...]).astype(BF16)
+
+    def begin_rows(rows, part):
+        near = send(rows.at[chunk(0, part)], rows.at[chunk(1, part)], core)
+        far = send(rows.at[chunk(0, part)], rows.at[chunk(2, part)], line)
+        return near, far
+
+    def forward_rows(rows, part, far):
+        far.wait()
+        return send(rows.at[chunk(2, part)], rows.at[chunk(3, part)], core)
+
+    ready = None
+    if enter:
+        source_t = ref[SOURCE]
+
+        def entering(pieces):
+            return turned(joined([source_t[:, chunk(*piece)] for piece in pieces], 1)).astype(BF16)
+
+        far, pass_on, near, mine, total = scatter(ENTER, entering, ref[ENTER_W])
+        loaded(ENTER_W)
+        greeted()
+        point(0)
+        if COTANGENT_HBM in ref:
+            moved = courier.swap(ref[COTANGENT_HBM], ref[MOVED_HBM])
+        passing = [far(part) for part in range(PARTS)]
+        lines = [pass_on(part, passing[part]) for part in range(PARTS)]
+        near_sum = near()
+        mine()
+        point(1)
+        near_sum.wait()
+        point(2)
+
+        def ready(part):
+            lines[part].wait()
+            at = place(part)
+            if backward:
+                grad, gains, shifts = norm_backward(
+                    ref[ENTER_AT][at, :], ref[ENTER_GAIN][...], total(part)
+                )
+                state[at, :] = value[at, :] + grad
+                add_wide(0, gains)
+                add_wide(1, shifts)
+            else:
+                state[at, :] = value[at, :] + (total(part) + ref[ENTER_BIAS][...])
+            ref[ENTERED][at, :] = state[at, :]
+
+    else:
+        greeted()
+        point(0)
+
+        if COTANGENT in ref:
+            lowered = mat(value[...].astype(BF16), ref[REORDER][...])
+            ref[ROWS_OUT][...] = lowered.astype(BF16)
+            moved = courier.swap(ref[ROWS_OUT], ref[MOVED_HBM])
+            state[...] = mat(ref[COTANGENT][...], ref[REORDER][...])
+
+        def ready(part):
+            at = place(part)
+            if COTANGENT not in ref:
+                state[at, :] = value[at, :]
+
+    if mix:
+        rows, act, slope = ref[ROWS], ref[ACT], ref[SLOPE]
+        first, second = ref[FIRST], ref[SECOND]
+        units = first.shape[1]
+        if backward:
+            ref[UNIT_SUMS][...] = jnp.zeros(ref[UNIT_SUMS].shape, F32)
+        begun = []
+        for part in range(PARTS):
+            ready(part)
+            lowered = lower(
+                state[place(part), :], ref.get(MIX_GAIN), ref.get(MIX_SHIFT)
+            )
+            rows[chunk(0, part), :] = lowered
+            begun.append(begin_rows(rows, part))
+            if backward:
+                add_wide(2, jnp.sum(lowered.astype(F32), axis=0))
+
+        def expand(pieces):
+            taken = joined([rows[chunk(*piece), :] for piece in pieces])
+
+            def strip(at, carry):
+                columns = strips(at)
+                up = mat(taken, first[:, columns])
+                tilt = None
+                if backward:
+                    slopes = joined([slope[chunk(*piece), columns] for piece in pieces])
+                    out = (up * slopes.astype(F32)).astype(BF16)
+                    ref[UNIT_SUMS][:, columns] += jnp.sum(
+                        out.astype(F32), axis=0, keepdims=True
+                    )
+                else:
+                    up = up + ref[FIRST_BIAS][:, columns]
+                    sigmoid = 1.0 / (1.0 + jnp.exp(-1.702 * up))
+                    out = (up * sigmoid).astype(BF16)
+                    tilt = (sigmoid + 1.702 * up * sigmoid * (1.0 - sigmoid)).astype(BF16)
+                for index, piece in enumerate(pieces):
+                    at_rows = slice(index * step, (index + 1) * step)
+                    act[chunk(*piece), columns] = out[at_rows]
+                    if tilt is not None:
+                        slope[chunk(*piece), columns] = tilt[at_rows]
+                return carry
+
+            lax.fori_loop(0, units // STRIP, strip, 0)
+
+        def acting(pieces):
+            return joined([act[chunk(*piece), :] for piece in pieces])
+
+        far, pass_on, near, mine, total = scatter(MIX, acting, second)
+        loaded(FIRST)
+        if backward:
+            loaded(SLOPE)
+        expand([(0, part) for part in range(PARTS)])
+        for part in range(PARTS):
+            begun[part][0].wait()
+        point(3)
+        expand([(1, part) for part in range(PARTS)])
+        loaded(SECOND)
+        near_sum = near()
+        point(4)
+        forwards = [forward_rows(rows, 0, begun[0][1])]
+        mine()
+        lines = []
+        for part in range(PARTS):
+            forwards[part].wait()
+            expand([(2, part), (3, part)])
+            lines.append(pass_on(part, far(part)))
+            if part + 1 < PARTS:
+                forwards.append(forward_rows(rows, part + 1, begun[part + 1][1]))
+            point(5 + part)
+        saves.append(local(rows, ref[ROWS_HBM]))
+        saves.append(local(act, ref[ACT_HBM]))
+        if not backward:
+            saves.append(local(slope, ref[SLOPE_HBM]))
+        near_sum.wait()
+
+        def ready(part):
+            lines[part].wait()
+            at = place(part)
+            if backward:
+                grad, gains, shifts = norm_backward(
+                    ref[MIX_AT][at, :], ref[MIX_GAIN][...], total(part)
+                )
+                state[at, :] = state[at, :] + grad
+                add_wide(3, gains)
+                add_wide(4, shifts)
+            else:
+                state[at, :] = state[at, :] + (total(part) + ref[SECOND_BIAS][...])
+            ref[MIXED][at, :] = state[at, :]
+
+    if leave:
+        rows2, weight, target = ref[ROWS2], ref[LEAVE_W], ref[TARGET]
+        begun = []
+        for part in range(PARTS):
+            ready(part)
+            lowered = lower(
+                state[place(part), :], ref.get(LEAVE_GAIN), ref.get(LEAVE_SHIFT)
+            )
+            rows2[chunk(0, part), :] = lowered
+            begun.append(begin_rows(rows2, part))
+            if backward:
+                add_wide(5, jnp.sum(lowered.astype(F32), axis=0))
+
+        def leaving(pieces):
+            result = mat(joined([rows2[chunk(*piece), :] for piece in pieces]), weight[...])
+            if not backward:
+                result = result + ref[LEAVE_BIAS][...]
+            result = turned(result)
+            if not backward:
+                cos, sin = (
+                    joined([ref[name][:, chunk(*piece)] for piece in pieces], 1)
+                    for name in (COSINE, SINE)
+                )
+                half, third = HD // 2, result.shape[0] // 3
+                blocks = []
+                for base in range(0, 2 * third, HD):
+                    low, high = result[base : base + half], result[base + half : base + HD]
+                    blocks += [low * cos - high * sin, high * cos + low * sin]
+                result = jnp.concatenate(blocks + [result[2 * third :]], axis=0)
+            result = result.astype(BF16)
+            for index, piece in enumerate(pieces):
+                target[:, chunk(*piece)] = result[:, index * step : (index + 1) * step]
+
+        loaded(LEAVE_W)
+        point(7)
+        leaving([(0, part) for part in range(PARTS)])
+        for part in range(PARTS):
+            begun[part][0].wait()
+        leaving([(1, part) for part in range(PARTS)])
+        point(8)
+        forwards = [forward_rows(rows2, part, begun[part][1]) for part in range(PARTS)]
+        for part in range(PARTS):
+            forwards[part].wait()
+            leaving([(2, part), (3, part)])
+        saves.append(local(rows2, ref[ROWS2_HBM]))
+    else:
+        for part in range(PARTS):
+            ready(part)
+    if REORDER in ref and COTANGENT not in ref:
+        lowered = mat(state[...].astype(BF16), ref[REORDER][...]).astype(BF16)
+        rows_out = ref[ROWS_OUT]
+        rows_out[...] = lowered
+        moved = courier.swap(rows_out, ref[MOVED_HBM])
+    point(9)
+    if MOVED_HBM in ref:
+        moved()
+    for save in saves:
+        save.wait()
+    courier.finish_all()
+
+
+class Weight:
+    def __init__(self, pack, begin, end):
+        self.pack, self.begin, self.end = pack, begin, end
+
+
+def chain_call(stages, backward, collective, operands, packs, jobs=()):
+    enter, mix, leave = stages
+    count, width = operands[VALUE].shape
+    step = count // PARTS
+    shape = jax.ShapeDtypeStruct
+    vmem, anywhere = pl.BlockSpec(memory_space=pltpu.VMEM), pl.BlockSpec(memory_space=pl.ANY)
+    outputs, scratch = {}, {}
+    buffers = lambda kind: pltpu.VMEM((PARTS, step, width), kind)
+    scratch[STATE] = pltpu.VMEM((count, width), F32)
+    scratch[OWN] = buffers(F32)
+    scratch[FAR_OWN] = buffers(F32)
+    remote, here = 0, 0
+    if backward:
+        outputs[WIDE_SUMS] = shape((8, width), F32)
+    flops = 0
+    plan = []
+    passed = {}
+    needs, makes, job_scratch, job_remote, job_here = pack_buffers([job[1:] for job in jobs], packs)
+    scratch.update(job_scratch)
+    remote, here = remote + job_remote, here + job_here
+    for name, value in operands.items():
+        if not isinstance(value, Weight):
+            passed[name] = value
+            continue
+        blocks, row = [], 0
+        for part in (PAIR, LOW, HIGH, CORNER, ALL):
+            piece = (value.pack, part)
+            if piece not in packs and piece not in makes:
+                continue
+            if piece not in makes:
+                passed[piece] = packs[piece]
+            array = makes.get(piece, packs.get(piece))
+            for index in range(array.shape[0]):
+                blocks.append((piece, index, row, array.shape[1], value.begin, value.end))
+                row += array.shape[1]
+        plan.append((name, blocks))
+        scratch[name] = pltpu.VMEM((width, value.end - value.begin), BF16)
+        here += len(blocks)
+        flops += 8 * count * width * (value.end - value.begin)
+    passed.update({name: value for name, value in needs.items() if name not in passed})
+    outputs.update(makes)
+    for stage, prefix in ((enter, ENTER), (mix, MIX)):
+        if stage:
+            for name in (FAR_OUT, FAR_IN, LINE_OUT, LINE_IN, NEAR_OUT, NEAR_IN):
+                scratch[prefix, name] = buffers(BF16)
+            remote += 2 * PARTS + 1
+    if enter:
+        outputs[ENTERED] = shape((count, width), F32)
+    if mix:
+        units = operands[FIRST].end - operands[FIRST].begin
+        scratch[ROWS] = pltpu.VMEM((4 * count, width), BF16)
+        scratch[ACT] = pltpu.VMEM((4 * count, units), BF16)
+        scratch[SLOPE] = pltpu.VMEM((4 * count, units), BF16)
+        outputs[MIXED] = shape((count, width), F32)
+        outputs[ROWS_HBM] = shape((4 * count, width), BF16)
+        outputs[ACT_HBM] = shape((4 * count, units), BF16)
+        if backward:
+            outputs[UNIT_SUMS] = shape((1, units), F32)
+        else:
+            outputs[SLOPE_HBM] = shape((4 * count, units), BF16)
+        remote += 3 * PARTS
+        here += 3
+    if leave:
+        columns = leave
+        scratch[ROWS2] = pltpu.VMEM((4 * count, width), BF16)
+        outputs[TARGET] = shape((columns, 4 * count), BF16)
+        outputs[ROWS2_HBM] = shape((4 * count, width), BF16)
+        remote += 3 * PARTS
+        here += 1
+    if REORDER in operands or COTANGENT_HBM in operands:
+        if REORDER in operands:
+            scratch[ROWS_OUT] = pltpu.VMEM((count, width), BF16)
+        outputs[MOVED_HBM] = shape((count, width), BF16)
+        remote, here = remote + 1, here + 1
+    scratch[REMOTE] = pltpu.SemaphoreType.DMA((2, remote))
+    scratch[HERE] = pltpu.SemaphoreType.DMA((here,))
+    names = tuple(passed) + tuple(outputs) + tuple(scratch)
+    spec = lambda name: anywhere if isinstance(name, tuple) or name >= FIRST_HBM else vmem
+    results = pl.pallas_call(
+        functools.partial(chain_kernel, stages, backward, names, plan, jobs),
+        name="chain_backward" if backward else "chain_forward",
+        out_shape=tuple(outputs.values()),
+        in_specs=[spec(name) for name in passed],
+        out_specs=tuple(spec(name) for name in outputs),
+        scratch_shapes=list(scratch.values()),
+        compiler_params=pltpu.CompilerParams(
+            collective_id=collective, has_side_effects=True, vmem_limit_bytes=54 << 20
+        ),
+        cost_estimate=pl.CostEstimate(
+            flops=flops, bytes_accessed=(16 << 20) * sum(map(bool, stages)), transcendentals=0
+        ),
+    )(*passed.values())
+    results = dict(zip(outputs, results))
+    packs.update({name: results[name] for name in makes})
+    return results
+
+
 def make_body(dp, mp):
     assert mp == 4 and dp >= 2 and dp & (dp - 1) == 0
     count = dp * mp
@@ -256,55 +1027,45 @@
     def swapped(d, m):
         return (d & ~1 | m >> 1) * mp + ((d & 1) << 1 | m & 1)
 
-    swap_pairs = [(d * mp + m, swapped(d, m)) for d in range(dp) for m in range(mp)]
+    swap_pairs = [
+        (d * mp + m, swapped(d, m)) for d in range(dp) for m in range(mp) if d & 1 != m >> 1
+    ]
 
     def swap(value):
-        return lax.ppermute(value, ("dp", "mp"), swap_pairs)
-
-    def gather_blocks(mine):
-        pair = swap(jnp.stack([mine, core_side(mine)]))
-        if len(high_bits) == 2:
-            low, high = high_bits
-            by_low, by_high = across(pair, low), across(pair, high)
-            pieces = [pair, by_low, by_high, across(by_low[:1], high), across(by_high[1:], low)]
-        else:
-            pieces = [pair]
-            for bit in high_bits:
-                pieces = pieces + [across(piece, bit) for piece in pieces]
-        return [
-            jnp.concatenate([piece[:, g] for piece in pieces], axis=0).reshape(D, mine.shape[-1])
-            for g in range(mine.shape[0])
-        ]
-
-    def scatter_blocks(grads):
-        blocks = [grad.reshape(dp, D // dp, grad.shape[-1]) for grad in grads]
-
-        def pick(begin, end):
-            return jnp.stack([block[begin:end] for block in blocks], axis=1)
-
-        def add(*terms):
-            total = terms[0].astype(F32)
-            for term in terms[1:]:
-                total = total + term.astype(F32)
-            return total.astype(BF16)
-
-        if len(high_bits) == 2:
-            low, high = high_bits
-            first = across(pick(6, 7), high)
-            second = across(pick(7, 8), low)
-            by_low = jnp.concatenate([add(pick(2, 3), first), pick(3, 4)], axis=0)
-            by_high = jnp.concatenate([pick(4, 5), add(pick(5, 6), second)], axis=0)
-            total = add(pick(0, 2), across(by_low, low), across(by_high, high))
-        else:
-            total = pick(0, dp)
-            for bit in high_bits[::-1]:
-                half = total.shape[0] // 2
-                total = add(total[:half], across(total[half:], bit))
+        stays = (lax.axis_index("dp") & 1) == (lax.axis_index("mp") >> 1)
+        return jnp.where(stays, value, lax.ppermute(value, ("dp", "mp"), swap_pairs))
+
+    balanced = len(high_bits) == 2
+
+    def gather_pair(mine):
+        return swap(jnp.stack([mine, core_side(mine)]))
+
+    def gather_sides(pair):
+        for bit in high_bits:
+            pair = jnp.concatenate([pair, across(pair, bit)], axis=0)
+        return (pair,)
+
+    def add(*terms):
+        total = terms[0].astype(F32)
+        for term in terms[1:]:
+            total = total + term.astype(F32)
+        return total.astype(BF16)
+
+    def scatter_blocks(grad):
+        total = grad.reshape(dp, D // dp, -1)
+        for bit in high_bits[::-1]:
+            half = total.shape[0] // 2
+            total = add(total[:half], across(total[half:], bit))
         total = swap(total)
         return total[0].astype(F32) + core_side(total[1]).astype(F32)
 
+    def arranged(values):
+        index = lax.axis_index("dp") * mp + lax.axis_index("mp")
+        at = jnp.arange(count, dtype=jnp.int32)
+        order = (at[:, None] ^ index) == at[None, :]
+        return dot(order.astype(F32), values, 1, 0, precision=HIGHEST)
+
     def gather_vectors(mine):
-        index = lax.axis_index("dp") * mp + lax.axis_index("mp")
         values = mine[None]
         bit = 1
         while bit < count:
@@ -314,9 +1075,7 @@
                 got = lax.ppermute(values, "mp", [(i, i ^ bit) for i in range(mp)])
             values = jnp.concatenate([values, got], axis=0)
             bit *= 2
-        at = jnp.arange(count, dtype=jnp.int32)
-        order = (at[:, None] ^ index) == at[None, :]
-        return dot(order.astype(F32), values, 1, 0, precision=HIGHEST)
+        return arranged(values)
 
     def scatter_vectors(values):
         index = lax.axis_index("dp") * mp + lax.axis_index("mp")
@@ -333,17 +1092,6 @@
             values = jnp.where(top, high, low) + got
             bit //= 2
         return values[0]
-
-    def gather_rows(mine):
-        near = core_side(mine)
-        far = line_side(mine)
-        return [mine, near, far, core_side(far)]
-
-    def scatter_rows(part):
-        far = part(2) + core_side(part(3).astype(BF16)).astype(F32)
-        far = line_side(far.astype(BF16))
-        near = part(0) + core_side(part(1).astype(BF16)).astype(F32)
-        return near + far.astype(F32)
 
     def body(
         hidden_in,
@@ -381,37 +1129,86 @@
         def turn_low(values):
             return dot(values.astype(BF16), reorder_low, 1, 0)
 
-        hidden = turn_low(swap(hidden_in.astype(BF16)))
         qkv_width, proj_width = 3 * columns, columns
-        qkv_space, proj_space = -(-qkv_width // 128) * 128, -(-proj_width // 128) * 128
-
-        def pack_attention(for_qkv, for_proj):
-            return jnp.concatenate(
-                [
-                    jnp.pad(for_qkv, ((0, 0), (0, qkv_space - qkv_width))),
-                    jnp.pad(for_proj, ((0, 0), (0, proj_space - proj_width))),
-                ],
-                axis=1,
-            )
-
-        def unpack_attention(packed):
-            return packed[:, :qkv_width], packed[:, qkv_space : qkv_space + proj_width]
-
-        weights = []
+        packs = {}
         for layer in range(LAYERS):
-            mine = pack_attention(
-                qkv_weight[layer].transpose(1, 0, 2).reshape(depth, qkv_width),
-                proj_weight[layer].T,
-            )
-            w_qkv, w_proj = unpack_attention(gather_blocks(mine[None])[0])
-            w_up, w_down = gather_blocks(jnp.stack([up_weight[layer], down_weight[layer].T]))
-            weights.append((w_qkv, w_proj, w_up, w_down))
+            mine = qkv_weight[layer].transpose(1, 0, 2).reshape(depth, qkv_width)
+            packs[(QKV, layer), MINE] = mine
+            packs[(PROJ, layer), MINE] = proj_weight[layer].T
+            packs[(UP, layer), MINE] = up_weight[layer]
+            packs[(DOWN, layer), MINE] = down_weight[layer].T
 
         wide = (pre_gain, pre_bias, proj_bias, mid_gain, mid_bias, down_bias)
         packed = jnp.concatenate(
             [item.reshape(-1) for item in wide] + [qkv_bias.reshape(-1), up_bias.reshape(-1)]
         )
-        packed = gather_vectors(packed)
+        length = picture_ids.shape[0]
+        quarter = length // mp
+        row_at = jnp.arange(length, dtype=jnp.int32)
+        codes = jnp.where(pad_mask == 1, picture_ids, 1024 + row_at)
+        row_facts = jnp.concatenate([codes[None], positions], axis=0)
+        hidden = hidden_in.astype(BF16)
+        jobs = {}
+        if balanced:
+            space = -(-packed.shape[0] // 1024) * 1024
+            begun = start_call(
+                3 * LAYERS + 1,
+                hidden,
+                jnp.pad(row_facts, ((0, 5), (0, 0))),
+                jnp.pad(packed, (0, space - packed.shape[0])).reshape(-1, 128),
+                (((QKV, 0), 1), ((QKV, 0), 2), ((PROJ, 0), 1), ((UP, 0), 1), ((QKV, 0), 3)),
+                packs,
+            )
+            hidden, row_facts = begun[MOVED_HBM], begun[ROW_FACTS_HBM][:3]
+            packed = arranged(begun[VECTORS_HBM].reshape(count, space))[:, : packed.shape[0]]
+            schedule = {
+                (LEAVE, 0): {
+                    0: ((UP, 0, 2), (PROJ, 0, 2), (DOWN, 0, 1)),
+                    8: ((PROJ, 0, 3),),
+                },
+                (FORWARD, 0): {
+                    0: ((UP, 0, 3), (DOWN, 0, 2)),
+                    2: ((QKV, 1, 1), (PROJ, 1, 1)),
+                    3: ((DOWN, 0, 3),),
+                    4: ((UP, 1, 1), (QKV, 1, 2)),
+                    6: ((QKV, 1, 3), (UP, 1, 2)),
+                },
+                (LEAVE, 1): {
+                    0: ((UP, 1, 3), (PROJ, 1, 2), (DOWN, 1, 1)),
+                    8: ((PROJ, 1, 3),),
+                },
+                (FORWARD, 1): {0: ((DOWN, 1, 2),), 2: ((DOWN, 1, 3),)},
+                (BACKWARD, 0): {
+                    0: ((UP, 1, 4), (DOWN, 1, 4)),
+                    1: ((UP, 1, 5),),
+                    4: ((DOWN, 1, 5), (QKV, 1, 4), (PROJ, 1, 4)),
+                    5: ((UP, 1, 6),),
+                    8: ((DOWN, 1, 6), (QKV, 1, 5), (PROJ, 1, 5)),
+                },
+                (BACKWARD, FINAL): {
+                    0: ((UP, 0, 4), (DOWN, 0, 4), (QKV, 1, 6), (PROJ, 1, 6)),
+                    1: ((UP, 0, 5),),
+                    9: (
+                        *((QKV, 0, 4), (PROJ, 0, 4), (DOWN, 0, 5), (UP, 1, 7), (DOWN, 1, 7)),
+                        *((UP, 0, 6), (QKV, 0, 5), (PROJ, 0, 5), (QKV, 1, 7), (PROJ, 1, 7)),
+                        *((DOWN, 0, 6), (UP, 0, 7), (QKV, 0, 6), (PROJ, 0, 6)),
+                        *((DOWN, 0, 7), (QKV, 0, 7), (PROJ, 0, 7)),
+                    ),
+                },
+            }
+            jobs = {
+                kernel: tuple(
+                    (at, (name, layer), step)
+                    for at, steps in points.items()
+                    for name, layer, step in steps
+                )
+                for kernel, points in schedule.items()
+            }
+        else:
+            for name in list(packs):
+                packs[name[0], ALL] = gather_sides(gather_pair(packs[name]))[0].reshape(1, D, -1)
+            hidden, row_facts, packed = swap(hidden), swap(row_facts), gather_vectors(packed)
+        hidden = turn_low(hidden)
         each = D // count
         wide_count = len(wide) * LAYERS
         split = (wide_count + 3 * LAYERS) * each
@@ -429,11 +1226,6 @@
             up_all.reshape(LAYERS, -1), quarter_at * units, units, 1
         )
 
-        length = picture_ids.shape[0]
-        quarter = length // mp
-        row_at = jnp.arange(length, dtype=jnp.int32)
-        codes = jnp.where(pad_mask == 1, picture_ids, 1024 + row_at)
-        row_facts = swap(jnp.concatenate([codes[None], positions], axis=0))
         row_facts = jnp.concatenate(
             [
                 lax.dynamic_slice_in_dim(row_facts, (quarter_at ^ which) * quarter, quarter, 1)
@@ -444,109 +1236,182 @@
         codes = row_facts[0]
         facts = (tile_overlap(codes), *rotary_tables(row_facts[1:]), codes[None], codes[:, None])
 
-        kept = []
-        for layer in range(LAYERS):
-            w_qkv, w_proj, w_up, w_down = weights[layer]
-            start = hidden
-            normed = normalise(hidden)[0] * pre_gain_all[layer] + pre_bias_all[layer]
-            rows = gather_rows(normed.astype(BF16))
-            attn_rows = jnp.concatenate(rows, axis=0)
-            linear = dot(w_qkv, attn_rows, 0, 1) + qkv_bias_mine[layer][:, None]
-            qkv, mixed, log_sum = attend_forward(linear, facts)
-            attended = scatter_rows(
-                lambda i, a=mixed, w=w_proj: dot(a[:, i * quarter : (i + 1) * quarter], w, 0, 1)
+        row = lambda vector: vector[None]
+        weights = [
+            (
+                Weight((QKV, layer), 0, qkv_width),
+                Weight((PROJ, layer), 0, proj_width),
+                Weight((UP, layer), 0, units),
+                Weight((DOWN, layer), 0, units),
             )
-            middle = hidden + (attended + proj_bias_all[layer])
-            normed = normalise(middle)[0] * mid_gain_all[layer] + mid_bias_all[layer]
-            rows = gather_rows(normed.astype(BF16))
-            mid_rows = jnp.concatenate(rows, axis=0)
-            upward = dot(mid_rows, w_up, 1, 0) + up_bias_mine[layer]
-            sigmoid = 1.0 / (1.0 + jnp.exp(-1.702 * upward))
-            active = (upward * sigmoid).astype(BF16)
-            slope = (sigmoid + 1.702 * upward * sigmoid * (1.0 - sigmoid)).astype(BF16)
-            output = scatter_rows(
-                lambda i, a=active, w=w_down: dot(a[i * quarter : (i + 1) * quarter], w, 1, 1)
+            for layer in range(LAYERS)
+        ]
+
+        def leave_forward(layer):
+            return {
+                LEAVE_W: weights[layer][0],
+                LEAVE_GAIN: row(pre_gain_all[layer]),
+                LEAVE_SHIFT: row(pre_bias_all[layer]),
+                LEAVE_BIAS: row(qkv_bias_mine[layer]),
+                COSINE: facts[1],
+                SINE: facts[2],
+            }
+
+        def call_leave(layer, value):
+            return chain_call(
+                (False, False, qkv_width),
+                False,
+                layer,
+                {VALUE: value, **leave_forward(layer)},
+                packs,
+                jobs.get((LEAVE, layer), ()),
             )
-            hidden = middle + (output + down_bias_all[layer])
-            kept.append((start, attn_rows, qkv, mixed, log_sum, middle, mid_rows, active, slope))
-
-        out_hidden = swap(turn_low(hidden).astype(BF16)).astype(F32)
-        gradient = turn_low(swap(cotangent.astype(BF16)))
-        grads = []
-        parts = []
-        for layer in reversed(range(LAYERS)):
-            w_qkv, w_proj, w_up, w_down = weights[layer]
-            start, attn_rows, qkv, mixed, log_sum, middle, mid_rows, active, slope = kept[layer]
-            grad_out = gradient.astype(BF16)
-            down_bias_part = jnp.sum(grad_out.astype(F32), axis=0)
-            grad_rows = jnp.concatenate(gather_rows(grad_out), axis=0)
-            grad_up = (dot(grad_rows, w_down, 1, 0) * slope.astype(F32)).astype(BF16)
-            grad_normed = scatter_rows(
-                lambda i, a=grad_up, w=w_up: dot(a[i * quarter : (i + 1) * quarter], w, 1, 1)
+
+        def call_forward(layer, value, mixed, more):
+            return chain_call(
+                (True, True, False),
+                False,
+                LAYERS + layer,
+                {
+                    VALUE: value,
+                    SOURCE: mixed,
+                    ENTER_W: weights[layer][1],
+                    ENTER_BIAS: row(proj_bias_all[layer]),
+                    FIRST: weights[layer][2],
+                    SECOND: weights[layer][3],
+                    FIRST_BIAS: row(up_bias_mine[layer]),
+                    SECOND_BIAS: row(down_bias_all[layer]),
+                    MIX_GAIN: row(mid_gain_all[layer]),
+                    MIX_SHIFT: row(mid_bias_all[layer]),
+                    **more,
+                },
+                packs,
+                jobs.get((FORWARD, layer), ()),
             )
-            down_grad = dot(grad_rows, active, 0, 0, BF16)
-            up_bias_part = jnp.sum(grad_up.astype(F32), axis=0)
-            up_grad = dot(mid_rows, grad_up, 0, 0, BF16)
-            ffn_grads = scatter_blocks([up_grad, down_grad])
-            grad_middle, mid_gain_part, mid_bias_part = norm_backward(
-                middle, mid_gain_all[layer], grad_normed
+
+        def call_backward(layer, value, entering, middle, slope, more):
+            return chain_call(
+                (bool(entering), True, proj_width),
+                True,
+                2 * LAYERS + layer,
+                {
+                    VALUE: value,
+                    **entering,
+                    **more,
+                    FIRST: weights[layer][3],
+                    SECOND: weights[layer][2],
+                    SLOPE_HBM: slope,
+                    MIX_AT: middle,
+                    MIX_GAIN: row(mid_gain_all[layer]),
+                    LEAVE_W: weights[layer][1],
+                },
+                packs,
+                jobs.get((BACKWARD, layer), ()),
             )
-            gradient = gradient + grad_middle
-            grad_out = gradient.astype(BF16)
-            proj_bias_part = jnp.sum(grad_out.astype(F32), axis=0)
-            grad_rows = jnp.concatenate(gather_rows(grad_out), axis=0)
-            grad_mixed = dot(w_proj, grad_rows, 0, 1, BF16)
-            proj_grad = dot(grad_rows, mixed, 0, 1, BF16)
-            grad_linear = attend_backward(qkv, mixed, grad_mixed, log_sum, facts)
-            grad_normed = scatter_rows(
-                lambda i, a=grad_linear, w=w_qkv: dot(
-                    a[:, i * quarter : (i + 1) * quarter], w, 0, 1
+
+        def entering(layer, grad_linear, start):
+            return {
+                SOURCE: grad_linear,
+                ENTER_W: weights[layer][0],
+                ENTER_AT: start,
+                ENTER_GAIN: row(pre_gain_all[layer]),
+            }
+
+        leave0 = call_leave(0, hidden)
+        qkv0 = leave0[TARGET]
+        mixed0, log_sum0 = attend_forward(qkv0, facts)
+        state0 = call_forward(0, hidden, mixed0, {})
+        start1 = state0[MIXED]
+        leave1 = call_leave(1, start1)
+        qkv1 = leave1[TARGET]
+        mixed1, log_sum1 = attend_forward(qkv1, facts)
+        cotangent = cotangent.astype(BF16)
+        if balanced:
+            state1 = call_forward(1, start1, mixed1, {COTANGENT_HBM: cotangent})
+            back1 = call_backward(
+                1,
+                state1[MIXED],
+                {},
+                state1[ENTERED],
+                state1[SLOPE_HBM],
+                {COTANGENT: state1[MOVED_HBM], REORDER: reorder_low},
+            )
+            out_hidden = back1[MOVED_HBM]
+        else:
+            state1 = call_forward(1, start1, mixed1, {})
+            out_hidden = swap(turn_low(state1[MIXED]).astype(BF16))
+            gradient = turn_low(swap(cotangent))
+            back1 = call_backward(1, gradient, {}, state1[ENTERED], state1[SLOPE_HBM], {})
+        packs[(UP, 1), GRAD] = dot(state1[ROWS_HBM], back1[ACT_HBM], 0, 0, BF16)
+        packs[(DOWN, 1), GRAD] = dot(back1[ROWS_HBM], state1[ACT_HBM], 0, 0, BF16)
+        linear1 = attend_backward(qkv1, mixed1, back1[TARGET], log_sum1, facts)
+        packs[(QKV, 1), GRAD] = dot(leave1[ROWS2_HBM], linear1, 0, 1, BF16)
+        packs[(PROJ, 1), GRAD] = dot(back1[ROWS2_HBM], mixed1, 0, 1, BF16)
+        back0 = call_backward(
+            0,
+            back1[MIXED],
+            entering(1, linear1, start1),
+            state0[ENTERED],
+            state0[SLOPE_HBM],
+            {},
+        )
+        packs[(UP, 0), GRAD] = dot(state0[ROWS_HBM], back0[ACT_HBM], 0, 0, BF16)
+        packs[(DOWN, 0), GRAD] = dot(back0[ROWS_HBM], state0[ACT_HBM], 0, 0, BF16)
+        linear0 = attend_backward(qkv0, mixed0, back0[TARGET], log_sum0, facts)
+        packs[(QKV, 0), GRAD] = dot(leave0[ROWS2_HBM], linear0, 0, 1, BF16)
+        packs[(PROJ, 0), GRAD] = dot(back0[ROWS2_HBM], mixed0, 0, 1, BF16)
+        final = chain_call(
+            (True, False, False),
+            True,
+            3 * LAYERS,
+            {
+                VALUE: back0[MIXED],
+                **entering(0, linear0, hidden),
+                **({REORDER: reorder_low} if balanced else {}),
+            },
+            packs,
+            jobs.get((BACKWARD, FINAL), ()),
+        )
+        if balanced:
+            grad_hidden = final[MOVED_HBM].astype(F32)
+        else:
+            grad_hidden = swap(turn_low(final[ENTERED]).astype(BF16)).astype(F32)
+            for name in list(packs):
+                if name[1] == GRAD:
+                    packs[name[0], RESULT] = scatter_blocks(packs[name])
+        out_hidden = out_hidden.astype(F32)
+        grads, parts = [], []
+        for layer, back, linear in ((0, back0, linear0), (1, back1, linear1)):
+            result = lambda which: packs[(which, layer), RESULT]
+            grads.append(
+                (
+                    result(QKV).reshape(depth, 3, columns).transpose(1, 0, 2),
+                    result(PROJ).T,
+                    result(UP),
+                    result(DOWN).T,
                 )
             )
-            qkv_bias_part = jnp.sum(grad_linear.astype(F32), axis=1)
-            qkv_grad = dot(attn_rows, grad_linear, 0, 1, BF16)
-            attn_grads = scatter_blocks([pack_attention(qkv_grad, proj_grad)])[0]
-            qkv_grad, proj_grad = unpack_attention(attn_grads)
-            grad_start, pre_gain_part, pre_bias_part = norm_backward(
-                start, pre_gain_all[layer], grad_normed
-            )
-            gradient = gradient + grad_start
-            grads.append(
-                (
-                    qkv_grad.reshape(depth, 3, columns).transpose(1, 0, 2),
-                    proj_grad.T,
-                    ffn_grads[0],
-                    ffn_grads[1].T,
-                )
-            )
-            parts.append(
-                (
-                    (
-                        pre_gain_part,
-                        pre_bias_part,
-                        proj_bias_part,
-                        mid_gain_part,
-                        mid_bias_part,
-                        down_bias_part,
-                    ),
-                    qkv_bias_part.reshape(3, columns),
-                    up_bias_part,
-                )
-            )
-        grads, parts = grads[::-1], parts[::-1]
-        grad_hidden = swap(turn_low(gradient).astype(BF16)).astype(F32)
-
-        stacked = jnp.stack([part[0][i] for i in range(len(wide)) for part in parts])
+            qkv_bias_part = jnp.sum(linear.astype(F32), axis=1)
+            parts.append((qkv_bias_part.reshape(3, columns), back[UNIT_SUMS][0]))
+        sums = [back1[WIDE_SUMS], back0[WIDE_SUMS], final[WIDE_SUMS]]
+
+        stacked = jnp.stack(
+            [
+                sums[LAYERS - layer - which][at]
+                for which, at in ((0, 0), (0, 1), (1, 5), (1, 3), (1, 4), (1, 2))
+                for layer in range(LAYERS)
+            ]
+        )
         stacked = dot(stacked, reorder_full, 1, 0, precision=HIGHEST)
         qkv_padded = lax.dynamic_update_slice_in_dim(
             jnp.zeros((LAYERS * 3, D), F32),
-            jnp.concatenate([part[1] for part in parts], axis=0),
+            jnp.concatenate([part[0] for part in parts], axis=0),
             quarter_at * columns,
             1,
         )
         up_padded = lax.dynamic_update_slice_in_dim(
             jnp.zeros((LAYERS, units * mp), F32),
-            jnp.stack([part[2] for part in parts]),
+            jnp.stack([part[1] for part in parts]),
             quarter_at * units,
             1,
         )

time: 821 us -> 765 us (0.932)
  Pallas kernels: 53.9 us -> 646 us
  waiting for transfers between devices: 301 us -> 6.84 us
  starting transfers between devices: 183 us -> 2.26 us
  matrix products: 148 us -> 46.9 us
  other arithmetic: 56.2 us -> 16.6 us
  local copies, waits for them, and re-layouts: 62.9 us -> 38.6 us
    pallas_call x0 -> x8, Pallas kernels: none -> 593 us  [the longest x7 532 us: chain_call(): pl.pallas_call(functools.partial(chain_kernel, stages, backward, names, p...]
    ppermute x78 -> x3, waiting for transfers between devices: 143 us -> 3.98 us  [across(): return lax.ppermute(value, 'dp', [(i, i ^ bit) for i in range(dp)])]
    ppermute x31 -> x0, waiting for transfers between devices: 135 us -> none  [the longest x16 131 us: line_side(): return lax.ppermute(value, 'mp', [(i, i ^ 1) for i in range(mp)])]
    dot_general x54 -> x12, matrix products: 148 us -> 46.9 us  [dot(): lax.dot_general(left, right, (((left_dim,), (right_dim,)), ((), ())), pre...]
    ppermute x78 -> x3, starting transfers between devices: 98.6 us -> 2.12 us  [across(): return lax.ppermute(value, 'dp', [(i, i ^ bit) for i in range(dp)])]
    ppermute x31 -> x0, starting transfers between devices: 84.4 us -> none  [the longest x13 71.4 us: swap(): return lax.ppermute(value, ('dp', 'mp'), swap_pairs)]
    ppermute x2, waiting for transfers between devices: 23 us -> 2.86 us  [scatter_vectors(): got = lax.ppermute(sent, 'mp', [(i, i ^ bit) for i in range(mp)])]
    convert_element_type x18 -> x5, other arithmetic: 21.2 us -> 7.16 us  [the longest x1 3.07 us: body(): reorder_low = reorder.astype(BF16)]
  transfers between devices with their start and end apart: 111 -> 5, of which waited for: 41 -> 3; matrix products, arithmetic and copies ran while one was open for 29% -> 2% of each run, Pallas kernels for 7% -> 0%
where the time goes in v3:
time: 765 us; the launch traced here: 759 us
  Pallas kernels  646 us (84%)
  matrix products  46.9 us (6%)
  local copies, waits for them, and re-layouts  38.6 us (5%)
  other arithmetic  16.6 us (2%)
    pallas_call x7, Pallas kernels, chain_call(): pl.pallas_call(functools.partial(chain_kernel, stages, backward, names, p...  532 us
    pallas_call x1, Pallas kernels, start_call(): pl.pallas_call(functools.partial(start_kernel, jobs, names), name='start_...  60.5 us
    dot_general x12, matrix products, dot(): lax.dot_general(left, right, (((left_dim,), (right_dim,)), ((), ())), pre...  46.9 us
    pallas_call x2, Pallas kernels, attend_backward(): pl.pallas_call(backward_kernel, name='attend_backward', out_shape=jax.Sha...  26.8 us
    pallas_call x2, Pallas kernels, attend_forward(): pl.pallas_call(forward_kernel, name='attend_forward', out_shape=(jax.Shap...  26.3 us
  transfers between devices with their start and end apart: 5, of which 3 were waited for; matrix products, arithmetic and copies ran while one was open for 2% of the time, Pallas kernels for 0%

profile of v3, /device:TPU:0, one launch (start us, length us, event | category | flops | bytes accessed | tf_op | source)
XLA Modules:
  0.0 759.1 jit_solution(15910133397191113027)
XLA Ops:
  0.7 1.3 slice_bitcast_fusion.4
  2.4 1.1 reshape.201.refs_3_
  3.5 0.9 slice_bitcast_fusion.1
  8.1 60.5 %start_exchange.1 = (bf16[256,1280]{1,0:T(8,128)(2,1)}, s32[8,1024]{1,0:T(8,128)}, f32[32,16,128]{2,1,0:T(8,128)}, bf16[2,160,960]{2,1,0:T(8,128)(2,1)}, bf16[2,...) custom-call(bf16[256,1280]{1,0:T(8,128)(2,1)} %convert_element_type., ...), custom_call_target="tpu_custom_call" | custom-call | bytes 67108864 | tf_op jit(solution)/shard_map/start_exchange/pallas_call | solution.py:562
  68.6 1.3 fusion.7
  71.2 3.1 fusion.1.refs_2_.refs_8_
  74.3 2.1 fusion.2
  77.6 2.5 fusion.3.refs_0_.refs_6_
  83.1 1.1 reshape.206.refs_15_
  84.9 1.3 fusion.10
  86.9 47.5 %chain_forward.4 = (bf16[2,160,1280]{2,1,0:T(8,128)(2,1)}, bf16[2,160,1280]{2,1,0:T(8,128)(2,1)}, bf16[2,160,320]{2,1,0:T(8,128)(2,1)}, bf16[2,160,320]{2,1,0:T(...) custom-call(f32[256,1280]{1,0:T(8,128)} %fusion.3.refs_0_.refs_6_, ...), custom_call_target="tpu_custom_call" | custom-call | flops 2516582400 | bytes 16777216 | tf_op jit(solution)/shard_map/chain_forward/pallas_call | solution.py:994
  134.4 1.5 copy-done.6
  135.9 13.2 %attend_forward.2 = (bf16[320,1024]{1,0:T(8,128)(2,1)S(1)}, f32[4,1,1024]{2,1,0:T(1,128)S(1)}) custom-call(s32[16]{0:T(128)S(1)} %reshape.217.active, bf16[960,1024]{1,0:T(8,128)(2,1)S(1)} %copy-done.6, s32[1,1024]{1,0:T(1,128)S(1)} %get-tuple-element.235.code_row, s32[1024,1]{1,0:T(8,128)S(1)} %copy.81.code_col), custom_call_target="tpu_custom_call" | custom-call | flops 1342177280 | bytes 4194304 | tf_op jit(solution)/shard_map/attend_forward/pallas_call | solution.py:180
  149.9 97.5 %chain_forward.5 = (bf16[2,160,1280]{2,1,0:T(8,128)(2,1)}, bf16[2,160,1280]{2,1,0:T(8,128)(2,1)}, bf16[2,160,1280]{2,1,0:T(8,128)(2,1)}, bf16[2,160,960]{2,1,0:T...) custom-call(f32[256,1280]{1,0:T(8,128)} %fusion.3.refs_0_.refs_6_, ...), custom_call_target="tpu_custom_call" | custom-call | flops 7549747200 | bytes 33554432 | tf_op jit(solution)/shard_map/chain_forward/pallas_call | solution.py:994
  247.4 32.7 %chain_forward.6 = (bf16[2,160,1280]{2,1,0:T(8,128)(2,1)}, bf16[2,160,320]{2,1,0:T(8,128)(2,1)}, bf16[2,160,320]{2,1,0:T(8,128)(2,1)}, bf16[2,160,1280]{2,1,0:T(...) custom-call(f32[256,1280]{1,0:T(8,128)} %get-tuple-element.116.refs_0_.refs_6_, ...), custom_call_target="tpu_custom_call" | custom-call | flops 2516582400 | bytes 16777216 | tf_op jit(solution)/shard_map/chain_forward/pallas_call | solution.py:994
  280.1 1.5 copy-done.4
  281.7 13.1 %attend_forward.3 = (bf16[320,1024]{1,0:T(8,128)(2,1)S(1)}, f32[4,1,1024]{2,1,0:T(1,128)S(1)}) custom-call(s32[16]{0:T(128)S(1)} %reshape.217.active, bf16[960,1024]{1,0:T(8,128)(2,1)S(1)} %copy-done.4, s32[1,1024]{1,0:T(1,128)S(1)} %get-tuple-element.235.code_row, s32[1024,1]{1,0:T(8,128)S(1)} %copy.81.code_col), custom_call_target="tpu_custom_call" | custom-call | flops 1342177280 | bytes 4194304 | tf_op jit(solution)/shard_map/attend_forward/pallas_call | solution.py:180
  296.5 66.0 %chain_forward.7 = (bf16[2,160,1280]{2,1,0:T(8,128)(2,1)}, bf16[2,160,1280]{2,1,0:T(8,128)(2,1)}, bf16[2,160,1280]{2,1,0:T(8,128)(2,1)}, f32[256,1280]{1,0:T(8,1...) custom-call(f32[256,1280]{1,0:T(8,128)} %get-tuple-element.116.refs_, ...), custom_call_target="tpu_custom_call" | custom-call | flops 7549747200 | bytes 33554432 | tf_op jit(solution)/shard_map/chain_forward/pallas_call | solution.py:994
  362.6 66.8 %chain_backward.3 = (f32[8,1280]{1,0:T(8,128)}, f32[256,1280]{1,0:T(8,128)}, bf16[1024,1280]{1,0:T(8,128)(2,1)}, bf16[1024,1280]{1,0:T(8,128)(2,1)}, f32[1,1280]...) custom-call(f32[256,1280]{1,0:T(8,128)} %get-tuple-element.132.refs_0_, ...), custom_call_target="tpu_custom_call" | custom-call | flops 7549747200 | bytes 33554432 | tf_op jit(solution)/shard_map/chain_backward/pallas_call | solution.py:994
  429.5 4.4 convolution_convert_fusion.6.refs_26_.refs_14_
  433.9 13.4 %attend_backward.2.refs_1_ = bf16[960,1024]{1,0:T(8,128)(2,1)S(1)} custom-call(s32[16]{0:T(128)S(1)} %reshape.217.active, bf16[960,1024]{1,0:T(8,128)(2,1)S(1)} %copy-done.5, bf16[320,1024]{1,0:T(8,128)(2,1)S(1)} %copy-done.11, bf16[320,1024]{1,0:T(8,128)(2,1)S(1)} %copy-done.13, f32[4,1,1024]{2,1,0:T(1,128)S(1)} %get-tuple-element.142.log_sum, ...), custom_call_target="tpu_custom_call" | custom-call | flops 3355443200 | bytes 10485760 | tf_op jit(solution)/shard_map/attend_backward/pallas_call | solution.py:208
  447.7 4.3 convolution_convert_fusion.4.refs_25_.refs_11_
  452.1 5.0 convolution_convert_fusion.2.refs_24_
  457.1 5.3 convolution_convert_fusion.3.refs_23_
  462.4 100.4 %chain_backward.4 = (f32[8,1280]{1,0:T(8,128)}, bf16[2,160,1280]{2,1,0:T(8,128)(2,1)}, bf16[2,160,1280]{2,1,0:T(8,128)(2,1)}, bf16[2,160,1280]{2,1,0:T(8,128)(2,...) custom-call(f32[256,1280]{1,0:T(8,128)} %get-tuple-element.140.refs_, ...), custom_call_target="tpu_custom_call" | custom-call | flops 10066329600 | bytes 50331648 | tf_op jit(solution)/shard_map/chain_backward/pallas_call | solution.py:994
  562.8 2.8 convolution_convert_fusion.7
  565.6 1.3 copy.90.refs_18_
  566.9 1.5 copy-done.7
  568.4 1.1 copy-done.12
  569.5 13.4 %attend_backward.3.refs_1_ = bf16[960,1024]{1,0:T(8,128)(2,1)S(1)} custom-call(s32[16]{0:T(128)S(1)} %reshape.217.active, bf16[960,1024]{1,0:T(8,128)(2,1)S(1)} %copy-done.7, bf16[320,1024]{1,0:T(8,128)(2,1)S(1)} %copy-done.9, bf16[320,1024]{1,0:T(8,128)(2,1)S(1)} %copy-done.12, f32[4,1,1024]{2,1,0:T(1,128)S(1)} %get-tuple-element.157.log_sum, ...), custom_call_target="tpu_custom_call" | custom-call | flops 3355443200 | bytes 10485760 | tf_op jit(solution)/shard_map/attend_backward/pallas_call | solution.py:208
  583.3 4.0 convolution_convert_fusion.5
  587.3 4.8 copy.89.refs_17_
  592.1 8.0 %convolution_convert_fusion.refs_10_ = bf16[1280,1280]{1,0:T(8,128)(2,1)} fusion(bf16[1024,1280]{1,0:T(8,128)(2,1)} %get-tuple-element.160, bf16[1024,1280]{1,0:T(8,128)(2,1)} %get-tuple-element.161), kind=kOutput, calls=%fused_computation | convolution fusion | flops 3357081600 | bytes 8519680 | tf_op jit(solution)/shard_map/dot_general | solution.py:36
  600.1 5.0 convolution_convert_fusion.1.refs_9_
  605.2 121.6 %chain_backward.5 = (f32[8,1280]{1,0:T(8,128)}, bf16[2,160,1280]{2,1,0:T(8,128)(2,1)}, bf16[2,160,1280]{2,1,0:T(8,128)(2,1)}, bf16[2,160,960]{2,1,0:T(8,128)(2,1...) custom-call(f32[256,1280]{1,0:T(8,128)} %get-tuple-element.155.refs_, ...), custom_call_target="tpu_custom_call" | custom-call | flops 2516582400 | bytes 16777216 | tf_op jit(solution)/shard_map/chain_backward/pallas_call | solution.py:994
  727.9 2.1 fusion
  731.5 1.0 collective-permute-start
  732.5 3.4 collective-permute-done
  736.0 1.0 collective-permute-start.1
  737.1 2.4 pad_maximum_fusion.2
  740.2 1.3 pad_maximum_fusion.1
  741.5 1.5 reshape.213
  743.0 1.3 reshape.214
  744.5 1.7 pad_maximum_fusion
  746.2 2.9 collective-permute-done.3
  750.0 1.2 copy.93
  751.2 1.1 convert_element_type.80
  752.3 1.1 convert_element_type.71
  (196 shorter events, 23.7 us)
Async XLA Ops:
  0.6 2.9 copy-start.16
  0.7 3.8 copy-start.24
  0.7 4.5 copy-start.14
  2.3 3.8 copy-start.32
  2.3 3.8 copy-start.33
  2.3 3.8 copy-start.29
  2.3 4.4 copy-start.34
  2.4 4.5 copy-start.35
  2.4 4.5 copy-start.37
  2.4 4.6 copy-start.38
  2.4 4.7 copy-start.39
  2.4 4.8 copy-start.40
  2.4 4.8 copy-start.41
  2.4 4.9 copy-start.42
  71.2 6.4 copy-start.36
  281.6 14.0 %copy-start.15 = (f32[256,1280]{1,0:T(8,128)S(1)}, f32[256,1280]{1,0:T(8,128)}, u32[]{:S(2)}) copy-start(f32[256,1280]{1,0:T(8,128)} %param.33) | copy-start | bytes 3932164
  362.6 66.9 %copy-start.11 = (bf16[320,1024]{1,0:T(8,128)(2,1)S(1)}, bf16[320,1024]{1,0:T(8,128)(2,1)}, u32[]{:S(2)}) copy-start(bf16[320,1024]{1,0:T(8,128)(2,1)} %copy-done.10) | copy-start | bytes 1966084
  429.5 4.5 copy-start.2
  429.5 4.4 copy-start.3
  429.5 4.4 copy-start.5
  429.5 4.4 copy-start.13
  433.9 13.8 %copy-start.43 = (bf16[1024,1280]{1,0:T(8,128)(2,1)S(1)}, bf16[1024,1280]{1,0:T(8,128)(2,1)}, u32[]{:S(2)}) copy-start(bf16[1024,1280]{1,0:T(8,128)(2,1)} %get-tuple-element.153) | copy-start | bytes 7864324
  447.4 4.7 copy-start.1
  447.7 4.3 copy-start.47
  447.7 4.3 copy-start.50
  452.1 5.1 copy-start.46
  452.1 5.1 copy-start.49
  462.4 100.4 %copy-start.9 = (bf16[320,1024]{1,0:T(8,128)(2,1)S(1)}, bf16[320,1024]{1,0:T(8,128)(2,1)}, u32[]{:S(2)}) copy-start(bf16[320,1024]{1,0:T(8,128)(2,1)} %copy-done.8) | copy-start | bytes 1966084
  569.5 13.8 %copy-start.44 = (bf16[1024,1280]{1,0:T(8,128)(2,1)S(1)}, bf16[1024,1280]{1,0:T(8,128)(2,1)}, u32[]{:S(2)}) copy-start(bf16[1024,1280]{1,0:T(8,128)(2,1)} %get-tuple-element.166) | copy-start | bytes 7864324
  582.9 4.3 copy-start
  592.1 8.0 %copy-start.45 = (bf16[1024,1280]{1,0:T(8,128)(2,1)S(1)}, bf16[1024,1280]{1,0:T(8,128)(2,1)}, u32[]{:S(2)}) copy-start(bf16[1024,1280]{1,0:T(8,128)(2,1)} %get-tuple-element.159) | copy-start | bytes 7864324
  592.1 8.0 %copy-start.48 = (bf16[1024,1280]{1,0:T(8,128)(2,1)S(1)}, bf16[1024,1280]{1,0:T(8,128)(2,1)}, u32[]{:S(2)}) copy-start(bf16[1024,1280]{1,0:T(8,128)(2,1)} %get-tuple-element.158) | copy-start | bytes 7864324
  605.2 122.5 %copy-start.27 = (f32[8,1280]{1,0:T(8,128)S(1)}, f32[8,1280]{1,0:T(8,128)}, u32[]{:S(2)}) copy-start(f32[8,1280]{1,0:T(8,128)} %get-tuple-element.172) | copy-start | bytes 122884
  605.2 122.6 %copy-start.28 = (f32[8,1280]{1,0:T(8,128)S(1)}, f32[8,1280]{1,0:T(8,128)}, u32[]{:S(2)}) copy-start(f32[8,1280]{1,0:T(8,128)} %get-tuple-element.173) | copy-start | bytes 122884
  726.8 4.4 copy-start.30
  726.8 4.4 copy-start.31
  726.8 10.3 %copy-start.20 = (f32[160,1280]{1,0:T(8,128)S(1)}, f32[160,1280]{1,0:T(8,128)}, u32[]{:S(2)}) copy-start(f32[160,1280]{1,0:T(8,128)} %get-tuple-element.183) | copy-start | bytes 2457604
  730.9 9.3 %copy-start.18 = (f32[160,1280]{1,0:T(8,128)S(1)}, f32[160,1280]{1,0:T(8,128)}, u32[]{:S(2)}) copy-start(f32[160,1280]{1,0:T(8,128)} %get-tuple-element.181) | copy-start | bytes 2457604
  730.9 9.3 %copy-start.19 = (f32[160,1280]{1,0:T(8,128)S(1)}, f32[160,1280]{1,0:T(8,128)}, u32[]{:S(2)}) copy-start(f32[160,1280]{1,0:T(8,128)} %get-tuple-element.180) | copy-start | bytes 2457604
  731.5 4.4 collective-permute-start
  736.0 4.0 collective-permute-start.1
  739.5 3.5 copy-start.21
  740.1 4.3 collective-permute-start.2
  743.0 6.1 copy-start.25
  743.0 6.1 copy-start.26
  744.4 4.6 collective-permute-start.3
  746.1 5.0 copy-start.23
  749.0 4.4 collective-permute-start.4
  (8 other events, 12.3 us)

commit v4 on v3

--- a/solution.py
+++ b/solution.py
@@ -4,6 +4,7 @@
 import jax.numpy as jnp
 from jax import lax
 from jax.experimental import pallas as pl
+from jax.experimental.layout import Layout, with_layout_constraint
 from jax.experimental.pallas import tpu as pltpu
 from jax.sharding import PartitionSpec as P
 
@@ -11,6 +12,7 @@
 HD = 80
 LAYERS = 2
 EPSILON = 1e-06
+AXES = ("dp", "mp")
 F32 = jnp.float32
 BF16 = jnp.bfloat16
 HIGHEST = lax.Precision.HIGHEST
@@ -40,6 +42,10 @@
         preferred_element_type=F32,
         precision=precision,
     ).astype(kind)
+
+
+def grad_dot(left, right, left_dim, right_dim):
+    return with_layout_constraint(dot(left, right, left_dim, right_dim, BF16), Layout((0, 1)))
 
 
 def rotary_tables(coords):
@@ -242,6 +248,7 @@
     ROWS, ROWS2, ROWS_OUT, SECOND, SECOND_BIAS, SLOPE, SOURCE, STATE, SUMS, TARGET, UNIT_SUMS,
     UP, VALUE, WIDE_SUMS,
 ) = range(69)
+ONE, OTHER = 103, 104
 COTANGENT, COSINE, SINE = 100, 101, 102
 FIRST_HBM = 200
 COTANGENT_HBM = FIRST_HBM + 50
@@ -413,12 +420,13 @@
         block = lambda at: buffer(GRAD).at[at * depth : (at + 1) * depth]
         sums = ref[SUMS, pack]
         if step == 5:
-            corners, from_low, from_high = buffer(CORNERS), buffer(FROM_LOW), buffer(FROM_HIGH)
+            from_low, from_high = buffer(FROM_LOW), buffer(FROM_HIGH)
+            corners = [buffer(CORNERS).at[at] for at in range(2)]
             copies = [
                 self.send(block(3), from_low.at[1], LOW),
                 self.send(block(4), from_high.at[0], HIGH),
             ]
-            term = self.fetch(columns, [block(2), block(5), corners.at[0], corners.at[1]])
+            term = self.fetch(columns, [block(2), block(5), *corners])
             for at in range(2):
                 sums[at] = (term(at) + term(2 + at)).astype(BF16)
             copies.append(self.send(sums.at[0], from_low.at[0], LOW))
@@ -504,9 +512,8 @@
     needs, makes, scratch = {}, {}, {}
     for pack, step in jobs:
         for part in PACK_NEEDS[step]:
-            name = (pack, part)
-            if name not in makes:
-                needs[name] = packs[name]
+            if (pack, part) not in makes:
+                needs[pack, part] = packs[pack, part]
         if step < 4:
             depth, columns = packs[(pack, MINE)].shape
         else:
@@ -938,7 +945,7 @@
             passed[name] = value
             continue
         blocks, row = [], 0
-        for part in (PAIR, LOW, HIGH, CORNER, ALL):
+        for part in (PAIR, LOW, HIGH, CORNER, ONE, OTHER, ALL):
             piece = (value.pack, part)
             if piece not in packs and piece not in makes:
                 continue
@@ -1151,6 +1158,9 @@
         jobs = {}
         if balanced:
             space = -(-packed.shape[0] // 1024) * 1024
+            late = packs[(QKV, 1), MINE], packs[(DOWN, 1), MINE], packs[(PROJ, 1), MINE]
+            hidden, late = lax.optimization_barrier((hidden, late))
+            packs[(QKV, 1), MINE], packs[(DOWN, 1), MINE], packs[(PROJ, 1), MINE] = late
             begun = start_call(
                 3 * LAYERS + 1,
                 hidden,
@@ -1167,17 +1177,13 @@
                     8: ((PROJ, 0, 3),),
                 },
                 (FORWARD, 0): {
-                    0: ((UP, 0, 3), (DOWN, 0, 2)),
-                    2: ((QKV, 1, 1), (PROJ, 1, 1)),
-                    3: ((DOWN, 0, 3),),
-                    4: ((UP, 1, 1), (QKV, 1, 2)),
-                    6: ((QKV, 1, 3), (UP, 1, 2)),
+                    0: ((DOWN, 0, 3), (QKV, 1, 1)),
+                    2: ((PROJ, 1, 1),),
+                    4: ((QKV, 1, 2), (PROJ, 1, 2), (UP, 1, 1)),
+                    6: ((QKV, 1, 3), (PROJ, 1, 3)),
                 },
-                (LEAVE, 1): {
-                    0: ((UP, 1, 3), (PROJ, 1, 2), (DOWN, 1, 1)),
-                    8: ((PROJ, 1, 3),),
-                },
-                (FORWARD, 1): {0: ((DOWN, 1, 2),), 2: ((DOWN, 1, 3),)},
+                (LEAVE, 1): {0: ((UP, 1, 2), (DOWN, 1, 1))},
+                (FORWARD, 1): {0: ((DOWN, 1, 3),)},
                 (BACKWARD, 0): {
                     0: ((UP, 1, 4), (DOWN, 1, 4)),
                     1: ((UP, 1, 5),),
@@ -1186,13 +1192,13 @@
                     8: ((DOWN, 1, 6), (QKV, 1, 5), (PROJ, 1, 5)),
                 },
                 (BACKWARD, FINAL): {
-                    0: ((UP, 0, 4), (DOWN, 0, 4), (QKV, 1, 6), (PROJ, 1, 6)),
+                    0: ((UP, 0, 4), (DOWN, 0, 4)),
                     1: ((UP, 0, 5),),
+                    2: ((QKV, 1, 6), (PROJ, 1, 6), (QKV, 0, 4), (PROJ, 0, 4)),
                     9: (
-                        *((QKV, 0, 4), (PROJ, 0, 4), (DOWN, 0, 5), (UP, 1, 7), (DOWN, 1, 7)),
-                        *((UP, 0, 6), (QKV, 0, 5), (PROJ, 0, 5), (QKV, 1, 7), (PROJ, 1, 7)),
-                        *((DOWN, 0, 6), (UP, 0, 7), (QKV, 0, 6), (PROJ, 0, 6)),
-                        *((DOWN, 0, 7), (QKV, 0, 7), (PROJ, 0, 7)),
+                        *((UP, 0, 6), (DOWN, 0, 5), (QKV, 0, 5), (UP, 1, 7), (DOWN, 1, 7)),
+                        *((DOWN, 0, 6), (PROJ, 0, 5), (QKV, 1, 7), (PROJ, 1, 7), (UP, 0, 7)),
+                        *((QKV, 0, 6), (PROJ, 0, 6), (DOWN, 0, 7), (QKV, 0, 7), (PROJ, 0, 7)),
                     ),
                 },
             }
@@ -1317,12 +1323,30 @@
                 ENTER_GAIN: row(pre_gain_all[layer]),
             }
 
+        def beside_forward(layer):
+            if not balanced:
+                return
+            low, high = high_bits
+            up, down = (UP, layer), (DOWN, layer)
+            packs[up, ONE] = across(packs[up, LOW][:1], high)
+            packs[up, OTHER] = across(packs[up, HIGH][1:], low)
+            packs[down, LOW] = across(packs[down, PAIR], low)
+            packs[down, HIGH] = across(packs[down, PAIR], high)
+
+        hidden, wide_all, qkv_bias_mine, up_bias_mine, facts = lax.optimization_barrier(
+            (hidden, wide_all, qkv_bias_mine, up_bias_mine, facts)
+        )
+        pre_gain_all, pre_bias_all, proj_bias_all, mid_gain_all, mid_bias_all, down_bias_all = (
+            wide_all[i] for i in range(len(wide))
+        )
         leave0 = call_leave(0, hidden)
+        beside_forward(0)
         qkv0 = leave0[TARGET]
         mixed0, log_sum0 = attend_forward(qkv0, facts)
         state0 = call_forward(0, hidden, mixed0, {})
         start1 = state0[MIXED]
         leave1 = call_leave(1, start1)
+        beside_forward(1)
         qkv1 = leave1[TARGET]
         mixed1, log_sum1 = attend_forward(qkv1, facts)
         cotangent = cotangent.astype(BF16)
@@ -1342,11 +1366,11 @@
             out_hidden = swap(turn_low(state1[MIXED]).astype(BF16))
             gradient = turn_low(swap(cotangent))
             back1 = call_backward(1, gradient, {}, state1[ENTERED], state1[SLOPE_HBM], {})
-        packs[(UP, 1), GRAD] = dot(state1[ROWS_HBM], back1[ACT_HBM], 0, 0, BF16)
-        packs[(DOWN, 1), GRAD] = dot(back1[ROWS_HBM], state1[ACT_HBM], 0, 0, BF16)
+        packs[(UP, 1), GRAD] = grad_dot(state1[ROWS_HBM], back1[ACT_HBM], 0, 0)
+        packs[(DOWN, 1), GRAD] = grad_dot(back1[ROWS_HBM], state1[ACT_HBM], 0, 0)
         linear1 = attend_backward(qkv1, mixed1, back1[TARGET], log_sum1, facts)
-        packs[(QKV, 1), GRAD] = dot(leave1[ROWS2_HBM], linear1, 0, 1, BF16)
-        packs[(PROJ, 1), GRAD] = dot(back1[ROWS2_HBM], mixed1, 0, 1, BF16)
+        packs[(QKV, 1), GRAD] = grad_dot(leave1[ROWS2_HBM], linear1, 0, 1)
+        packs[(PROJ, 1), GRAD] = grad_dot(back1[ROWS2_HBM], mixed1, 0, 1)
         back0 = call_backward(
             0,
             back1[MIXED],
@@ -1355,11 +1379,14 @@
             state0[SLOPE_HBM],
             {},
         )
-        packs[(UP, 0), GRAD] = dot(state0[ROWS_HBM], back0[ACT_HBM], 0, 0, BF16)
-        packs[(DOWN, 0), GRAD] = dot(back0[ROWS_HBM], state0[ACT_HBM], 0, 0, BF16)
-        linear0 = attend_backward(qkv0, mixed0, back0[TARGET], log_sum0, facts)
-        packs[(QKV, 0), GRAD] = dot(leave0[ROWS2_HBM], linear0, 0, 1, BF16)
-        packs[(PROJ, 0), GRAD] = dot(back0[ROWS2_HBM], mixed0, 0, 1, BF16)
+        packs[(UP, 0), GRAD] = grad_dot(state0[ROWS_HBM], back0[ACT_HBM], 0, 0)
+        packs[(DOWN, 0), GRAD] = grad_dot(back0[ROWS_HBM], state0[ACT_HBM], 0, 0)
+        target0, packs[(UP, 0), GRAD], packs[(DOWN, 0), GRAD] = lax.optimization_barrier(
+            (back0[TARGET], packs[(UP, 0), GRAD], packs[(DOWN, 0), GRAD])
+        )
+        linear0 = attend_backward(qkv0, mixed0, target0, log_sum0, facts)
+        packs[(QKV, 0), GRAD] = grad_dot(leave0[ROWS2_HBM], linear0, 0, 1)
+        packs[(PROJ, 0), GRAD] = grad_dot(back0[ROWS2_HBM], mixed0, 0, 1)
         final = chain_call(
             (True, False, False),
             True,

time: 765 us -> 748 us (0.978)
  Pallas kernels: 646 us -> 610 us
  waiting for transfers between devices: 6.84 us -> 21.6 us
  starting transfers between devices: 2.26 us -> 10.6 us
    pallas_call x7, Pallas kernels: 532 us -> 496 us  [chain_call(): pl.pallas_call(functools.partial(chain_kernel, stages, backward, names, p...]
    ppermute x3 -> x11, waiting for transfers between devices: 3.98 us -> 17.5 us  [across(): return lax.ppermute(value, 'dp', [(i, i ^ bit) for i in range(dp)])]
    ppermute x3 -> x11, starting transfers between devices: 2.12 us -> 10.5 us  [across(): return lax.ppermute(value, 'dp', [(i, i ^ bit) for i in range(dp)])]
  transfers between devices with their start and end apart: 5 -> 13, of which waited for: 3 -> 5; matrix products, arithmetic and copies ran while one was open for 2% -> 3% of each run, Pallas kernels for 0% -> 4%
where the time goes in v4:
time: 748 us; the launch traced here: 738 us
  Pallas kernels  610 us (82%)
  matrix products  45.8 us (6%)
  local copies, waits for them, and re-layouts  31.7 us (4%)
  waiting for transfers between devices  21.6 us (3%)
  other arithmetic  15.5 us (2%)
  starting transfers between devices  10.6 us (1%)
    pallas_call x7, Pallas kernels, chain_call(): pl.pallas_call(functools.partial(chain_kernel, stages, backward, names, p...  496 us
    pallas_call x1, Pallas kernels, start_call(): pl.pallas_call(functools.partial(start_kernel, jobs, names), name='start_...  60.5 us
    dot_general x12, matrix products, dot(): lax.dot_general(left, right, (((left_dim,), (right_dim,)), ((), ())), pre...  45.8 us
    pallas_call x2, Pallas kernels, attend_backward(): pl.pallas_call(backward_kernel, name='attend_backward', out_shape=jax.Sha...  27.2 us
    pallas_call x2, Pallas kernels, attend_forward(): pl.pallas_call(forward_kernel, name='attend_forward', out_shape=(jax.Shap...  26.3 us
    ppermute x11, waiting for transfers between devices, across(): return lax.ppermute(value, 'dp', [(i, i ^ bit) for i in range(dp)])  17.5 us
  transfers between devices with their start and end apart: 13, of which 5 were waited for; matrix products, arithmetic and copies ran while one was open for 3% of the time, Pallas kernels for 4%

profile of v4, /device:TPU:0, one launch (start us, length us, event | category | flops | bytes accessed | tf_op | source)
XLA Modules:
  0.0 737.8 jit_solution(1484888858883234507)
XLA Ops:
  0.7 1.3 slice_bitcast_fusion.4
  2.3 1.1 reshape.188.refs_19_
  6.3 1.1 reshape.198.refs_3_
  10.4 60.5 %start_exchange.1 = (bf16[256,1280]{1,0:T(8,128)(2,1)}, s32[8,1024]{1,0:T(8,128)}, f32[32,16,128]{2,1,0:T(8,128)}, bf16[2,160,960]{2,1,0:T(8,128)(2,1)}, bf16[2,...) custom-call(bf16[256,1280]{1,0:T(8,128)(2,1)} %convert_element_type., ...), custom_call_target="tpu_custom_call" | custom-call | bytes 67108864 | tf_op jit(solution)/shard_map/start_exchange/pallas_call | solution.py:569
  70.9 1.3 fusion.9
  75.6 2.2 fusion.4
  77.9 2.6 fusion.3.refs_0_.refs_6_
  80.5 1.3 fusion.12
  83.1 39.1 %chain_forward.4 = (bf16[2,160,1280]{2,1,0:T(8,128)(2,1)}, bf16[2,160,1280]{2,1,0:T(8,128)(2,1)}, bf16[2,160,320]{2,1,0:T(8,128)(2,1)}, bf16[2,160,320]{2,1,0:T(...) custom-call(f32[256,1280]{1,0:T(8,128)} %fusion.3.refs_0_.refs_6_, ...), custom_call_target="tpu_custom_call" | custom-call | flops 2516582400 | bytes 16777216 | tf_op jit(solution)/shard_map/chain_forward/pallas_call | solution.py:1001
  122.3 1.6 collective-permute-start.2
  124.4 1.3 slice.305
  125.7 1.6 collective-permute-start
  127.3 1.0 slice.306
  129.1 1.5 copy-done.4
  130.7 13.2 %attend_forward.2 = (bf16[320,1024]{1,0:T(8,128)(2,1)S(1)}, f32[4,1,1024]{2,1,0:T(1,128)S(1)}) custom-call(s32[16]{0:T(128)S(1)} %reshape.214.active, bf16[960,1024]{1,0:T(8,128)(2,1)S(1)} %copy-done.4, s32[1,1024]{1,0:T(1,128)S(1)} %get-tuple-element.126.code_row, s32[1024,1]{1,0:T(8,128)S(1)} %copy.59.code_col), custom_call_target="tpu_custom_call" | custom-call | flops 1342177280 | bytes 4194304 | tf_op jit(solution)/shard_map/attend_forward/pallas_call | solution.py:186
  145.3 7.1 collective-permute-done.refs_10_.refs_15_
  153.6 72.9 %chain_forward.5 = (bf16[2,160,1280]{2,1,0:T(8,128)(2,1)}, bf16[2,160,960]{2,1,0:T(8,128)(2,1)}, bf16[2,160,320]{2,1,0:T(8,128)(2,1)}, bf16[2,160,960]{2,1,0:T(8...) custom-call(f32[256,1280]{1,0:T(8,128)} %fusion.3.refs_0_.refs_6_, ...), custom_call_target="tpu_custom_call" | custom-call | flops 7549747200 | bytes 33554432 | tf_op jit(solution)/shard_map/chain_forward/pallas_call | solution.py:1001
  226.4 32.4 %chain_forward.6 = (bf16[2,160,1280]{2,1,0:T(8,128)(2,1)}, bf16[2,160,1280]{2,1,0:T(8,128)(2,1)}, bf16[2,160,1280]{2,1,0:T(8,128)(2,1)}, bf16[960,1024]{1,0:T(8,128)(2,1)}, bf16[1024,1280]{1,0:T(8,128)(2,1)}) custom-call(f32[256,1280]{1,0:T(8,128)} %get-tuple-element.138.refs_0_.refs_6_, bf16[2,160,960]{2,1,0:T(8,128)(2,1)} %get-tuple-element.139.refs_1_.refs_2_, ...), custom_call_target="tpu_custom_call" | custom-call | flops 2516582400 | bytes 16777216 | tf_op jit(solution)/shard_map/chain_forward/pallas_call | solution.py:1001
  258.8 1.4 collective-permute-start.6
  260.9 1.0 slice.322
  262.0 1.4 collective-permute-start.4
  263.3 1.0 slice.323
  265.2 3.1 fusion.1.refs_2_.refs_8_
  269.1 13.2 %attend_forward.3 = (bf16[320,1024]{1,0:T(8,128)(2,1)S(1)}, f32[4,1,1024]{2,1,0:T(1,128)S(1)}) custom-call(s32[16]{0:T(128)S(1)} %reshape.214.active, bf16[960,1024]{1,0:T(8,128)(2,1)S(1)} %copy-done.6, s32[1,1024]{1,0:T(1,128)S(1)} %get-tuple-element.126.code_row, s32[1024,1]{1,0:T(8,128)S(1)} %copy.59.code_col), custom_call_target="tpu_custom_call" | custom-call | flops 1342177280 | bytes 4194304 | tf_op jit(solution)/shard_map/attend_forward/pallas_call | solution.py:186
  283.1 6.4 collective-permute-done.4.refs_10_
  289.5 61.6 %chain_forward.7 = (bf16[2,160,1280]{2,1,0:T(8,128)(2,1)}, f32[256,1280]{1,0:T(8,128)}, f32[256,1280]{1,0:T(8,128)}, bf16[1024,1280]{1,0:T(8,128)(2,1)}, bf16[10...) custom-call(f32[256,1280]{1,0:T(8,128)} %get-tuple-element.138.refs_0_.refs_6_, ...), custom_call_target="tpu_custom_call" | custom-call | flops 7549747200 | bytes 33554432 | tf_op jit(solution)/shard_map/chain_forward/pallas_call | solution.py:1001
  351.1 68.3 %chain_backward.3 = (f32[8,1280]{1,0:T(8,128)}, f32[256,1280]{1,0:T(8,128)}, bf16[1024,1280]{1,0:T(8,128)(2,1)}, bf16[1024,1280]{1,0:T(8,128)(2,1)}, f32[1,1280]...) custom-call(f32[256,1280]{1,0:T(8,128)} %get-tuple-element.154.refs_0_, ...), custom_call_target="tpu_custom_call" | custom-call | flops 7549747200 | bytes 33554432 | tf_op jit(solution)/shard_map/chain_backward/pallas_call | solution.py:1001
  419.5 4.3 convolution_convert_fusion.7.refs_27_.refs_14_
  423.8 13.8 %attend_backward.2.refs_1_ = bf16[960,1024]{1,0:T(8,128)(2,1)S(1)} custom-call(s32[16]{0:T(128)S(1)} %reshape.214.active, bf16[960,1024]{1,0:T(8,128)(2,1)S(1)} %copy-done.6, bf16[320,1024]{1,0:T(8,128)(2,1)S(1)} %copy-done.10, bf16[320,1024]{1,0:T(8,128)(2,1)S(1)} %copy-done.12, f32[4,1,1024]{2,1,0:T(1,128)S(1)} %get-tuple-element.162.log_sum, ...), custom_call_target="tpu_custom_call" | custom-call | flops 3355443200 | bytes 10485760 | tf_op jit(solution)/shard_map/attend_backward/pallas_call | solution.py:214
  438.0 4.3 convolution_convert_fusion.5.refs_26_.refs_11_
  442.4 5.1 convolution_convert_fusion.2.refs_25_
  447.5 5.0 convolution_convert_fusion.3.refs_24_
  452.5 99.8 %chain_backward.4 = (f32[8,1280]{1,0:T(8,128)}, bf16[2,160,1280]{2,1,0:T(8,128)(2,1)}, bf16[2,160,1280]{2,1,0:T(8,128)(2,1)}, bf16[2,160,1280]{2,1,0:T(8,128)(2,...) custom-call(f32[256,1280]{1,0:T(8,128)} %get-tuple-element.160.refs_, ...), custom_call_target="tpu_custom_call" | custom-call | flops 10066329600 | bytes 50331648 | tf_op jit(solution)/shard_map/chain_backward/pallas_call | solution.py:1001
  552.4 4.4 convolution_convert_fusion.6.refs_18_
  556.8 5.1 convolution_convert_fusion.refs_10_
  561.9 5.1 convolution_convert_fusion.1.refs_9_
  566.9 13.4 %attend_backward.3.refs_1_ = bf16[960,1024]{1,0:T(8,128)(2,1)S(1)} custom-call(s32[16]{0:T(128)S(1)} %reshape.214.active, bf16[960,1024]{1,0:T(8,128)(2,1)S(1)} %copy-done.5, bf16[320,1024]{1,0:T(8,128)(2,1)S(1)} %copy-done.8, bf16[320,1024]{1,0:T(8,128)(2,1)S(1)} %copy-done.11, f32[4,1,1024]{2,1,0:T(1,128)S(1)} %get-tuple-element.179.log_sum, ...), custom_call_target="tpu_custom_call" | custom-call | flops 3355443200 | bytes 10485760 | tf_op jit(solution)/shard_map/attend_backward/pallas_call | solution.py:214
  580.7 4.2 convolution_convert_fusion.4.refs_17_
  585.0 122.3 %chain_backward.5 = (f32[8,1280]{1,0:T(8,128)}, bf16[2,160,1280]{2,1,0:T(8,128)(2,1)}, bf16[2,160,1280]{2,1,0:T(8,128)(2,1)}, bf16[2,160,1280]{2,1,0:T(8,128)(2,...) custom-call(f32[256,1280]{1,0:T(8,128)} %get-tuple-element.172.refs_, ...), custom_call_target="tpu_custom_call" | custom-call | flops 2516582400 | bytes 16777216 | tf_op jit(solution)/shard_map/chain_backward/pallas_call | solution.py:1001
  708.4 2.1 fusion
  712.0 1.0 collective-permute-start.8
  713.0 3.5 collective-permute-done.8
  717.5 2.5 pad_maximum_fusion.2
  720.7 1.3 pad_maximum_fusion.1
  723.4 4.1 collective-permute-done.11
  728.4 1.2 copy.65
  729.6 1.1 convert_element_type.80
  730.8 1.1 convert_element_type.71
  (223 shorter events, 30.5 us)
Async XLA Ops:
  0.7 4.3 copy-start.13
  5.1 4.4 copy-start.43
  5.2 4.4 copy-start.44
  70.9 7.0 copy-start.38
  122.3 30.1 %collective-permute-start.2 = (bf16[2,160,1280]{2,1,0:T(8,128)(2,1)}, bf16[2,160,1280]{2,1,0:T(8,128)(2,1)S(1)}, u32[]{:S(2)}, u32[]{:S(2)}) collective-permute-start(bf16[2,160,1280]{2,1,0:T(8,128)(2,1)} %get-tuple-element.134.refs_12_.refs_8_), channel_id=1, source_target_pairs={{0,8},{4,12},{8,0},{12,4},{16,24},{20,28},{24,16},{28,20},{1,9},{5... | collective-permute-start | bytes 2457608 | tf_op jit(solution)/shard_map/ppermute | solution.py:1026
  123.8 28.6 %collective-permute-start.3 = (bf16[2,160,1280]{2,1,0:T(8,128)(2,1)}, bf16[2,160,1280]{2,1,0:T(8,128)(2,1)S(1)}, u32[]{:S(2)}, u32[]{:S(2)}) collective-permute-start(bf16[2,160,1280]{2,1,0:T(8,128)(2,1)} %get-tuple-element.134.refs_12_.refs_8_), channel_id=1, source_target_pairs={{0,16},{4,20},{8,24},{12,28},{16,0},{20,4},{24,8},{28,12},{1,17},{... | collective-permute-start | bytes 2457608 | tf_op jit(solution)/shard_map/ppermute | solution.py:1026
  125.7 26.7 %collective-permute-start = (bf16[1,160,1280]{2,1,0:T(8,128)(2,1)S(1)}, bf16[1,160,1280]{2,1,0:T(8,128)(2,1)}, u32[]{:S(2)}, u32[]{:S(2)}) collective-permute-start(bf16[1,160,1280]{2,1,0:T(8,128)(2,1)S(1)} %slice.305), channel_id=1, source_target_pairs={{0,16},{4,20},{8,24},{12,28},{16,0},{20,4},{24,8},{28,12},{1,17},{... | collective-permute-start | bytes 1228808 | tf_op jit(solution)/shard_map/ppermute | solution.py:1026
  128.3 24.1 %collective-permute-start.1 = (bf16[1,160,1280]{2,1,0:T(8,128)(2,1)S(1)}, bf16[1,160,1280]{2,1,0:T(8,128)(2,1)}, u32[]{:S(2)}, u32[]{:S(2)}) collective-permute-start(bf16[1,160,1280]{2,1,0:T(8,128)(2,1)S(1)} %slice.306), channel_id=1, source_target_pairs={{0,8},{4,12},{8,0},{12,4},{16,24},{20,28},{24,16},{28,20},{1,9},{5... | collective-permute-start | bytes 1228808 | tf_op jit(solution)/shard_map/ppermute | solution.py:1026
  258.8 9.4 %copy-start.14 = (f32[256,1280]{1,0:T(8,128)S(1)}, f32[256,1280]{1,0:T(8,128)}, u32[]{:S(2)}) copy-start(f32[256,1280]{1,0:T(8,128)} %param.33) | copy-start | bytes 3932164
  258.8 30.7 %collective-permute-start.6 = (bf16[2,160,1280]{2,1,0:T(8,128)(2,1)}, bf16[2,160,1280]{2,1,0:T(8,128)(2,1)}, u32[]{:S(2)}, u32[]{:S(2)}) collective-permute-start(bf16[2,160,1280]{2,1,0:T(8,128)(2,1)} %get-tuple-element.153.refs_12_.refs_3_), channel_id=1, source_target_pairs={{0,8},{4,12},{8,0},{12,4},{16,24},{20,28},{24,16},{28,20},{1,9},{5... | collective-permute-start | bytes 2457608 | tf_op jit(solution)/shard_map/ppermute | solution.py:1026
  260.2 29.3 %collective-permute-start.7 = (bf16[2,160,1280]{2,1,0:T(8,128)(2,1)}, bf16[2,160,1280]{2,1,0:T(8,128)(2,1)}, u32[]{:S(2)}, u32[]{:S(2)}) collective-permute-start(bf16[2,160,1280]{2,1,0:T(8,128)(2,1)} %get-tuple-element.153.refs_12_.refs_3_), channel_id=1, source_target_pairs={{0,16},{4,20},{8,24},{12,28},{16,0},{20,4},{24,8},{28,12},{1,17},{... | collective-permute-start | bytes 2457608 | tf_op jit(solution)/shard_map/ppermute | solution.py:1026
  262.0 27.6 %collective-permute-start.4 = (bf16[1,160,1280]{2,1,0:T(8,128)(2,1)S(1)}, bf16[1,160,1280]{2,1,0:T(8,128)(2,1)}, u32[]{:S(2)}, u32[]{:S(2)}) collective-permute-start(bf16[1,160,1280]{2,1,0:T(8,128)(2,1)S(1)} %slice.322), channel_id=1, source_target_pairs={{0,16},{4,20},{8,24},{12,28},{16,0},{20,4},{24,8},{28,12},{1,17},{... | collective-permute-start | bytes 1228808 | tf_op jit(solution)/shard_map/ppermute | solution.py:1026
  264.4 4.8 copy-start.6
  264.4 25.2 %collective-permute-start.5 = (bf16[1,160,1280]{2,1,0:T(8,128)(2,1)S(1)}, bf16[1,160,1280]{2,1,0:T(8,128)(2,1)}, u32[]{:S(2)}, u32[]{:S(2)}) collective-permute-start(bf16[1,160,1280]{2,1,0:T(8,128)(2,1)S(1)} %slice.323), channel_id=1, source_target_pairs={{0,8},{4,12},{8,0},{12,4},{16,24},{20,28},{24,16},{28,20},{1,9},{5... | collective-permute-start | bytes 1228808 | tf_op jit(solution)/shard_map/ppermute | solution.py:1026
  351.1 68.3 %copy-start.10 = (bf16[320,1024]{1,0:T(8,128)(2,1)S(1)}, bf16[320,1024]{1,0:T(8,128)(2,1)}, u32[]{:S(2)}) copy-start(bf16[320,1024]{1,0:T(8,128)(2,1)} %copy-done.9) | copy-start | bytes 1966084
  419.5 4.4 copy-start.2
  419.5 4.4 copy-start.3
  419.5 4.4 copy-start.12
  423.8 14.2 %copy-start.46 = (bf16[1024,1280]{1,0:T(8,128)(2,1)S(1)}, bf16[1024,1280]{1,0:T(8,128)(2,1)}, u32[]{:S(2)}) copy-start(bf16[1024,1280]{1,0:T(8,128)(2,1)} %get-tuple-element.170) | copy-start | bytes 7864324
  437.7 4.7 copy-start.1
  438.0 4.3 copy-start.50
  442.4 5.1 copy-start.49
  442.4 5.1 copy-start.53
  452.5 99.9 %copy-start.8 = (bf16[320,1024]{1,0:T(8,128)(2,1)S(1)}, bf16[320,1024]{1,0:T(8,128)(2,1)}, u32[]{:S(2)}) copy-start(bf16[320,1024]{1,0:T(8,128)(2,1)} %copy-done.7) | copy-start | bytes 1966084
  552.4 4.4 copy-start.48
  552.4 4.4 copy-start.52
  556.8 5.1 copy-start.47
  556.8 5.1 copy-start.51
  561.9 5.1 copy-start.5
  561.9 5.1 copy-start.11
  566.9 13.8 %copy-start.45 = (bf16[1024,1280]{1,0:T(8,128)(2,1)S(1)}, bf16[1024,1280]{1,0:T(8,128)(2,1)}, u32[]{:S(2)}) copy-start(bf16[1024,1280]{1,0:T(8,128)(2,1)} %get-tuple-element.186) | copy-start | bytes 7864324
  580.4 4.6 copy-start
  584.9 123.2 %copy-start.27 = (f32[8,1280]{1,0:T(8,128)S(1)}, f32[8,1280]{1,0:T(8,128)}, u32[]{:S(2)}) copy-start(f32[8,1280]{1,0:T(8,128)} %get-tuple-element.192) | copy-start | bytes 122884
  585.0 123.2 %copy-start.28 = (f32[8,1280]{1,0:T(8,128)S(1)}, f32[8,1280]{1,0:T(8,128)}, u32[]{:S(2)}) copy-start(f32[8,1280]{1,0:T(8,128)} %get-tuple-element.193) | copy-start | bytes 122884
  707.3 4.3 copy-start.30
  707.3 4.3 copy-start.31
  707.3 10.2 %copy-start.19 = (f32[160,1280]{1,0:T(8,128)S(1)}, f32[160,1280]{1,0:T(8,128)}, u32[]{:S(2)}) copy-start(f32[160,1280]{1,0:T(8,128)} %get-tuple-element.203) | copy-start | bytes 2457604
  711.4 9.3 %copy-start.17 = (f32[160,1280]{1,0:T(8,128)S(1)}, f32[160,1280]{1,0:T(8,128)}, u32[]{:S(2)}) copy-start(f32[160,1280]{1,0:T(8,128)} %get-tuple-element.201) | copy-start | bytes 2457604
  711.4 9.3 %copy-start.18 = (f32[160,1280]{1,0:T(8,128)S(1)}, f32[160,1280]{1,0:T(8,128)}, u32[]{:S(2)}) copy-start(f32[160,1280]{1,0:T(8,128)} %get-tuple-element.200) | copy-start | bytes 2457604
  712.0 4.4 collective-permute-start.8
  716.5 4.0 collective-permute-start.9
  717.5 4.5 copy-start.21
  720.6 2.2 collective-permute-start.10
  722.4 5.2 copy-start.25
  722.4 5.2 copy-start.26
  722.8 4.6 collective-permute-start.11
  723.4 6.3 copy-start.23
  727.5 4.4 collective-permute-start.12
  (20 other events, 58.3 us)

commit v5 on v4

--- a/solution.py
+++ b/solution.py
@@ -99,18 +99,30 @@
             def _():
                 keys = tiles(k_at)
                 bias = tile_bias(code_col, code_row, keys, queries)
-                for head in range(heads):
-                    q_base, v_base = head * HD, (2 * heads + head) * HD
-                    scores = mat(k_rows[head, keys, :], qkv[q_base : q_base + HD, queries]) + bias
-                    old = top[head]
-                    new = jnp.maximum(old, jnp.max(scores, axis=0, keepdims=True))
-                    chance = jnp.exp2((scores - new) * SCORE_SCALE)
-                    fade = jnp.exp2((old - new) * SCORE_SCALE)
-                    top[head] = new
-                    total[head] = total[head] * fade + jnp.sum(chance, axis=0, keepdims=True)
-                    acc[head] = acc[head] * fade + mat(
-                        qkv[v_base : v_base + HD, keys], chance.astype(BF16)
+                every = range(heads)
+                scores = [
+                    mat(k_rows[head, keys, :], qkv[head * HD : (head + 1) * HD, queries]) + bias
+                    for head in every
+                ]
+                old = [top[head] for head in every]
+                new = [
+                    jnp.maximum(old[head], jnp.max(scores[head], axis=0, keepdims=True))
+                    for head in every
+                ]
+                chance = [jnp.exp2((scores[head] - new[head]) * SCORE_SCALE) for head in every]
+                fade = [jnp.exp2((old[head] - new[head]) * SCORE_SCALE) for head in every]
+                added = [jnp.sum(chance[head], axis=0, keepdims=True) for head in every]
+                products = [
+                    mat(
+                        qkv[(2 * heads + head) * HD : (2 * heads + head + 1) * HD, keys],
+                        chance[head].astype(BF16),
                     )
+                    for head in every
+                ]
+                for head in every:
+                    top[head] = new[head]
+                    total[head] = total[head] * fade[head] + added[head]
+                    acc[head] = acc[head] * fade[head] + products[head]
 
             return carry
 
@@ -146,16 +158,28 @@
             def _():
                 keys = tiles(k_at)
                 bias = tile_bias(code_col, code_row, keys, queries)
-                for head in range(heads):
-                    rows = slice(head * HD, (head + 1) * HD)
-                    k_base = (heads + head) * HD
-                    scores = mat(k_rows[head, keys, :], qkv[rows, queries]) + bias
-                    chance = jnp.exp2(scores * SCORE_SCALE - log_sum[head, :, queries])
-                    grad_chance = mat(v_rows[head, keys, :], grad_mixed[rows, queries])
-                    grad_score = (chance * (grad_chance - centre[head, :, queries])).astype(BF16)
-                    grad_v[head, :, keys] += mat_turned(grad_mixed[rows, queries], chance.astype(BF16))
-                    grad_k[head, :, keys] += mat_turned(qkv[rows, queries], grad_score)
-                    grad_q[head, :, queries] += mat(qkv[k_base : k_base + HD, keys], grad_score)
+                every = range(heads)
+                rows = [slice(head * HD, (head + 1) * HD) for head in every]
+                scores = [mat(k_rows[h, keys, :], qkv[rows[h], queries]) + bias for h in every]
+                raised = [mat(v_rows[h, keys, :], grad_mixed[rows[h], queries]) for h in every]
+                chance = [
+                    jnp.exp2(scores[h] * SCORE_SCALE - log_sum[h, :, queries]) for h in every
+                ]
+                pulled = [
+                    (chance[h] * (raised[h] - centre[h, :, queries])).astype(BF16) for h in every
+                ]
+                for_v = [
+                    mat_turned(grad_mixed[rows[h], queries], chance[h].astype(BF16)) for h in every
+                ]
+                for_k = [mat_turned(qkv[rows[h], queries], pulled[h]) for h in every]
+                for_q = [
+                    mat(qkv[(heads + h) * HD : (heads + h + 1) * HD, keys], pulled[h])
+                    for h in every
+                ]
+                for h in every:
+                    grad_v[h, :, keys] += for_v[h]
+                    grad_k[h, :, keys] += for_k[h]
+                    grad_q[h, :, queries] += for_q[h]
 
             return carry
 
@@ -655,7 +679,7 @@
                 begin += size
             return carry
 
-        lax.fori_loop(0, width // STRIP, strip, 0)
+        lax.fori_loop(0, width // STRIP, strip, 0, unroll=True)
 
     def put(target, index):
         def store(columns, result):
@@ -807,7 +831,7 @@
                         slope[chunk(*piece), columns] = tilt[at_rows]
                 return carry
 
-            lax.fori_loop(0, units // STRIP, strip, 0)
+            lax.fori_loop(0, units // STRIP, strip, 0, unroll=True)
 
         def acting(pieces):
             return joined([act[chunk(*piece), :] for piece in pieces])
@@ -1177,13 +1201,13 @@
                     8: ((PROJ, 0, 3),),
                 },
                 (FORWARD, 0): {
-                    0: ((DOWN, 0, 3), (QKV, 1, 1)),
-                    2: ((PROJ, 1, 1),),
+                    0: ((DOWN, 0, 2), (QKV, 1, 1)),
+                    2: ((DOWN, 0, 3), (PROJ, 1, 1)),
                     4: ((QKV, 1, 2), (PROJ, 1, 2), (UP, 1, 1)),
                     6: ((QKV, 1, 3), (PROJ, 1, 3)),
                 },
                 (LEAVE, 1): {0: ((UP, 1, 2), (DOWN, 1, 1))},
-                (FORWARD, 1): {0: ((DOWN, 1, 3),)},
+                (FORWARD, 1): {0: ((DOWN, 1, 2),), 2: ((DOWN, 1, 3),)},
                 (BACKWARD, 0): {
                     0: ((UP, 1, 4), (DOWN, 1, 4)),
                     1: ((UP, 1, 5),),
@@ -1327,11 +1351,9 @@
             if not balanced:
                 return
             low, high = high_bits
-            up, down = (UP, layer), (DOWN, layer)
+            up = (UP, layer)
             packs[up, ONE] = across(packs[up, LOW][:1], high)
             packs[up, OTHER] = across(packs[up, HIGH][1:], low)
-            packs[down, LOW] = across(packs[down, PAIR], low)
-            packs[down, HIGH] = across(packs[down, PAIR], high)
 
         hidden, wide_all, qkv_bias_mine, up_bias_mine, facts = lax.optimization_barrier(
             (hidden, wide_all, qkv_bias_mine, up_bias_mine, facts)

time: 748 us -> 707 us (0.945)
  Pallas kernels: 610 us -> 588 us
  waiting for transfers between devices: 21.6 us -> 7.9 us
    ppermute x11 -> x7, waiting for transfers between devices: 17.5 us -> 3.82 us  [across(): return lax.ppermute(value, 'dp', [(i, i ^ bit) for i in range(dp)])]
    pallas_call x2, Pallas kernels: 26.3 us -> 15.7 us  [attend_forward(): pl.pallas_call(forward_kernel, name='attend_forward', out_shape=(jax.Shap...]
  transfers between devices with their start and end apart: 13 -> 9, of which waited for: 5 -> 3; matrix products, arithmetic and copies ran while one was open for 3% -> 2% of each run, Pallas kernels for 4% -> 2%
where the time goes in v5:
time: 707 us; the launch traced here: 698 us
  Pallas kernels  588 us (83%)
  matrix products  46 us (7%)
  local copies, waits for them, and re-layouts  31.5 us (4%)
  other arithmetic  15.5 us (2%)
  waiting for transfers between devices  7.9 us (1%)
    pallas_call x7, Pallas kernels, chain_call(): pl.pallas_call(functools.partial(chain_kernel, stages, backward, names, p...  492 us
    pallas_call x1, Pallas kernels, start_call(): pl.pallas_call(functools.partial(start_kernel, jobs, names), name='start_...  60.5 us
    dot_general x12, matrix products, dot(): lax.dot_general(left, right, (((left_dim,), (right_dim,)), ((), ())), pre...  46 us
    pallas_call x2, Pallas kernels, attend_backward(): pl.pallas_call(backward_kernel, name='attend_backward', out_shape=jax.Sha...  20.4 us
    pallas_call x2, Pallas kernels, attend_forward(): pl.pallas_call(forward_kernel, name='attend_forward', out_shape=(jax.Shap...  15.7 us
  transfers between devices with their start and end apart: 9, of which 3 were waited for; matrix products, arithmetic and copies ran while one was open for 2% of the time, Pallas kernels for 2%

profile of v5, /device:TPU:0, one launch (start us, length us, event | category | flops | bytes accessed | tf_op | source)
XLA Modules:
  0.0 698.1 jit_solution(7402981817455479468)
XLA Ops:
  0.7 1.3 slice_bitcast_fusion.4
  2.3 1.1 reshape.188.refs_17_
  3.4 0.9 slice_bitcast_fusion.1
  6.3 1.1 reshape.198.refs_3_
  7.4 0.9 slice_bitcast_fusion
  10.4 60.5 %start_exchange.1 = (bf16[256,1280]{1,0:T(8,128)(2,1)}, s32[8,1024]{1,0:T(8,128)}, f32[32,16,128]{2,1,0:T(8,128)}, bf16[2,160,960]{2,1,0:T(8,128)(2,1)}, bf16[2,...) custom-call(bf16[256,1280]{1,0:T(8,128)(2,1)} %convert_element_type., ...), custom_call_target="tpu_custom_call" | custom-call | bytes 67108864 | tf_op jit(solution)/shard_map/start_exchange/pallas_call | solution.py:593
  70.9 1.3 fusion.9
  75.7 2.2 fusion.4
  77.9 2.6 fusion.3.refs_0_.refs_6_
  80.5 1.3 fusion.12
  83.1 39.1 %chain_forward.4 = (bf16[2,160,1280]{2,1,0:T(8,128)(2,1)}, bf16[2,160,1280]{2,1,0:T(8,128)(2,1)}, bf16[2,160,320]{2,1,0:T(8,128)(2,1)}, bf16[2,160,320]{2,1,0:T(...) custom-call(f32[256,1280]{1,0:T(8,128)} %fusion.3.refs_0_.refs_6_, ...), custom_call_target="tpu_custom_call" | custom-call | flops 2516582400 | bytes 16777216 | tf_op jit(solution)/shard_map/chain_forward/pallas_call | solution.py:1025
  122.3 1.0 slice.305
  123.3 1.6 collective-permute-start
  124.9 1.0 slice.306
  127.0 1.5 copy-done.4
  128.5 7.8 %attend_forward.2 = (bf16[320,1024]{1,0:T(8,128)(2,1)S(1)}, f32[4,1,1024]{2,1,0:T(1,128)S(1)}) custom-call(s32[16]{0:T(128)S(1)} %reshape.214.active, bf16[960,1024]{1,0:T(8,128)(2,1)S(1)} %copy-done.4, s32[1,1024]{1,0:T(1,128)S(1)} %get-tuple-element.130.code_row, s32[1024,1]{1,0:T(8,128)S(1)} %copy.59.code_col), custom_call_target="tpu_custom_call" | custom-call | flops 1342177280 | bytes 4194304 | tf_op jit(solution)/shard_map/attend_forward/pallas_call | solution.py:210
  138.7 73.2 %chain_forward.5 = (bf16[2,160,1280]{2,1,0:T(8,128)(2,1)}, bf16[2,160,1280]{2,1,0:T(8,128)(2,1)}, bf16[2,160,960]{2,1,0:T(8,128)(2,1)}, bf16[2,160,1280]{2,1,0:T...) custom-call(f32[256,1280]{1,0:T(8,128)} %fusion.3.refs_0_.refs_6_, ...), custom_call_target="tpu_custom_call" | custom-call | flops 7549747200 | bytes 33554432 | tf_op jit(solution)/shard_map/chain_forward/pallas_call | solution.py:1025
  212.0 34.6 %chain_forward.6 = (bf16[2,160,1280]{2,1,0:T(8,128)(2,1)}, bf16[2,160,1280]{2,1,0:T(8,128)(2,1)}, bf16[2,160,1280]{2,1,0:T(8,128)(2,1)}, bf16[960,1024]{1,0:T(8,128)(2,1)}, bf16[1024,1280]{1,0:T(8,128)(2,1)}) custom-call(f32[256,1280]{1,0:T(8,128)} %get-tuple-element.142.refs_0_.refs_6_, bf16[2,160,960]{2,1,0:T(8,128)(2,1)} %get-tuple-element.143.refs_1_.refs_2_, ...), custom_call_target="tpu_custom_call" | custom-call | flops 2516582400 | bytes 16777216 | tf_op jit(solution)/shard_map/chain_forward/pallas_call | solution.py:1025
  246.6 1.1 slice.322
  247.7 1.1 collective-permute-start.2
  248.8 1.0 slice.323
  249.8 1.0 collective-permute-start.3
  250.9 3.1 fusion.1.refs_2_.refs_8_
  254.8 7.8 %attend_forward.3 = (bf16[320,1024]{1,0:T(8,128)(2,1)S(1)}, f32[4,1,1024]{2,1,0:T(1,128)S(1)}) custom-call(s32[16]{0:T(128)S(1)} %reshape.214.active, bf16[960,1024]{1,0:T(8,128)(2,1)S(1)} %copy-done.6, s32[1,1024]{1,0:T(1,128)S(1)} %get-tuple-element.130.code_row, s32[1024,1]{1,0:T(8,128)S(1)} %copy.59.code_col), custom_call_target="tpu_custom_call" | custom-call | flops 1342177280 | bytes 4194304 | tf_op jit(solution)/shard_map/attend_forward/pallas_call | solution.py:210
  263.5 62.0 %chain_forward.7 = (bf16[2,160,1280]{2,1,0:T(8,128)(2,1)}, bf16[2,160,1280]{2,1,0:T(8,128)(2,1)}, bf16[2,160,1280]{2,1,0:T(8,128)(2,1)}, f32[256,1280]{1,0:T(8,1...) custom-call(f32[256,1280]{1,0:T(8,128)} %get-tuple-element.142.refs_, ...), custom_call_target="tpu_custom_call" | custom-call | flops 7549747200 | bytes 33554432 | tf_op jit(solution)/shard_map/chain_forward/pallas_call | solution.py:1025
  325.6 63.5 %chain_backward.3 = (f32[8,1280]{1,0:T(8,128)}, f32[256,1280]{1,0:T(8,128)}, bf16[1024,1280]{1,0:T(8,128)(2,1)}, bf16[1024,1280]{1,0:T(8,128)(2,1)}, f32[1,1280]...) custom-call(f32[256,1280]{1,0:T(8,128)} %get-tuple-element.158.refs_0_, ...), custom_call_target="tpu_custom_call" | custom-call | flops 7549747200 | bytes 33554432 | tf_op jit(solution)/shard_map/chain_backward/pallas_call | solution.py:1025
  389.1 4.3 convolution_convert_fusion.7.refs_27_.refs_14_
  393.4 10.2 %attend_backward.2.refs_1_ = bf16[960,1024]{1,0:T(8,128)(2,1)S(1)} custom-call(s32[16]{0:T(128)S(1)} %reshape.214.active, bf16[960,1024]{1,0:T(8,128)(2,1)S(1)} %copy-done.6, bf16[320,1024]{1,0:T(8,128)(2,1)S(1)} %copy-done.10, bf16[320,1024]{1,0:T(8,128)(2,1)S(1)} %copy-done.12, f32[4,1,1024]{2,1,0:T(1,128)S(1)} %get-tuple-element.168.log_sum, ...), custom_call_target="tpu_custom_call" | custom-call | flops 3355443200 | bytes 10485760 | tf_op jit(solution)/shard_map/attend_backward/pallas_call | solution.py:238
  404.0 4.3 convolution_convert_fusion.5.refs_26_.refs_11_
  408.4 5.1 convolution_convert_fusion.2.refs_25_
  413.4 5.2 convolution_convert_fusion.3.refs_24_
  418.7 98.6 %chain_backward.4 = (f32[8,1280]{1,0:T(8,128)}, bf16[2,160,1280]{2,1,0:T(8,128)(2,1)}, bf16[2,160,1280]{2,1,0:T(8,128)(2,1)}, bf16[2,160,1280]{2,1,0:T(8,128)(2,...) custom-call(f32[256,1280]{1,0:T(8,128)} %get-tuple-element.166.refs_, ...), custom_call_target="tpu_custom_call" | custom-call | flops 10066329600 | bytes 50331648 | tf_op jit(solution)/shard_map/chain_backward/pallas_call | solution.py:1025
  517.3 4.4 convolution_convert_fusion.6.refs_18_
  521.7 5.1 convolution_convert_fusion.refs_10_
  526.8 5.1 convolution_convert_fusion.1.refs_9_
  531.8 10.2 %attend_backward.3.refs_1_ = bf16[960,1024]{1,0:T(8,128)(2,1)S(1)} custom-call(s32[16]{0:T(128)S(1)} %reshape.214.active, bf16[960,1024]{1,0:T(8,128)(2,1)S(1)} %copy-done.5, bf16[320,1024]{1,0:T(8,128)(2,1)S(1)} %copy-done.8, bf16[320,1024]{1,0:T(8,128)(2,1)S(1)} %copy-done.11, f32[4,1,1024]{2,1,0:T(1,128)S(1)} %get-tuple-element.187.log_sum, ...), custom_call_target="tpu_custom_call" | custom-call | flops 3355443200 | bytes 10485760 | tf_op jit(solution)/shard_map/attend_backward/pallas_call | solution.py:238
  542.4 4.2 convolution_convert_fusion.4.refs_17_
  546.6 121.0 %chain_backward.5 = (f32[8,1280]{1,0:T(8,128)}, bf16[2,160,1280]{2,1,0:T(8,128)(2,1)}, bf16[2,160,1280]{2,1,0:T(8,128)(2,1)}, bf16[2,160,1280]{2,1,0:T(8,128)(2,...) custom-call(f32[256,1280]{1,0:T(8,128)} %get-tuple-element.180.refs_, ...), custom_call_target="tpu_custom_call" | custom-call | flops 2516582400 | bytes 16777216 | tf_op jit(solution)/shard_map/chain_backward/pallas_call | solution.py:1025
  668.7 2.1 fusion
  672.6 1.1 collective-permute-start.4
  673.6 3.3 collective-permute-done.4
  677.1 1.1 collective-permute-start.5
  678.2 2.5 pad_maximum_fusion.2
  681.2 1.3 pad_maximum_fusion.1
  683.9 4.1 collective-permute-done.7
  688.9 1.2 copy.65
  690.1 1.1 convert_element_type.80
  691.3 1.1 convert_element_type.71
  (215 shorter events, 25.7 us)
Async XLA Ops:
  0.7 4.4 copy-start.13
  5.1 4.1 copy-start.40
  5.1 4.2 copy-start.41
  5.2 4.3 copy-start.42
  5.2 4.4 copy-start.43
  5.2 4.4 copy-start.44
  70.9 7.0 %copy-start.36 = (bf16[256,1280]{1,0:T(8,128)(2,1)S(1)}, bf16[256,1280]{1,0:T(8,128)(2,1)}, u32[]{:S(2)}) copy-start(bf16[256,1280]{1,0:T(8,128)(2,1)} %get-tuple-element.114) | copy-start | bytes 1966084
  123.3 14.5 %collective-permute-start = (bf16[1,160,1280]{2,1,0:T(8,128)(2,1)S(1)}, bf16[1,160,1280]{2,1,0:T(8,128)(2,1)S(1)}, u32[]{:S(2)}, u32[]{:S(2)}) collective-permute-start(bf16[1,160,1280]{2,1,0:T(8,128)(2,1)S(1)} %slice.305), channel_id=1, source_target_pairs={{0,16},{4,20},{8,24},{12,28},{16,0},{20,4},{24,8},{28,12},{1,17},{... | collective-permute-start | bytes 1228808 | tf_op jit(solution)/shard_map/ppermute | solution.py:1050
  125.9 11.9 %collective-permute-start.1 = (bf16[1,160,1280]{2,1,0:T(8,128)(2,1)S(1)}, bf16[1,160,1280]{2,1,0:T(8,128)(2,1)S(1)}, u32[]{:S(2)}, u32[]{:S(2)}) collective-permute-start(bf16[1,160,1280]{2,1,0:T(8,128)(2,1)S(1)} %slice.306), channel_id=1, source_target_pairs={{0,8},{4,12},{8,0},{12,4},{16,24},{20,28},{24,16},{28,20},{1,9},{5... | collective-permute-start | bytes 1228808 | tf_op jit(solution)/shard_map/ppermute | solution.py:1050
  246.5 7.4 %copy-start.14 = (f32[256,1280]{1,0:T(8,128)S(1)}, f32[256,1280]{1,0:T(8,128)}, u32[]{:S(2)}) copy-start(f32[256,1280]{1,0:T(8,128)} %param.33) | copy-start | bytes 3932164
  247.7 15.8 %collective-permute-start.2 = (bf16[1,160,1280]{2,1,0:T(8,128)(2,1)S(1)}, bf16[1,160,1280]{2,1,0:T(8,128)(2,1)}, u32[]{:S(2)}, u32[]{:S(2)}) collective-permute-start(bf16[1,160,1280]{2,1,0:T(8,128)(2,1)S(1)} %slice.322), channel_id=1, source_target_pairs={{0,16},{4,20},{8,24},{12,28},{16,0},{20,4},{24,8},{28,12},{1,17},{... | collective-permute-start | bytes 1228808 | tf_op jit(solution)/shard_map/ppermute | solution.py:1050
  249.8 5.0 copy-start.6
  249.8 13.7 %collective-permute-start.3 = (bf16[1,160,1280]{2,1,0:T(8,128)(2,1)S(1)}, bf16[1,160,1280]{2,1,0:T(8,128)(2,1)}, u32[]{:S(2)}, u32[]{:S(2)}) collective-permute-start(bf16[1,160,1280]{2,1,0:T(8,128)(2,1)S(1)} %slice.323), channel_id=1, source_target_pairs={{0,8},{4,12},{8,0},{12,4},{16,24},{20,28},{24,16},{28,20},{1,9},{5... | collective-permute-start | bytes 1228808 | tf_op jit(solution)/shard_map/ppermute | solution.py:1050
  325.6 63.5 %copy-start.10 = (bf16[320,1024]{1,0:T(8,128)(2,1)S(1)}, bf16[320,1024]{1,0:T(8,128)(2,1)}, u32[]{:S(2)}) copy-start(bf16[320,1024]{1,0:T(8,128)(2,1)} %copy-done.9) | copy-start | bytes 1966084
  389.1 4.4 copy-start.2
  389.1 4.4 copy-start.3
  389.1 4.4 copy-start.12
  393.4 10.5 %copy-start.46 = (bf16[1024,1280]{1,0:T(8,128)(2,1)S(1)}, bf16[1024,1280]{1,0:T(8,128)(2,1)}, u32[]{:S(2)}) copy-start(bf16[1024,1280]{1,0:T(8,128)(2,1)} %get-tuple-element.178) | copy-start | bytes 7864324
  403.6 4.7 copy-start.1
  404.0 4.3 copy-start.50
  404.0 4.3 copy-start.54
  408.3 5.1 copy-start.49
  408.4 5.1 copy-start.53
  418.7 98.6 %copy-start.8 = (bf16[320,1024]{1,0:T(8,128)(2,1)S(1)}, bf16[320,1024]{1,0:T(8,128)(2,1)}, u32[]{:S(2)}) copy-start(bf16[320,1024]{1,0:T(8,128)(2,1)} %copy-done.7) | copy-start | bytes 1966084
  517.3 4.4 copy-start.48
  517.3 4.4 copy-start.52
  521.7 5.1 copy-start.47
  521.7 5.1 copy-start.51
  526.8 5.1 copy-start.5
  526.8 5.1 copy-start.11
  531.8 10.5 %copy-start.45 = (bf16[1024,1280]{1,0:T(8,128)(2,1)S(1)}, bf16[1024,1280]{1,0:T(8,128)(2,1)}, u32[]{:S(2)}) copy-start(bf16[1024,1280]{1,0:T(8,128)(2,1)} %get-tuple-element.194) | copy-start | bytes 7864324
  542.0 4.6 copy-start
  546.6 121.9 %copy-start.27 = (f32[8,1280]{1,0:T(8,128)S(1)}, f32[8,1280]{1,0:T(8,128)}, u32[]{:S(2)}) copy-start(f32[8,1280]{1,0:T(8,128)} %get-tuple-element.200) | copy-start | bytes 122884
  546.6 121.9 %copy-start.28 = (f32[8,1280]{1,0:T(8,128)S(1)}, f32[8,1280]{1,0:T(8,128)}, u32[]{:S(2)}) copy-start(f32[8,1280]{1,0:T(8,128)} %get-tuple-element.201) | copy-start | bytes 122884
  667.6 4.6 copy-start.30
  667.6 4.6 copy-start.31
  667.6 10.5 %copy-start.19 = (f32[160,1280]{1,0:T(8,128)S(1)}, f32[160,1280]{1,0:T(8,128)}, u32[]{:S(2)}) copy-start(f32[160,1280]{1,0:T(8,128)} %get-tuple-element.211) | copy-start | bytes 2457604
  672.0 9.3 %copy-start.17 = (f32[160,1280]{1,0:T(8,128)S(1)}, f32[160,1280]{1,0:T(8,128)}, u32[]{:S(2)}) copy-start(f32[160,1280]{1,0:T(8,128)} %get-tuple-element.209) | copy-start | bytes 2457604
  672.0 9.3 %copy-start.18 = (f32[160,1280]{1,0:T(8,128)S(1)}, f32[160,1280]{1,0:T(8,128)}, u32[]{:S(2)}) copy-start(f32[160,1280]{1,0:T(8,128)} %get-tuple-element.208) | copy-start | bytes 2457604
  672.6 4.4 collective-permute-start.4
  677.1 4.0 collective-permute-start.5
  678.2 4.3 copy-start.21
  681.1 2.2 collective-permute-start.6
  682.9 5.2 copy-start.25
  682.9 5.2 copy-start.26
  683.3 4.6 collective-permute-start.7
  683.9 6.3 copy-start.23
  688.0 4.4 collective-permute-start.8
  (16 other events, 40.8 us)

commit v6 on v5

--- a/solution.py
+++ b/solution.py
@@ -1197,7 +1197,8 @@
             packed = arranged(begun[VECTORS_HBM].reshape(count, space))[:, : packed.shape[0]]
             schedule = {
                 (LEAVE, 0): {
-                    0: ((UP, 0, 2), (PROJ, 0, 2), (DOWN, 0, 1)),
+                    0: ((UP, 0, 2), (PROJ, 0, 2)),
+                    7: ((DOWN, 0, 1),),
                     8: ((PROJ, 0, 3),),
                 },
                 (FORWARD, 0): {
@@ -1206,7 +1207,7 @@
                     4: ((QKV, 1, 2), (PROJ, 1, 2), (UP, 1, 1)),
                     6: ((QKV, 1, 3), (PROJ, 1, 3)),
                 },
-                (LEAVE, 1): {0: ((UP, 1, 2), (DOWN, 1, 1))},
+                (LEAVE, 1): {0: ((UP, 1, 2),), 7: ((DOWN, 1, 1),)},
                 (FORWARD, 1): {0: ((DOWN, 1, 2),), 2: ((DOWN, 1, 3),)},
                 (BACKWARD, 0): {
                     0: ((UP, 1, 4), (DOWN, 1, 4)),

time: 707 us -> 709 us (level)
  no operation moved by 1% of the time
where the time goes in v6:
time: 709 us; the launch traced here: 702 us
  Pallas kernels  592 us (83%)
  matrix products  46 us (6%)
  local copies, waits for them, and re-layouts  31.5 us (4%)
  other arithmetic  15.5 us (2%)
  waiting for transfers between devices  7.45 us (1%)
  starting transfers between devices  7.38 us (1%)
    pallas_call x7, Pallas kernels, chain_call(): pl.pallas_call(functools.partial(chain_kernel, stages, backward, names, p...  496 us
    pallas_call x1, Pallas kernels, start_call(): pl.pallas_call(functools.partial(start_kernel, jobs, names), name='start_...  60.5 us
    dot_general x12, matrix products, dot(): lax.dot_general(left, right, (((left_dim,), (right_dim,)), ((), ())), pre...  46 us
    pallas_call x2, Pallas kernels, attend_backward(): pl.pallas_call(backward_kernel, name='attend_backward', out_shape=jax.Sha...  20.4 us
    pallas_call x2, Pallas kernels, attend_forward(): pl.pallas_call(forward_kernel, name='attend_forward', out_shape=(jax.Shap...  15.7 us
  transfers between devices with their start and end apart: 9, of which 3 were waited for; matrix products, arithmetic and copies ran while one was open for 2% of the time, Pallas kernels for 2%

profile of v6, /device:TPU:0, one launch (start us, length us, event | category | flops | bytes accessed | tf_op | source)
XLA Modules:
  0.0 702.0 jit_solution(14194303062865356509)
XLA Ops:
  0.7 1.3 slice_bitcast_fusion.4
  2.3 1.1 reshape.188.refs_17_
  3.4 0.9 slice_bitcast_fusion.1
  5.2 0.9 convert_element_type.64.refs_0_
  6.3 1.1 reshape.198.refs_3_
  7.4 0.9 slice_bitcast_fusion
  10.4 60.5 %start_exchange.1 = (bf16[256,1280]{1,0:T(8,128)(2,1)}, s32[8,1024]{1,0:T(8,128)}, f32[32,16,128]{2,1,0:T(8,128)}, bf16[2,160,960]{2,1,0:T(8,128)(2,1)}, bf16[2,...) custom-call(bf16[256,1280]{1,0:T(8,128)(2,1)} %convert_element_type., ...), custom_call_target="tpu_custom_call" | custom-call | bytes 67108864 | tf_op jit(solution)/shard_map/start_exchange/pallas_call | solution.py:593
  70.9 1.3 fusion.9
  75.7 2.2 fusion.4
  77.9 2.6 fusion.3.refs_0_.refs_6_
  80.5 1.3 fusion.12
  83.1 39.1 %chain_forward.4 = (bf16[2,160,1280]{2,1,0:T(8,128)(2,1)}, bf16[2,160,1280]{2,1,0:T(8,128)(2,1)}, bf16[2,160,320]{2,1,0:T(8,128)(2,1)}, bf16[2,160,320]{2,1,0:T(...) custom-call(f32[256,1280]{1,0:T(8,128)} %fusion.3.refs_0_.refs_6_, ...), custom_call_target="tpu_custom_call" | custom-call | flops 2516582400 | bytes 16777216 | tf_op jit(solution)/shard_map/chain_forward/pallas_call | solution.py:1025
  122.3 1.0 slice.305
  123.3 1.6 collective-permute-start
  124.9 1.0 slice.306
  127.0 1.5 copy-done.4
  128.5 7.8 %attend_forward.2 = (bf16[320,1024]{1,0:T(8,128)(2,1)S(1)}, f32[4,1,1024]{2,1,0:T(1,128)S(1)}) custom-call(s32[16]{0:T(128)S(1)} %reshape.214.active, bf16[960,1024]{1,0:T(8,128)(2,1)S(1)} %copy-done.4, s32[1,1024]{1,0:T(1,128)S(1)} %get-tuple-element.130.code_row, s32[1024,1]{1,0:T(8,128)S(1)} %copy.59.code_col), custom_call_target="tpu_custom_call" | custom-call | flops 1342177280 | bytes 4194304 | tf_op jit(solution)/shard_map/attend_forward/pallas_call | solution.py:210
  138.7 73.2 %chain_forward.5 = (bf16[2,160,1280]{2,1,0:T(8,128)(2,1)}, bf16[2,160,1280]{2,1,0:T(8,128)(2,1)}, bf16[2,160,960]{2,1,0:T(8,128)(2,1)}, bf16[2,160,1280]{2,1,0:T...) custom-call(f32[256,1280]{1,0:T(8,128)} %fusion.3.refs_0_.refs_6_, ...), custom_call_target="tpu_custom_call" | custom-call | flops 7549747200 | bytes 33554432 | tf_op jit(solution)/shard_map/chain_forward/pallas_call | solution.py:1025
  212.0 36.3 %chain_forward.6 = (bf16[2,160,1280]{2,1,0:T(8,128)(2,1)}, bf16[2,160,1280]{2,1,0:T(8,128)(2,1)}, bf16[2,160,1280]{2,1,0:T(8,128)(2,1)}, bf16[960,1024]{1,0:T(8,128)(2,1)}, bf16[1024,1280]{1,0:T(8,128)(2,1)}) custom-call(f32[256,1280]{1,0:T(8,128)} %get-tuple-element.142.refs_0_.refs_6_, bf16[2,160,960]{2,1,0:T(8,128)(2,1)} %get-tuple-element.143.refs_1_.refs_2_, ...), custom_call_target="tpu_custom_call" | custom-call | flops 2516582400 | bytes 16777216 | tf_op jit(solution)/shard_map/chain_forward/pallas_call | solution.py:1025
  248.3 1.1 slice.322
  249.4 1.3 collective-permute-start.2
  250.7 1.0 slice.323
  252.6 3.1 fusion.1.refs_2_.refs_8_
  256.6 7.8 %attend_forward.3 = (bf16[320,1024]{1,0:T(8,128)(2,1)S(1)}, f32[4,1,1024]{2,1,0:T(1,128)S(1)}) custom-call(s32[16]{0:T(128)S(1)} %reshape.214.active, bf16[960,1024]{1,0:T(8,128)(2,1)S(1)} %copy-done.6, s32[1,1024]{1,0:T(1,128)S(1)} %get-tuple-element.130.code_row, s32[1024,1]{1,0:T(8,128)S(1)} %copy.59.code_col), custom_call_target="tpu_custom_call" | custom-call | flops 1342177280 | bytes 4194304 | tf_op jit(solution)/shard_map/attend_forward/pallas_call | solution.py:210
  265.3 64.4 %chain_forward.7 = (bf16[2,160,1280]{2,1,0:T(8,128)(2,1)}, bf16[2,160,1280]{2,1,0:T(8,128)(2,1)}, bf16[2,160,1280]{2,1,0:T(8,128)(2,1)}, f32[256,1280]{1,0:T(8,1...) custom-call(f32[256,1280]{1,0:T(8,128)} %get-tuple-element.142.refs_, ...), custom_call_target="tpu_custom_call" | custom-call | flops 7549747200 | bytes 33554432 | tf_op jit(solution)/shard_map/chain_forward/pallas_call | solution.py:1025
  329.6 63.4 %chain_backward.3 = (f32[8,1280]{1,0:T(8,128)}, f32[256,1280]{1,0:T(8,128)}, bf16[1024,1280]{1,0:T(8,128)(2,1)}, bf16[1024,1280]{1,0:T(8,128)(2,1)}, f32[1,1280]...) custom-call(f32[256,1280]{1,0:T(8,128)} %get-tuple-element.158.refs_0_, ...), custom_call_target="tpu_custom_call" | custom-call | flops 7549747200 | bytes 33554432 | tf_op jit(solution)/shard_map/chain_backward/pallas_call | solution.py:1025
  393.0 4.3 convolution_convert_fusion.7.refs_27_.refs_14_
  397.4 10.2 %attend_backward.2.refs_1_ = bf16[960,1024]{1,0:T(8,128)(2,1)S(1)} custom-call(s32[16]{0:T(128)S(1)} %reshape.214.active, bf16[960,1024]{1,0:T(8,128)(2,1)S(1)} %copy-done.6, bf16[320,1024]{1,0:T(8,128)(2,1)S(1)} %copy-done.10, bf16[320,1024]{1,0:T(8,128)(2,1)S(1)} %copy-done.12, f32[4,1,1024]{2,1,0:T(1,128)S(1)} %get-tuple-element.168.log_sum, ...), custom_call_target="tpu_custom_call" | custom-call | flops 3355443200 | bytes 10485760 | tf_op jit(solution)/shard_map/attend_backward/pallas_call | solution.py:238
  408.0 4.3 convolution_convert_fusion.5.refs_26_.refs_11_
  412.3 5.1 convolution_convert_fusion.2.refs_25_
  417.4 5.2 convolution_convert_fusion.3.refs_24_
  422.6 98.7 %chain_backward.4 = (f32[8,1280]{1,0:T(8,128)}, bf16[2,160,1280]{2,1,0:T(8,128)(2,1)}, bf16[2,160,1280]{2,1,0:T(8,128)(2,1)}, bf16[2,160,1280]{2,1,0:T(8,128)(2,...) custom-call(f32[256,1280]{1,0:T(8,128)} %get-tuple-element.166.refs_, ...), custom_call_target="tpu_custom_call" | custom-call | flops 10066329600 | bytes 50331648 | tf_op jit(solution)/shard_map/chain_backward/pallas_call | solution.py:1025
  521.4 4.4 convolution_convert_fusion.6.refs_18_
  525.8 5.1 convolution_convert_fusion.refs_10_
  530.8 5.1 convolution_convert_fusion.1.refs_9_
  535.9 10.2 %attend_backward.3.refs_1_ = bf16[960,1024]{1,0:T(8,128)(2,1)S(1)} custom-call(s32[16]{0:T(128)S(1)} %reshape.214.active, bf16[960,1024]{1,0:T(8,128)(2,1)S(1)} %copy-done.5, bf16[320,1024]{1,0:T(8,128)(2,1)S(1)} %copy-done.8, bf16[320,1024]{1,0:T(8,128)(2,1)S(1)} %copy-done.11, f32[4,1,1024]{2,1,0:T(1,128)S(1)} %get-tuple-element.187.log_sum, ...), custom_call_target="tpu_custom_call" | custom-call | flops 3355443200 | bytes 10485760 | tf_op jit(solution)/shard_map/attend_backward/pallas_call | solution.py:238
  546.4 4.2 convolution_convert_fusion.4.refs_17_
  550.7 120.8 %chain_backward.5 = (f32[8,1280]{1,0:T(8,128)}, bf16[2,160,1280]{2,1,0:T(8,128)(2,1)}, bf16[2,160,1280]{2,1,0:T(8,128)(2,1)}, bf16[2,160,1280]{2,1,0:T(8,128)(2,...) custom-call(f32[256,1280]{1,0:T(8,128)} %get-tuple-element.180.refs_, ...), custom_call_target="tpu_custom_call" | custom-call | flops 2516582400 | bytes 16777216 | tf_op jit(solution)/shard_map/chain_backward/pallas_call | solution.py:1025
  672.6 2.1 fusion
  676.4 1.3 collective-permute-start.4
  677.7 3.1 collective-permute-done.4
  681.0 1.3 collective-permute-start.5
  682.3 2.5 pad_maximum_fusion.2
  685.1 1.3 pad_maximum_fusion.1
  687.8 4.1 collective-permute-done.7
  692.8 1.2 copy.65
  694.0 1.1 convert_element_type.80
  695.2 1.1 convert_element_type.71
  (215 shorter events, 25.5 us)
Async XLA Ops:
  0.7 4.4 copy-start.13
  5.1 4.1 copy-start.40
  5.1 4.2 copy-start.41
  5.2 4.3 copy-start.42
  5.2 4.4 copy-start.43
  5.2 4.4 copy-start.44
  70.9 7.0 copy-start.36
  123.3 14.5 %collective-permute-start = (bf16[1,160,1280]{2,1,0:T(8,128)(2,1)S(1)}, bf16[1,160,1280]{2,1,0:T(8,128)(2,1)S(1)}, u32[]{:S(2)}, u32[]{:S(2)}) collective-permute-start(bf16[1,160,1280]{2,1,0:T(8,128)(2,1)S(1)} %slice.305), channel_id=1, source_target_pairs={{0,16},{4,20},{8,24},{12,28},{16,0},{20,4},{24,8},{28,12},{1,17},{... | collective-permute-start | bytes 1228808 | tf_op jit(solution)/shard_map/ppermute | solution.py:1050
  125.9 11.9 %collective-permute-start.1 = (bf16[1,160,1280]{2,1,0:T(8,128)(2,1)S(1)}, bf16[1,160,1280]{2,1,0:T(8,128)(2,1)S(1)}, u32[]{:S(2)}, u32[]{:S(2)}) collective-permute-start(bf16[1,160,1280]{2,1,0:T(8,128)(2,1)S(1)} %slice.306), channel_id=1, source_target_pairs={{0,8},{4,12},{8,0},{12,4},{16,24},{20,28},{24,16},{28,20},{1,9},{5... | collective-permute-start | bytes 1228808 | tf_op jit(solution)/shard_map/ppermute | solution.py:1050
  248.3 7.4 %copy-start.14 = (f32[256,1280]{1,0:T(8,128)S(1)}, f32[256,1280]{1,0:T(8,128)}, u32[]{:S(2)}) copy-start(f32[256,1280]{1,0:T(8,128)} %param.33) | copy-start | bytes 3932164
  249.4 15.9 %collective-permute-start.2 = (bf16[1,160,1280]{2,1,0:T(8,128)(2,1)S(1)}, bf16[1,160,1280]{2,1,0:T(8,128)(2,1)}, u32[]{:S(2)}, u32[]{:S(2)}) collective-permute-start(bf16[1,160,1280]{2,1,0:T(8,128)(2,1)S(1)} %slice.322), channel_id=1, source_target_pairs={{0,16},{4,20},{8,24},{12,28},{16,0},{20,4},{24,8},{28,12},{1,17},{... | collective-permute-start | bytes 1228808 | tf_op jit(solution)/shard_map/ppermute | solution.py:1050
  251.7 4.9 copy-start.6
  251.7 13.5 %collective-permute-start.3 = (bf16[1,160,1280]{2,1,0:T(8,128)(2,1)S(1)}, bf16[1,160,1280]{2,1,0:T(8,128)(2,1)}, u32[]{:S(2)}, u32[]{:S(2)}) collective-permute-start(bf16[1,160,1280]{2,1,0:T(8,128)(2,1)S(1)} %slice.323), channel_id=1, source_target_pairs={{0,8},{4,12},{8,0},{12,4},{16,24},{20,28},{24,16},{28,20},{1,9},{5... | collective-permute-start | bytes 1228808 | tf_op jit(solution)/shard_map/ppermute | solution.py:1050
  329.6 63.4 %copy-start.10 = (bf16[320,1024]{1,0:T(8,128)(2,1)S(1)}, bf16[320,1024]{1,0:T(8,128)(2,1)}, u32[]{:S(2)}) copy-start(bf16[320,1024]{1,0:T(8,128)(2,1)} %copy-done.9) | copy-start | bytes 1966084
  393.0 4.4 copy-start.2
  393.0 4.4 copy-start.3
  393.0 4.4 copy-start.12
  397.4 10.5 %copy-start.46 = (bf16[1024,1280]{1,0:T(8,128)(2,1)S(1)}, bf16[1024,1280]{1,0:T(8,128)(2,1)}, u32[]{:S(2)}) copy-start(bf16[1024,1280]{1,0:T(8,128)(2,1)} %get-tuple-element.178) | copy-start | bytes 7864324
  407.6 4.7 copy-start.1
  407.9 4.3 copy-start.50
  408.0 4.3 copy-start.54
  412.3 5.1 copy-start.49
  412.3 5.1 copy-start.53
  422.6 98.7 %copy-start.8 = (bf16[320,1024]{1,0:T(8,128)(2,1)S(1)}, bf16[320,1024]{1,0:T(8,128)(2,1)}, u32[]{:S(2)}) copy-start(bf16[320,1024]{1,0:T(8,128)(2,1)} %copy-done.7) | copy-start | bytes 1966084
  521.3 4.4 copy-start.48
  521.3 4.4 copy-start.52
  525.8 5.1 copy-start.47
  525.8 5.1 copy-start.51
  530.8 5.1 copy-start.5
  530.8 5.1 copy-start.11
  535.9 10.5 %copy-start.45 = (bf16[1024,1280]{1,0:T(8,128)(2,1)S(1)}, bf16[1024,1280]{1,0:T(8,128)(2,1)}, u32[]{:S(2)}) copy-start(bf16[1024,1280]{1,0:T(8,128)(2,1)} %get-tuple-element.194) | copy-start | bytes 7864324
  546.1 4.6 copy-start
  550.7 121.7 %copy-start.27 = (f32[8,1280]{1,0:T(8,128)S(1)}, f32[8,1280]{1,0:T(8,128)}, u32[]{:S(2)}) copy-start(f32[8,1280]{1,0:T(8,128)} %get-tuple-element.200) | copy-start | bytes 122884
  550.7 121.7 %copy-start.28 = (f32[8,1280]{1,0:T(8,128)S(1)}, f32[8,1280]{1,0:T(8,128)}, u32[]{:S(2)}) copy-start(f32[8,1280]{1,0:T(8,128)} %get-tuple-element.201) | copy-start | bytes 122884
  671.5 4.6 copy-start.30
  671.5 4.6 copy-start.31
  671.5 10.8 %copy-start.19 = (f32[160,1280]{1,0:T(8,128)S(1)}, f32[160,1280]{1,0:T(8,128)}, u32[]{:S(2)}) copy-start(f32[160,1280]{1,0:T(8,128)} %get-tuple-element.211) | copy-start | bytes 2457604
  675.8 9.3 %copy-start.17 = (f32[160,1280]{1,0:T(8,128)S(1)}, f32[160,1280]{1,0:T(8,128)}, u32[]{:S(2)}) copy-start(f32[160,1280]{1,0:T(8,128)} %get-tuple-element.209) | copy-start | bytes 2457604
  675.8 9.3 %copy-start.18 = (f32[160,1280]{1,0:T(8,128)S(1)}, f32[160,1280]{1,0:T(8,128)}, u32[]{:S(2)}) copy-start(f32[160,1280]{1,0:T(8,128)} %get-tuple-element.208) | copy-start | bytes 2457604
  676.4 4.4 collective-permute-start.4
  681.0 4.0 collective-permute-start.5
  682.3 4.1 copy-start.21
  685.0 2.2 collective-permute-start.6
  686.8 5.2 copy-start.25
  686.8 5.2 copy-start.26
  687.2 4.6 collective-permute-start.7
  687.8 6.3 copy-start.23
  691.9 4.4 collective-permute-start.8
  (16 other events, 40.6 us)

commit v7 on v5

--- a/solution.py
+++ b/solution.py
@@ -822,8 +822,9 @@
                 else:
                     up = up + ref[FIRST_BIAS][:, columns]
                     sigmoid = 1.0 / (1.0 + jnp.exp(-1.702 * up))
-                    out = (up * sigmoid).astype(BF16)
-                    tilt = (sigmoid + 1.702 * up * sigmoid * (1.0 - sigmoid)).astype(BF16)
+                    gated = up * sigmoid
+                    out = gated.astype(BF16)
+                    tilt = (sigmoid + 1.702 * gated * (1.0 - sigmoid)).astype(BF16)
                 for index, piece in enumerate(pieces):
                     at_rows = slice(index * step, (index + 1) * step)
                     act[chunk(*piece), columns] = out[at_rows]

time: 707 us -> 706 us (level)
  no operation moved by 1% of the time
where the time goes in v7:
time: 706 us; the launch traced here: 697 us
  Pallas kernels  587 us (83%)
  matrix products  46 us (7%)
  local copies, waits for them, and re-layouts  31.5 us (4%)
  other arithmetic  15.5 us (2%)
  waiting for transfers between devices  7.9 us (1%)
    pallas_call x7, Pallas kernels, chain_call(): pl.pallas_call(functools.partial(chain_kernel, stages, backward, names, p...  490 us
    pallas_call x1, Pallas kernels, start_call(): pl.pallas_call(functools.partial(start_kernel, jobs, names), name='start_...  60.5 us
    dot_general x12, matrix products, dot(): lax.dot_general(left, right, (((left_dim,), (right_dim,)), ((), ())), pre...  46 us
    pallas_call x2, Pallas kernels, attend_backward(): pl.pallas_call(backward_kernel, name='attend_backward', out_shape=jax.Sha...  20.4 us
    pallas_call x2, Pallas kernels, attend_forward(): pl.pallas_call(forward_kernel, name='attend_forward', out_shape=(jax.Shap...  15.7 us
  transfers between devices with their start and end apart: 9, of which 3 were waited for; matrix products, arithmetic and copies ran while one was open for 2% of the time, Pallas kernels for 2%

profile of v7, /device:TPU:0, one launch (start us, length us, event | category | flops | bytes accessed | tf_op | source)
XLA Modules:
  0.0 696.6 jit_solution(702815437777258942)
XLA Ops:
  0.7 1.3 slice_bitcast_fusion.4
  2.3 1.1 reshape.188.refs_17_
  3.4 0.9 slice_bitcast_fusion.1
  6.3 1.1 reshape.198.refs_3_
  7.4 0.9 slice_bitcast_fusion
  10.4 60.5 %start_exchange.1 = (bf16[256,1280]{1,0:T(8,128)(2,1)}, s32[8,1024]{1,0:T(8,128)}, f32[32,16,128]{2,1,0:T(8,128)}, bf16[2,160,960]{2,1,0:T(8,128)(2,1)}, bf16[2,...) custom-call(bf16[256,1280]{1,0:T(8,128)(2,1)} %convert_element_type., ...), custom_call_target="tpu_custom_call" | custom-call | bytes 67108864 | tf_op jit(solution)/shard_map/start_exchange/pallas_call | solution.py:593
  70.9 1.3 fusion.9
  75.7 2.2 fusion.4
  77.9 2.6 fusion.3.refs_0_.refs_6_
  80.5 1.3 fusion.12
  83.1 39.1 %chain_forward.4 = (bf16[2,160,1280]{2,1,0:T(8,128)(2,1)}, bf16[2,160,1280]{2,1,0:T(8,128)(2,1)}, bf16[2,160,320]{2,1,0:T(8,128)(2,1)}, bf16[2,160,320]{2,1,0:T(...) custom-call(f32[256,1280]{1,0:T(8,128)} %fusion.3.refs_0_.refs_6_, ...), custom_call_target="tpu_custom_call" | custom-call | flops 2516582400 | bytes 16777216 | tf_op jit(solution)/shard_map/chain_forward/pallas_call | solution.py:1026
  122.3 1.0 slice.305
  123.3 1.6 collective-permute-start
  124.9 1.0 slice.306
  127.0 1.5 copy-done.4
  128.5 7.8 %attend_forward.2 = (bf16[320,1024]{1,0:T(8,128)(2,1)S(1)}, f32[4,1,1024]{2,1,0:T(1,128)S(1)}) custom-call(s32[16]{0:T(128)S(1)} %reshape.214.active, bf16[960,1024]{1,0:T(8,128)(2,1)S(1)} %copy-done.4, s32[1,1024]{1,0:T(1,128)S(1)} %get-tuple-element.130.code_row, s32[1024,1]{1,0:T(8,128)S(1)} %copy.59.code_col), custom_call_target="tpu_custom_call" | custom-call | flops 1342177280 | bytes 4194304 | tf_op jit(solution)/shard_map/attend_forward/pallas_call | solution.py:210
  138.7 73.2 %chain_forward.5 = (bf16[2,160,1280]{2,1,0:T(8,128)(2,1)}, bf16[2,160,1280]{2,1,0:T(8,128)(2,1)}, bf16[2,160,960]{2,1,0:T(8,128)(2,1)}, bf16[2,160,1280]{2,1,0:T...) custom-call(f32[256,1280]{1,0:T(8,128)} %fusion.3.refs_0_.refs_6_, ...), custom_call_target="tpu_custom_call" | custom-call | flops 7549747200 | bytes 33554432 | tf_op jit(solution)/shard_map/chain_forward/pallas_call | solution.py:1026
  211.9 33.1 %chain_forward.6 = (bf16[2,160,1280]{2,1,0:T(8,128)(2,1)}, bf16[2,160,1280]{2,1,0:T(8,128)(2,1)}, bf16[2,160,1280]{2,1,0:T(8,128)(2,1)}, bf16[960,1024]{1,0:T(8,128)(2,1)}, bf16[1024,1280]{1,0:T(8,128)(2,1)}) custom-call(f32[256,1280]{1,0:T(8,128)} %get-tuple-element.142.refs_0_.refs_6_, bf16[2,160,960]{2,1,0:T(8,128)(2,1)} %get-tuple-element.143.refs_1_.refs_2_, ...), custom_call_target="tpu_custom_call" | custom-call | flops 2516582400 | bytes 16777216 | tf_op jit(solution)/shard_map/chain_forward/pallas_call | solution.py:1026
  245.0 1.1 slice.322
  246.2 1.1 collective-permute-start.2
  247.3 1.0 slice.323
  248.3 1.0 collective-permute-start.3
  249.4 3.1 fusion.1.refs_2_.refs_8_
  253.3 7.8 %attend_forward.3 = (bf16[320,1024]{1,0:T(8,128)(2,1)S(1)}, f32[4,1,1024]{2,1,0:T(1,128)S(1)}) custom-call(s32[16]{0:T(128)S(1)} %reshape.214.active, bf16[960,1024]{1,0:T(8,128)(2,1)S(1)} %copy-done.6, s32[1,1024]{1,0:T(1,128)S(1)} %get-tuple-element.130.code_row, s32[1024,1]{1,0:T(8,128)S(1)} %copy.59.code_col), custom_call_target="tpu_custom_call" | custom-call | flops 1342177280 | bytes 4194304 | tf_op jit(solution)/shard_map/attend_forward/pallas_call | solution.py:210
  262.0 61.8 %chain_forward.7 = (bf16[2,160,1280]{2,1,0:T(8,128)(2,1)}, bf16[2,160,1280]{2,1,0:T(8,128)(2,1)}, bf16[2,160,1280]{2,1,0:T(8,128)(2,1)}, f32[256,1280]{1,0:T(8,1...) custom-call(f32[256,1280]{1,0:T(8,128)} %get-tuple-element.142.refs_, ...), custom_call_target="tpu_custom_call" | custom-call | flops 7549747200 | bytes 33554432 | tf_op jit(solution)/shard_map/chain_forward/pallas_call | solution.py:1026
  323.8 63.7 %chain_backward.3 = (f32[8,1280]{1,0:T(8,128)}, f32[256,1280]{1,0:T(8,128)}, bf16[1024,1280]{1,0:T(8,128)(2,1)}, bf16[1024,1280]{1,0:T(8,128)(2,1)}, f32[1,1280]...) custom-call(f32[256,1280]{1,0:T(8,128)} %get-tuple-element.158.refs_0_, ...), custom_call_target="tpu_custom_call" | custom-call | flops 7549747200 | bytes 33554432 | tf_op jit(solution)/shard_map/chain_backward/pallas_call | solution.py:1026
  387.6 4.3 convolution_convert_fusion.7.refs_27_.refs_14_
  391.9 10.2 %attend_backward.2.refs_1_ = bf16[960,1024]{1,0:T(8,128)(2,1)S(1)} custom-call(s32[16]{0:T(128)S(1)} %reshape.214.active, bf16[960,1024]{1,0:T(8,128)(2,1)S(1)} %copy-done.6, bf16[320,1024]{1,0:T(8,128)(2,1)S(1)} %copy-done.10, bf16[320,1024]{1,0:T(8,128)(2,1)S(1)} %copy-done.12, f32[4,1,1024]{2,1,0:T(1,128)S(1)} %get-tuple-element.168.log_sum, ...), custom_call_target="tpu_custom_call" | custom-call | flops 3355443200 | bytes 10485760 | tf_op jit(solution)/shard_map/attend_backward/pallas_call | solution.py:238
  402.5 4.3 convolution_convert_fusion.5.refs_26_.refs_11_
  406.9 5.1 convolution_convert_fusion.2.refs_25_
  411.9 5.2 convolution_convert_fusion.3.refs_24_
  417.2 98.5 %chain_backward.4 = (f32[8,1280]{1,0:T(8,128)}, bf16[2,160,1280]{2,1,0:T(8,128)(2,1)}, bf16[2,160,1280]{2,1,0:T(8,128)(2,1)}, bf16[2,160,1280]{2,1,0:T(8,128)(2,...) custom-call(f32[256,1280]{1,0:T(8,128)} %get-tuple-element.166.refs_, ...), custom_call_target="tpu_custom_call" | custom-call | flops 10066329600 | bytes 50331648 | tf_op jit(solution)/shard_map/chain_backward/pallas_call | solution.py:1026
  515.7 4.4 convolution_convert_fusion.6.refs_18_
  520.1 5.1 convolution_convert_fusion.refs_10_
  525.2 5.1 convolution_convert_fusion.1.refs_9_
  530.3 10.2 %attend_backward.3.refs_1_ = bf16[960,1024]{1,0:T(8,128)(2,1)S(1)} custom-call(s32[16]{0:T(128)S(1)} %reshape.214.active, bf16[960,1024]{1,0:T(8,128)(2,1)S(1)} %copy-done.5, bf16[320,1024]{1,0:T(8,128)(2,1)S(1)} %copy-done.8, bf16[320,1024]{1,0:T(8,128)(2,1)S(1)} %copy-done.11, f32[4,1,1024]{2,1,0:T(1,128)S(1)} %get-tuple-element.187.log_sum, ...), custom_call_target="tpu_custom_call" | custom-call | flops 3355443200 | bytes 10485760 | tf_op jit(solution)/shard_map/attend_backward/pallas_call | solution.py:238
  540.8 4.2 convolution_convert_fusion.4.refs_17_
  545.0 121.0 %chain_backward.5 = (f32[8,1280]{1,0:T(8,128)}, bf16[2,160,1280]{2,1,0:T(8,128)(2,1)}, bf16[2,160,1280]{2,1,0:T(8,128)(2,1)}, bf16[2,160,1280]{2,1,0:T(8,128)(2,...) custom-call(f32[256,1280]{1,0:T(8,128)} %get-tuple-element.180.refs_, ...), custom_call_target="tpu_custom_call" | custom-call | flops 2516582400 | bytes 16777216 | tf_op jit(solution)/shard_map/chain_backward/pallas_call | solution.py:1026
  667.1 2.1 fusion
  671.0 1.1 collective-permute-start.4
  672.1 3.3 collective-permute-done.4
  675.5 1.1 collective-permute-start.5
  676.6 2.5 pad_maximum_fusion.2
  679.7 1.3 pad_maximum_fusion.1
  682.3 4.1 collective-permute-done.7
  687.3 1.2 copy.65
  688.6 1.1 convert_element_type.80
  689.7 1.1 convert_element_type.71
  (215 shorter events, 25.7 us)
Async XLA Ops:
  0.7 4.4 copy-start.13
  5.1 4.1 copy-start.40
  5.1 4.2 copy-start.41
  5.2 4.3 copy-start.42
  5.2 4.4 copy-start.43
  5.2 4.4 copy-start.44
  70.9 7.0 %copy-start.36 = (bf16[256,1280]{1,0:T(8,128)(2,1)S(1)}, bf16[256,1280]{1,0:T(8,128)(2,1)}, u32[]{:S(2)}) copy-start(bf16[256,1280]{1,0:T(8,128)(2,1)} %get-tuple-element.114) | copy-start | bytes 1966084
  123.3 14.5 %collective-permute-start = (bf16[1,160,1280]{2,1,0:T(8,128)(2,1)S(1)}, bf16[1,160,1280]{2,1,0:T(8,128)(2,1)S(1)}, u32[]{:S(2)}, u32[]{:S(2)}) collective-permute-start(bf16[1,160,1280]{2,1,0:T(8,128)(2,1)S(1)} %slice.305), channel_id=1, source_target_pairs={{0,16},{4,20},{8,24},{12,28},{16,0},{20,4},{24,8},{28,12},{1,17},{... | collective-permute-start | bytes 1228808 | tf_op jit(solution)/shard_map/ppermute | solution.py:1051
  125.9 11.9 %collective-permute-start.1 = (bf16[1,160,1280]{2,1,0:T(8,128)(2,1)S(1)}, bf16[1,160,1280]{2,1,0:T(8,128)(2,1)S(1)}, u32[]{:S(2)}, u32[]{:S(2)}) collective-permute-start(bf16[1,160,1280]{2,1,0:T(8,128)(2,1)S(1)} %slice.306), channel_id=1, source_target_pairs={{0,8},{4,12},{8,0},{12,4},{16,24},{20,28},{24,16},{28,20},{1,9},{5... | collective-permute-start | bytes 1228808 | tf_op jit(solution)/shard_map/ppermute | solution.py:1051
  245.0 7.4 %copy-start.14 = (f32[256,1280]{1,0:T(8,128)S(1)}, f32[256,1280]{1,0:T(8,128)}, u32[]{:S(2)}) copy-start(f32[256,1280]{1,0:T(8,128)} %param.33) | copy-start | bytes 3932164
  246.2 15.8 %collective-permute-start.2 = (bf16[1,160,1280]{2,1,0:T(8,128)(2,1)S(1)}, bf16[1,160,1280]{2,1,0:T(8,128)(2,1)}, u32[]{:S(2)}, u32[]{:S(2)}) collective-permute-start(bf16[1,160,1280]{2,1,0:T(8,128)(2,1)S(1)} %slice.322), channel_id=1, source_target_pairs={{0,16},{4,20},{8,24},{12,28},{16,0},{20,4},{24,8},{28,12},{1,17},{... | collective-permute-start | bytes 1228808 | tf_op jit(solution)/shard_map/ppermute | solution.py:1051
  248.3 5.0 copy-start.6
  248.3 13.7 %collective-permute-start.3 = (bf16[1,160,1280]{2,1,0:T(8,128)(2,1)S(1)}, bf16[1,160,1280]{2,1,0:T(8,128)(2,1)}, u32[]{:S(2)}, u32[]{:S(2)}) collective-permute-start(bf16[1,160,1280]{2,1,0:T(8,128)(2,1)S(1)} %slice.323), channel_id=1, source_target_pairs={{0,8},{4,12},{8,0},{12,4},{16,24},{20,28},{24,16},{28,20},{1,9},{5... | collective-permute-start | bytes 1228808 | tf_op jit(solution)/shard_map/ppermute | solution.py:1051
  323.8 63.7 %copy-start.10 = (bf16[320,1024]{1,0:T(8,128)(2,1)S(1)}, bf16[320,1024]{1,0:T(8,128)(2,1)}, u32[]{:S(2)}) copy-start(bf16[320,1024]{1,0:T(8,128)(2,1)} %copy-done.9) | copy-start | bytes 1966084
  387.6 4.4 copy-start.2
  387.6 4.4 copy-start.3
  387.6 4.4 copy-start.12
  391.9 10.5 %copy-start.46 = (bf16[1024,1280]{1,0:T(8,128)(2,1)S(1)}, bf16[1024,1280]{1,0:T(8,128)(2,1)}, u32[]{:S(2)}) copy-start(bf16[1024,1280]{1,0:T(8,128)(2,1)} %get-tuple-element.178) | copy-start | bytes 7864324
  402.1 4.7 copy-start.1
  402.5 4.3 copy-start.50
  402.5 4.3 copy-start.54
  406.8 5.1 copy-start.49
  406.9 5.1 copy-start.53
  417.2 98.5 %copy-start.8 = (bf16[320,1024]{1,0:T(8,128)(2,1)S(1)}, bf16[320,1024]{1,0:T(8,128)(2,1)}, u32[]{:S(2)}) copy-start(bf16[320,1024]{1,0:T(8,128)(2,1)} %copy-done.7) | copy-start | bytes 1966084
  515.7 4.4 copy-start.48
  515.7 4.4 copy-start.52
  520.1 5.1 copy-start.47
  520.1 5.1 copy-start.51
  525.2 5.1 copy-start.5
  525.2 5.1 copy-start.11
  530.3 10.5 %copy-start.45 = (bf16[1024,1280]{1,0:T(8,128)(2,1)S(1)}, bf16[1024,1280]{1,0:T(8,128)(2,1)}, u32[]{:S(2)}) copy-start(bf16[1024,1280]{1,0:T(8,128)(2,1)} %get-tuple-element.194) | copy-start | bytes 7864324
  540.5 4.6 copy-start
  545.0 121.9 %copy-start.27 = (f32[8,1280]{1,0:T(8,128)S(1)}, f32[8,1280]{1,0:T(8,128)}, u32[]{:S(2)}) copy-start(f32[8,1280]{1,0:T(8,128)} %get-tuple-element.200) | copy-start | bytes 122884
  545.0 121.9 %copy-start.28 = (f32[8,1280]{1,0:T(8,128)S(1)}, f32[8,1280]{1,0:T(8,128)}, u32[]{:S(2)}) copy-start(f32[8,1280]{1,0:T(8,128)} %get-tuple-element.201) | copy-start | bytes 122884
  666.0 4.6 copy-start.30
  666.0 4.6 copy-start.31
  666.0 10.5 %copy-start.19 = (f32[160,1280]{1,0:T(8,128)S(1)}, f32[160,1280]{1,0:T(8,128)}, u32[]{:S(2)}) copy-start(f32[160,1280]{1,0:T(8,128)} %get-tuple-element.211) | copy-start | bytes 2457604
  670.4 9.3 %copy-start.17 = (f32[160,1280]{1,0:T(8,128)S(1)}, f32[160,1280]{1,0:T(8,128)}, u32[]{:S(2)}) copy-start(f32[160,1280]{1,0:T(8,128)} %get-tuple-element.209) | copy-start | bytes 2457604
  670.4 9.3 %copy-start.18 = (f32[160,1280]{1,0:T(8,128)S(1)}, f32[160,1280]{1,0:T(8,128)}, u32[]{:S(2)}) copy-start(f32[160,1280]{1,0:T(8,128)} %get-tuple-element.208) | copy-start | bytes 2457604
  671.0 4.4 collective-permute-start.4
  675.5 4.0 collective-permute-start.5
  676.6 4.3 copy-start.21
  679.6 2.2 collective-permute-start.6
  681.3 5.2 copy-start.25
  681.3 5.2 copy-start.26
  681.8 4.6 collective-permute-start.7
  682.3 6.3 copy-start.23
  686.4 4.4 collective-permute-start.8
  (16 other events, 40.8 us)
